TPU v7x, 32 devices: a whole 2x2x4 slice. The times are simulated.
32 devices in a mesh: batch: 4 (over y, x), ctx: 8 (over z, core).
Axes of the slice: x: 2, y: 2, z: 4, core: 2. Of those that a mesh axis runs over, the one named last changes fastest.
Arguments:
- q_in: bfloat16 [16384, 2048], P(('batch', 'ctx')), parts along dimension 0, may hold values from -6 to 6
- k_in: bfloat16 [16384, 2048], P(('batch', 'ctx')), parts along dimension 0, may hold values from -6 to 6
- v_in: bfloat16 [16384, 2048], P(('batch', 'ctx')), parts along dimension 0, may hold values from -6 to 6
- z_in: bfloat16 [16384, 2048], P(('batch', 'ctx')), parts along dimension 0, may hold values from -6 to 6
- log_gate: float32 [16384, 16], P(('batch', 'ctx')), parts along dimension 0, may hold values from -1 to 0, as said below
- beta: float32 [16384, 16], P(('batch', 'ctx')), parts along dimension 0, may hold values from 0 to 1
- level_weight: float32 [16384, 16, 6], P(('batch', 'ctx')), parts along dimension 0, may hold values from 0.2 to 2
- conv_weight: float32 [3, 4, 2048], replicated, may hold values from -3 to 3
- norm_gain: float32 [128], replicated, may hold values from 0.25 to 1.75
Outputs:
- mixed_out: bfloat16 [16384, 2048], P(('batch', 'ctx')), parts along dimension 0
There are 4 independent parts, one for each index of `batch`. A program takes and returns all parts, laid end to end along the dimension named above; an argument that names none is the same for every part. Nothing has to cross between parts.
Inputs may be any that keep to these rules, and one draw needn't show every extreme that they name: `log_gate`: logarithms of forget gates, never positive.
All inputs are finite; a program needn't handle non-finite values.
Results may differ from a plain program's by a relative error of at most 0.0056.
Values may be sent and summed in bfloat16 or wider, within the bound.
No kernel may reach another device: no remote copies, remote signals or barrier semaphores. Data moves between devices by JAX's collectives and lax.ppermute only.
A program may use at most 128 MiB of HBM per device.

v0:
```python
import functools

import jax
import jax.numpy as jnp
from jax import lax
from jax.experimental import pallas as pl
from jax.experimental.pallas import tpu as pltpu
from jax.sharding import PartitionSpec as P

BLK = 128
SUB = 16
HEADS_PER_STEP = 2
EPS = 1e-06
BF = jnp.bfloat16
F32 = jnp.float32


def dot(first, second):
    return lax.dot_general(
        first, second, (((1,), (0,)), ((), ())), preferred_element_type=F32
    )


def silu(value):
    return value * pl.reciprocal(1.0 + jnp.exp(-value), approx=False)


def fill_padded(pad_ref, slot, x_ref, halo, lanes):
    pad_ref[slot, 4:8, :] = halo.astype(F32)
    pad_ref[slot, 8:, :] = x_ref[:, lanes].astype(F32)


def conv_rows(pad_ref, slot, taps, start, count):
    total = taps[0:1] * pad_ref[slot, start + 5 : start + 5 + count, :]
    for tap in range(1, 4):
        total = total + taps[tap : tap + 1] * pad_ref[
            slot, start + 5 + tap : start + 5 + tap + count, :
        ]
    return silu(total)


def unit(rows):
    return rows * lax.rsqrt(jnp.sum(rows * rows, axis=-1, keepdims=True) + EPS)


def iota2(shape, dim):
    return lax.broadcasted_iota(jnp.int32, shape, dim)


def decay_matrix(g_col, g_row, beta_row):
    size = g_col.shape[0]
    causal = iota2((size, BLK), 1) <= iota2((size, BLK), 0)
    return jnp.exp(jnp.where(causal, g_col - g_row, -1e30)) * beta_row


def make_masks(mask_ref):
    row, col = iota2((BLK, BLK), 0), iota2((BLK, BLK), 1)
    size, index = SUB, 0
    while size < BLK:
        same = row // size == col // size
        pair = row // (2 * size) == col // (2 * size)
        high_low = pair & (row // size % 2 == 1) & (col // size % 2 == 0)
        mask_ref[index] = jnp.where(same, 1.0, 0.0).astype(BF)
        mask_ref[index + 1] = jnp.where(high_low, 1.0, 0.0).astype(BF)
        size, index = size * 2, index + 2


def tiled(packed, times, mask):
    return jnp.concatenate([packed.astype(BF)] * times, axis=0) * mask


def picked(lower, size, offset):
    groups = BLK // size if offset is None else BLK // (2 * size)
    step = size if offset is None else 2 * size
    first = 0 if offset is None else offset
    lane = iota2((size, BLK), 1) // step
    out = lower[first : first + size]
    for group in range(1, groups):
        begin = first + group * step
        out = jnp.where(lane == group, lower[begin : begin + size], out)
    return out


def inverses(lowers, mask_ref):
    count = len(lowers)
    every = range(count)
    row, col = iota2((SUB, BLK), 0), iota2((SUB, BLK), 1) % SUB
    eye = jnp.where(row == col, 1.0, 0.0).astype(F32)
    strict = col < row
    same = mask_ref[0]
    times = BLK // SUB
    powers = [jnp.where(strict, -picked(lower, SUB, None), 0.0) for lower in lowers]
    results = [eye + power for power in powers]
    powers = [dot(p.astype(BF), tiled(p, times, same)) for p in powers]
    reach = 2
    while reach < SUB // 2:
        both = [
            dot(
                jnp.concatenate([powers[i].astype(BF), results[i].astype(BF)], axis=0),
                tiled(powers[i], times, same),
            )
            for i in every
        ]
        powers = [b[:SUB] for b in both]
        results = [results[i] + both[i][SUB:] for i in every]
        reach *= 2
    results = [
        results[i] + dot(results[i].astype(BF), tiled(powers[i], times, same)) for i in every
    ]
    size, index = SUB, 0
    while size < BLK:
        times = BLK // size
        low = iota2((size, BLK), 1) // size % 2 == 0
        cross = [picked(lower, size, size).astype(BF) for lower in lowers]
        moved = [dot(cross[i], tiled(results[i], times, mask_ref[index])) for i in every]
        turned = [
            dot(results[i].astype(BF), tiled(moved[i], times, mask_ref[index + 1]))
            for i in every
        ]
        results = [
            jnp.concatenate(
                [jnp.where(low, results[i], 0.0), jnp.where(low, -turned[i], results[i])], axis=0
            )
            for i in every
        ]
        size, index = size * 2, index + 2
    return results


def key_side(
    rows_ref, g_ref, taps_ref, halo_ref, k_ref, v_ref,
    kt_ref, uw_ref, pair_ref, sent_ref, prior_ref, pad_ref, mask_ref,
):
    step = pl.program_id(0)

    @pl.when(step == 0)
    def _():
        make_masks(mask_ref)

    length = k_ref.shape[0]
    blocks = length // BLK
    turned_g = pltpu.roll(g_ref[...], BLK - HEADS_PER_STEP * step, 1)
    lowers, rights, tails, lasts = [], [], [], []
    for head in range(HEADS_PER_STEP):
        lanes = slice(head * BLK, (head + 1) * BLK)
        fill_padded(pad_ref, 2 * head, k_ref, halo_ref[1, :, lanes], lanes)
        fill_padded(pad_ref, 2 * head + 1, v_ref, halo_ref[2, :, lanes], lanes)
        for block in range(blocks):
            start = block * BLK
            tokens = slice(start, start + BLK)
            keys = unit(conv_rows(pad_ref, 2 * head, taps_ref[1, :, lanes], start, BLK)).astype(BF)
            values = conv_rows(pad_ref, 2 * head + 1, taps_ref[2, :, lanes], start, BLK).astype(BF)
            keys_f = keys.astype(F32)
            turned = keys_f.T
            turned_b = turned.astype(BF)
            kt_ref[head, :, tokens] = turned_b
            g_col = jnp.broadcast_to(turned_g[tokens, head : head + 1], (BLK, BLK))
            g_row = rows_ref[head, 0:1, tokens]
            beta_row = rows_ref[head, 1:2, tokens]
            g_last = g_row[:, BLK - 1 : BLK]
            lowers.append(decay_matrix(g_col, g_row, beta_row) * dot(keys, turned_b))
            rights.append(
                jnp.concatenate([values, (jnp.exp(g_col) * keys_f).astype(BF)], axis=1)
            )
            tails.append((turned * (jnp.exp(g_last - g_row) * beta_row)).astype(BF))
            lasts.append(jnp.exp(g_last))
    solved = inverses(lowers, mask_ref)
    maps = []
    for head in range(HEADS_PER_STEP):
        for block in range(blocks):
            i = head * blocks + block
            fresh = dot(solved[i].astype(BF), rights[i]).astype(BF)
            uw_ref[head, block * BLK : (block + 1) * BLK, :] = fresh
            maps.append(dot(tails[i], fresh))
    eye = jnp.where(iota2((BLK, BLK), 0) == iota2((BLK, BLK), 1), 1.0, 0.0).astype(F32)
    for head in range(HEADS_PER_STEP):
        i = head * blocks
        state_a = lasts[i] * eye - maps[i][:, BLK:]
        state_b = maps[i][:, :BLK]
        for block in range(1, blocks):
            i = head * blocks + block
            state = jnp.concatenate([state_a, state_b], axis=1)
            low = state.astype(BF)
            prior_ref[head, block - 1] = low
            state = lasts[i] * state - dot(maps[i][:, BLK:].astype(BF), low)
            state_a = state[:, :BLK]
            state_b = state[:, BLK:] + maps[i][:, :BLK]
        state = jnp.concatenate([state_a, state_b], axis=1)
        pair_ref[head] = state
        sent_ref[head] = state.astype(BF)


def query_side(
    rows_ref, g_ref, taps_ref, halo_ref, q_ref, kt_ref, uw_ref, prior_ref,
    carried_ref, local_ref, pad_ref,
):
    step = pl.program_id(0)
    length = q_ref.shape[0]
    blocks = length // BLK
    turned_g = pltpu.roll(g_ref[...], BLK - HEADS_PER_STEP * step, 1)
    for head in range(HEADS_PER_STEP):
        lanes = slice(head * BLK, (head + 1) * BLK)
        fill_padded(pad_ref, head, q_ref, halo_ref[0, :, lanes], lanes)
        for block in range(blocks):
            start = block * BLK
            tokens = slice(start, start + BLK)
            queries = unit(conv_rows(pad_ref, head, taps_ref[0, :, lanes], start, BLK)).astype(BF)
            g_col = jnp.broadcast_to(turned_g[tokens, head : head + 1], (BLK, BLK))
            g_row = rows_ref[head, 0:1, tokens]
            beta_row = rows_ref[head, 1:2, tokens]
            mixing = (
                decay_matrix(g_col, g_row, beta_row) * dot(queries, kt_ref[head, :, tokens])
            ).astype(BF)
            inner = dot(mixing, uw_ref[head, tokens, :])
            through = (jnp.exp(g_col) * queries.astype(F32) - inner[:, BLK:]).astype(BF)
            if block == 0:
                carried_ref[tokens, lanes] = through
                local_ref[tokens, lanes] = inner[:, :BLK].astype(local_ref.dtype)
            else:
                passed = dot(through, prior_ref[head, block - 1])
                carried_ref[tokens, lanes] = passed[:, :BLK].astype(carried_ref.dtype)
                local_ref[tokens, lanes] = (inner[:, :BLK] + passed[:, BLK:]).astype(
                    local_ref.dtype
                )


def finish_side(weight_ref, gain_ref, z_ref, carried_ref, local_ref, *rest):
    state_refs, out_ref = rest[:-1], rest[-1]
    step = pl.program_id(0)
    levels = len(state_refs)
    per_head = levels + 1
    width = weight_ref.shape[1]
    length = z_ref.shape[0]
    blocks = length // BLK
    stride = HEADS_PER_STEP * per_head
    for head in range(HEADS_PER_STEP):
        lanes = slice(head * BLK, (head + 1) * BLK)
        states = jnp.concatenate([ref[head] for ref in state_refs], axis=0)
        for block in range(blocks):
            tokens = slice(block * BLK, (block + 1) * BLK)
            weights = pltpu.roll(weight_ref[tokens, :], width - stride * step, 1)
            first = head * per_head
            carried = carried_ref[tokens, lanes].astype(F32)
            scaled = [
                (carried * weights[:, first + level : first + level + 1]).astype(BF)
                for level in range(1, per_head)
            ]
            far = dot(jnp.concatenate(scaled, axis=1), states)
            opened = weights[:, first : first + 1] * local_ref[tokens, lanes].astype(F32) + far
            square = jnp.sum(opened * opened, axis=-1, keepdims=True) * (1.0 / BLK)
            normed = opened * lax.rsqrt(square + EPS) * gain_ref[...]
            gate = z_ref[tokens, lanes].astype(F32)
            out_ref[tokens, lanes] = (normed * silu(gate)).astype(BF)


def combine_side(upper_ref, pair_ref, far_ref, reach_ref, next_ref, sent_ref, state_ref, new_reach_ref):
    heads = pair_ref.shape[0]

    @pl.when(upper_ref[0] == 1)
    def _():
        for head in range(heads):
            far = far_ref[head]
            own = pair_ref[head]
            seen = dot(reach_ref[head], far)
            new_reach_ref[head] = seen[:, :BLK].astype(BF)
            state_ref[head] = seen[:, BLK:].astype(BF)
            merged = dot(own[:, :BLK].astype(BF), far)
            merged = jnp.concatenate([merged[:, :BLK], merged[:, BLK:] + own[:, BLK:]], axis=1)
            next_ref[head] = merged
            sent_ref[head] = merged.astype(BF)

    @pl.when(upper_ref[0] == 0)
    def _():
        for head in range(heads):
            far = far_ref[head]
            merged = dot(far[:, :BLK], pair_ref[head].astype(BF))
            merged = jnp.concatenate(
                [merged[:, :BLK], merged[:, BLK:] + far[:, BLK:].astype(F32)], axis=1
            )
            next_ref[head] = merged
            sent_ref[head] = merged.astype(BF)
            state_ref[head] = jnp.zeros((BLK, BLK), BF)
            new_reach_ref[head] = reach_ref[head]


def top_side(upper_ref, far_ref, reach_ref, state_ref):
    @pl.when(upper_ref[0] == 1)
    def _():
        for head in range(far_ref.shape[0]):
            state_ref[head] = dot(reach_ref[head], far_ref[head]).astype(BF)

    @pl.when(upper_ref[0] == 0)
    def _():
        state_ref[...] = jnp.zeros(state_ref.shape, BF)


def shape_of(shape, dtype):
    return jax.ShapeDtypeStruct(shape, dtype)


def whole(shape):
    return pl.BlockSpec(shape, lambda i: (0,) * len(shape))


def by_head(shape):
    return pl.BlockSpec((HEADS_PER_STEP,) + shape, lambda i: (i,) + (0,) * len(shape))


def by_column(shape):
    lead = len(shape) - 1
    return pl.BlockSpec(shape, lambda i: (0,) * lead + (i,))


VMEM = pl.BlockSpec(memory_space=pltpu.VMEM)
SMEM = pl.BlockSpec(memory_space=pltpu.SMEM)


def per_device(q_in, k_in, v_in, z_in, log_gate, beta, level_weight, conv_weight, norm_gain):
    length, heads = log_gate.shape
    blocks = length // BLK
    width = HEADS_PER_STEP * BLK
    steps = heads // HEADS_PER_STEP
    ctx = lax.axis_size("ctx")
    levels = ctx.bit_length() - 1
    position = lax.axis_index("ctx")
    edge = jnp.stack([x[length - 4 :] for x in (q_in, k_in, v_in)], axis=0)
    halo = lax.ppermute(edge, "ctx", [(i, i + 1) for i in range(ctx - 1)])

    g = jnp.cumsum(log_gate.reshape(blocks, BLK, heads), axis=1).reshape(length, heads)
    g_pad = jnp.pad(g, ((0, 0), (0, BLK - heads)))
    rows = jnp.stack([g.T, beta.T], axis=1)
    weights = level_weight[:, :, : levels + 1].reshape(length, heads * (levels + 1))
    weights = jnp.pad(weights, ((0, 0), (0, -weights.shape[1] % BLK)))

    params = pltpu.CompilerParams(dimension_semantics=("arbitrary",), vmem_limit_bytes=60 << 20)
    kt, uw, pair, sent, prior = pl.pallas_call(
        key_side,
        grid=(steps,),
        in_specs=[
            by_head((2, length)), whole(g_pad.shape), by_column((3, 4, width)),
            by_column((3, 4, width)), by_column((length, width)), by_column((length, width)),
        ],
        out_specs=[
            by_head((BLK, length)), by_head((length, 2 * BLK)), by_head((BLK, 2 * BLK)),
            by_head((BLK, 2 * BLK)), by_head((blocks - 1, BLK, 2 * BLK)),
        ],
        out_shape=[
            shape_of((heads, BLK, length), BF), shape_of((heads, length, 2 * BLK), BF),
            shape_of((heads, BLK, 2 * BLK), F32), shape_of((heads, BLK, 2 * BLK), BF),
            shape_of((heads, blocks - 1, BLK, 2 * BLK), BF),
        ],
        scratch_shapes=[
            pltpu.VMEM((2 * HEADS_PER_STEP, length + 8, BLK), F32),
            pltpu.VMEM((6, BLK, BLK), BF),
        ],
        compiler_params=params,
        cost_estimate=pl.CostEstimate(flops=10**10, bytes_accessed=2 * 10**7, transcendentals=10**7),
        name="key_side",
    )(rows, g_pad, conv_weight, halo, k_in, v_in)

    carried, local = pl.pallas_call(
        query_side,
        grid=(steps,),
        in_specs=[
            by_head((2, length)), whole(g_pad.shape), by_column((3, 4, width)),
            by_column((3, 4, width)), by_column((length, width)), by_head((BLK, length)),
            by_head((length, 2 * BLK)), by_head((blocks - 1, BLK, 2 * BLK)),
        ],
        out_specs=[by_column((length, width)), by_column((length, width))],
        out_shape=[shape_of(q_in.shape, BF), shape_of(q_in.shape, BF)],
        scratch_shapes=[pltpu.VMEM((HEADS_PER_STEP, length + 8, BLK), F32)],
        compiler_params=params,
        cost_estimate=pl.CostEstimate(flops=10**10, bytes_accessed=2 * 10**7, transcendentals=10**7),
        name="query_side",
    )(rows, g_pad, conv_weight, halo, q_in, kt, uw, prior)

    reach = jnp.broadcast_to(jnp.eye(BLK, dtype=BF), (heads, BLK, BLK))
    states = []
    square = (heads, BLK, BLK)
    for level in range(levels - 1):
        far = lax.ppermute(sent, "ctx", [(i, i ^ 2**level) for i in range(ctx)])
        upper = (position // 2**level % 2).astype(jnp.int32).reshape(1)
        pair, sent, state, reach = pl.pallas_call(
            combine_side,
            in_specs=[SMEM, VMEM, VMEM, VMEM],
            out_specs=[VMEM] * 4,
            out_shape=[
                shape_of(pair.shape, F32), shape_of(pair.shape, BF), shape_of(square, BF),
                shape_of(square, BF),
            ],
            name="combine",
        )(upper, pair, far, reach)
        states.append(state)
    top = levels - 1
    far = lax.ppermute(
        sent[:, :, BLK:], "ctx", [(i, i + 2**top) for i in range(ctx - 2**top)]
    )
    upper = (position // 2**top % 2).astype(jnp.int32).reshape(1)
    states.append(
        pl.pallas_call(
            top_side,
            in_specs=[SMEM, VMEM, VMEM],
            out_specs=VMEM,
            out_shape=shape_of(square, BF),
            name="top",
        )(upper, far, reach)
    )
    return pl.pallas_call(
        finish_side,
        grid=(steps,),
        in_specs=[
            whole(weights.shape), whole((1, BLK)), by_column((length, width)),
            by_column((length, width)), by_column((length, width)),
        ]
        + [by_head((BLK, BLK))] * levels,
        out_specs=by_column((length, width)),
        out_shape=shape_of(z_in.shape, BF),
        compiler_params=params,
        name="finish_side",
    )(weights, norm_gain.reshape(1, BLK), z_in, carried, local, *states)


def solution(mesh):
    placed = (
        P(("batch", "ctx"), None),
        P(("batch", "ctx"), None),
        P(("batch", "ctx"), None),
        P(("batch", "ctx"), None),
        P(("batch", "ctx"), None),
        P(("batch", "ctx"), None),
        P(("batch", "ctx"), None, None),
        P(),
        P(),
    )
    return jax.shard_map(
        per_device, mesh=mesh, in_specs=placed, out_specs=P(("batch", "ctx"), None), check_vma=False
    )
```

profile of v0, /device:TPU:24, one launch (start us, length us, event | category | flops | bytes accessed | tf_op | source)
XLA Modules:
  0.0 129.6 jit_solution(10503685732891067922)
XLA Ops:
  0.0 0.8 slice_bitcast_fusion.2
  0.8 0.8 slice_bitcast_fusion
  1.6 1.9 %collective-permute-start = (bf16[3,4,2048]{2,1,0:T(4,128)(2,1)S(1)}, bf16[3,4,2048]{2,1,0:T(4,128)(2,1)S(1)}, u32[]{:S(2)}, u32[]{:S(2)}) collective-permute-start(bf16[3,4,2048]{2,1,0:T(4,128)(2,1)S(1)} %pad_maximum_fusion.1), channel_id=1, source_target_pairs={{0,1},{1,2},{2,3},{3,4},{4,5},{5,6},{6,7},{8,9},{9,10},{10,11},{11... | collective-permute-start | bytes 147464 | tf_op jit(solution)/shard_map/ppermute | solution.py:327
  3.6 0.9 copy.30
  4.4 0.9 copy.33
  5.3 0.3 reduce_window_sum.11
  5.6 0.8 copy.32.rows_ref
  6.4 0.7 pad.9.g_ref
  7.2 0.0 collective-permute-done.halo_ref
  7.2 0.0 copy-start.3
  7.2 0.6 copy-done.3
  7.8 27.8 %key_side.1 = (bf16[16,128,512]{2,1,0:T(8,128)(2,1)}, bf16[16,512,256]{2,1,0:T(8,128)(2,1)}, f32[16,128,256]{2,1,0:T(8,128)}, bf16[16,128,256]{2,1,0:T(8,128)(2,1)}, bf16[16,3,128,256]{3,2,1,0:T(8,128)(2,1)}) custom-call(f32[16,2,512]{2,1,0:T(2,128)} %copy.32.rows_ref, f32[512,128]{1,0:T(8,128)} %pad.9.g_ref, f32[3,4,2048]{2,1,0:T(4,128)} %taps_ref.3, ...), custom_call_target="tpu_custom_call" | custom-call | flops 10000000000 | bytes 20000000 | tf_op jit(solution)/shard_map/key_side/pallas_call | solution.py:336
  35.6 0.0 collective-permute-start.1
  35.7 2.8 %collective-permute-done.1.far_ref = bf16[16,128,256]{2,1,0:T(8,128)(2,1)S(1)} collective-permute-done((bf16[16,128,256]{2,1,0:T(8,128)(2,1)}, bf16[16,128,256]{2,1,0:T(8,128)(2,1)S(1)}, u32[]{:S(2)}, u32[]{:S(2)}) %collective-permute-start.1) | collective-permute-done | bytes 1048608 | tf_op jit(solution)/shard_map/ppermute | solution.py:381
  38.5 0.0 copy-start.1
  38.5 1.0 broadcast_in_dim.3.reach_ref
  39.5 0.2 copy-done.1
  39.7 0.0 slice-start
  39.7 4.6 %combine.2 = (f32[16,128,256]{2,1,0:T(8,128)}, bf16[16,128,256]{2,1,0:T(8,128)(2,1)}, bf16[16,128,128]{2,1,0:T(8,128)(2,1)}, bf16[16,128,128]{2,1,0:T(8,128)(2,1)}) custom-call(s32[1]{0:T(128)} %bitcast.10.upper_ref, f32[16,128,256]{2,1,0:T(8,128)} %get-tuple-element.24.pair_ref, bf16[16,128,256]{2,1,0:T(8,128)(2,1)} %copy-done.1, ...), custom_call_target="tpu_custom_call" | custom-call | tf_op jit(solution)/shard_map/combine/pallas_call | solution.py:383
  44.3 1.8 %collective-permute-start.2 = (bf16[16,128,256]{2,1,0:T(8,128)(2,1)}, bf16[16,128,256]{2,1,0:T(8,128)(2,1)S(1)}, u32[]{:S(2)}, u32[]{:S(2)}) collective-permute-start(bf16[16,128,256]{2,1,0:T(8,128)(2,1)} %get-tuple-element.28), channel_id=1, source_target_pairs={{0,2},{1,3},{2,0},{3,1},{4,6},{5,7},{6,4},{7,5},{8,10},{9,11},{10,... | collective-permute-start | bytes 3145736 | tf_op jit(solution)/shard_map/ppermute | solution.py:381
  46.0 0.0 slice-done
  46.0 0.1 copy.27
  46.2 0.1 copy.28
  46.3 0.8 pad.8.weight_ref
  47.1 23.1 %collective-permute-done.2.far_ref = bf16[16,128,256]{2,1,0:T(8,128)(2,1)S(1)} collective-permute-done((bf16[16,128,256]{2,1,0:T(8,128)(2,1)}, bf16[16,128,256]{2,1,0:T(8,128)(2,1)S(1)}, u32[]{:S(2)}, u32[]{:S(2)}) %collective-permute-start.2) | collective-permute-done | bytes 1048608 | tf_op jit(solution)/shard_map/ppermute | solution.py:381
  70.2 0.0 copy-start
  70.2 1.0 copy-done
  71.2 4.6 %combine.3 = (f32[16,128,256]{2,1,0:T(8,128)}, bf16[16,128,256]{2,1,0:T(8,128)(2,1)}, bf16[16,128,128]{2,1,0:T(8,128)(2,1)}, bf16[16,128,128]{2,1,0:T(8,128)(2,1)}) custom-call(s32[1]{0:T(128)} %bitcast.11.upper_ref, f32[16,128,256]{2,1,0:T(8,128)} %get-tuple-element.27.pair_ref, bf16[16,128,256]{2,1,0:T(8,128)(2,1)} %copy-done, ...), custom_call_target="tpu_custom_call" | custom-call | tf_op jit(solution)/shard_map/combine/pallas_call | solution.py:383
  75.8 1.1 slice.19
  76.9 1.3 collective-permute-start.3
  78.2 14.5 %query_side.1 = (bf16[512,2048]{1,0:T(8,128)(2,1)}, bf16[512,2048]{1,0:T(8,128)(2,1)}) custom-call(f32[16,2,512]{2,1,0:T(2,128)} %copy.32.rows_ref, f32[512,128]{1,0:T(8,128)} %pad.9.g_ref, f32[3,4,2048]{2,1,0:T(4,128)} %taps_ref.3, bf16[3,4,2048]{2,1,0:T(4,128)(2,1)} %copy-done.3, bf16[512,2048]{1,0:T(8,128)(2,1)} %q_ref.1, ...), custom_call_target="tpu_custom_call" | custom-call | flops 10000000000 | bytes 20000000 | tf_op jit(solution)/shard_map/query_side/pallas_call | solution.py:361
  92.7 11.8 %collective-permute-done.3.far_ref = bf16[16,128,128]{2,1,0:T(8,128)(2,1)S(1)} collective-permute-done((bf16[16,128,128]{2,1,0:T(8,128)(2,1)S(1)}, bf16[16,128,128]{2,1,0:T(8,128)(2,1)S(1)}, u32[]{:S(2)}, u32[]{:S(2)}) %collective-permute-start.3) | collective-permute-done | bytes 524320 | tf_op jit(solution)/shard_map/ppermute | solution.py:395
  104.5 0.0 copy-start.2
  104.5 0.8 copy-done.2
  105.3 2.3 %top.1.rest_2_ = bf16[16,128,128]{2,1,0:T(8,128)(2,1)} custom-call(s32[1]{0:T(128)} %bitcast.12.upper_ref, bf16[16,128,128]{2,1,0:T(8,128)(2,1)} %copy-done.2, bf16[16,128,128]{2,1,0:T(8,128)(2,1)} %get-tuple-element.32.reach_ref), custom_call_target="tpu_custom_call" | custom-call | tf_op jit(solution)/shard_map/top/pallas_call | solution.py:400
  107.6 22.0 %finish_side.1 = bf16[512,2048]{1,0:T(8,128)(2,1)} custom-call(f32[512,128]{1,0:T(8,128)} %pad.8.weight_ref, f32[1,128]{1,0:T(1,128)} %bitcast.25, bf16[512,2048]{1,0:T(8,128)(2,1)} %z_ref.1, bf16[512,2048]{1,0:T(8,128)(2,1)} %get-tuple-element.22.carried_ref, bf16[512,2048]{1,0:T(8,128)(2,1)} %get-tuple-element.23.local_ref, ...), custom_call_target="tpu_custom_call" | custom-call | tf_op jit(solution)/shard_map/finish_side/pallas_call | solution.py:408
  (4 shorter events, 0.1 us)
Async XLA Ops:
  1.6 5.6 %collective-permute-start = (bf16[3,4,2048]{2,1,0:T(4,128)(2,1)S(1)}, bf16[3,4,2048]{2,1,0:T(4,128)(2,1)S(1)}, u32[]{:S(2)}, u32[]{:S(2)}) collective-permute-start(bf16[3,4,2048]{2,1,0:T(4,128)(2,1)S(1)} %pad_maximum_fusion.1), channel_id=1, source_target_pairs={{0,1},{1,2},{2,3},{3,4},{4,5},{5,6},{6,7},{8,9},{9,10},{10,11},{11... | collective-permute-start | bytes 147464 | tf_op jit(solution)/shard_map/ppermute | solution.py:327
  7.2 0.6 copy-start.3
  35.6 2.9 %collective-permute-start.1 = (bf16[16,128,256]{2,1,0:T(8,128)(2,1)}, bf16[16,128,256]{2,1,0:T(8,128)(2,1)S(1)}, u32[]{:S(2)}, u32[]{:S(2)}) collective-permute-start(bf16[16,128,256]{2,1,0:T(8,128)(2,1)} %get-tuple-element.25), channel_id=1, source_target_pairs={{0,1},{1,0},{2,3},{3,2},{4,5},{5,4},{6,7},{7,6},{8,9},{9,8},{10,11... | collective-permute-start | bytes 3145736 | tf_op jit(solution)/shard_map/ppermute | solution.py:381
  38.5 1.2 copy-start.1
  39.7 6.3 %slice-start = ((f32[512,16,6]{0,1,2:T(8,128)}), f32[512,16,4]{0,1,2:T(8,128)S(1)}, s32[]{:S(2)}) async-start(f32[512,16,6]{0,1,2:T(8,128)} %param.15), calls=%async_computation | async-start | bytes 262144 | tf_op jit(solution)/shard_map/slice | solution.py:332
  44.3 25.9 %collective-permute-start.2 = (bf16[16,128,256]{2,1,0:T(8,128)(2,1)}, bf16[16,128,256]{2,1,0:T(8,128)(2,1)S(1)}, u32[]{:S(2)}, u32[]{:S(2)}) collective-permute-start(bf16[16,128,256]{2,1,0:T(8,128)(2,1)} %get-tuple-element.28), channel_id=1, source_target_pairs={{0,2},{1,3},{2,0},{3,1},{4,6},{5,7},{6,4},{7,5},{8,10},{9,11},{10,... | collective-permute-start | bytes 3145736 | tf_op jit(solution)/shard_map/ppermute | solution.py:381
  70.2 1.0 copy-start
  76.9 27.6 %collective-permute-start.3 = (bf16[16,128,128]{2,1,0:T(8,128)(2,1)S(1)}, bf16[16,128,128]{2,1,0:T(8,128)(2,1)S(1)}, u32[]{:S(2)}, u32[]{:S(2)}) collective-permute-start(bf16[16,128,128]{2,1,0:T(8,128)(2,1)S(1)} %slice.19), channel_id=1, source_target_pairs={{0,4},{1,5},{2,6},{3,7},{8,12},{9,13},{10,14},{11,15},{16,20},{17,... | collective-permute-start | bytes 1572872 | tf_op jit(solution)/shard_map/ppermute | solution.py:395
  104.5 0.8 copy-start.2
where the time goes:
time: 130 us
  Pallas kernels  75.8 us (58%)
  waiting for transfers between devices  37.7 us (29%)
  local copies, waits for them, and re-layouts  10.6 us (8%)
  starting transfers between devices  4.97 us (4%)
    pallas_call x1, Pallas kernels, per_device(): pl.pallas_call(key_side, grid=(steps,), in_specs=[by_head((2, length)), w...  27.8 us
    ppermute x2, waiting for transfers between devices, per_device(): far = lax.ppermute(sent, 'ctx', [(i, i ^ 2 ** level) for i in range(ctx)])  25.9 us
    pallas_call x1, Pallas kernels, per_device(): pl.pallas_call(finish_side, grid=(steps,), in_specs=[whole(weights.shape)...  22 us
    pallas_call x1, Pallas kernels, per_device(): pl.pallas_call(query_side, grid=(steps,), in_specs=[by_head((2, length)),...  14.5 us
    ppermute x1, waiting for transfers between devices, per_device(): lax.ppermute(sent[:, :, BLK:], 'ctx', [(i, i + 2 ** top) for i in range(c...  11.8 us
    pallas_call x2, Pallas kernels, per_device(): pl.pallas_call(combine_side, in_specs=[SMEM, VMEM, VMEM, VMEM], out_specs...  9.21 us
    unnamed x9, local copies, waits for them, and re-layouts  3.48 us
  transfers between devices with their start and end apart: 4, of which 3 were waited for; matrix products, arithmetic and copies ran while one was open for 4% of the time, Pallas kernels for 11%

commit v1 on v0

--- a/solution.py
+++ b/solution.py
@@ -191,16 +191,24 @@
 
 
 def query_side(
-    rows_ref, g_ref, taps_ref, halo_ref, q_ref, kt_ref, uw_ref, prior_ref,
-    carried_ref, local_ref, pad_ref,
+    odd_ref, rows_ref, g_ref, weight_ref, taps_ref, halo_ref, q_ref, kt_ref, uw_ref, prior_ref,
+    near_ref, *rest, first_step,
 ):
-    step = pl.program_id(0)
+    scaled_ref, base_ref, pad_ref = rest[-3:]
+    step = pl.program_id(0) + first_step
     length = q_ref.shape[0]
     blocks = length // BLK
+    levels = scaled_ref.shape[1] // (HEADS_PER_STEP * BLK) + 1
+    per_head = levels + 1
+    width = weight_ref.shape[1]
+    odd = odd_ref[0].astype(F32)
     turned_g = pltpu.roll(g_ref[...], BLK - HEADS_PER_STEP * step, 1)
+    turned_w = pltpu.roll(weight_ref[...], width - HEADS_PER_STEP * per_head * step, 1)
     for head in range(HEADS_PER_STEP):
         lanes = slice(head * BLK, (head + 1) * BLK)
         fill_padded(pad_ref, head, q_ref, halo_ref[0, :, lanes], lanes)
+        near = near_ref[head] * odd.astype(BF)
+        first = head * per_head
         for block in range(blocks):
             start = block * BLK
             tokens = slice(start, start + BLK)
@@ -212,86 +220,124 @@
                 decay_matrix(g_col, g_row, beta_row) * dot(queries, kt_ref[head, :, tokens])
             ).astype(BF)
             inner = dot(mixing, uw_ref[head, tokens, :])
-            through = (jnp.exp(g_col) * queries.astype(F32) - inner[:, BLK:]).astype(BF)
+            through = jnp.exp(g_col) * queries.astype(F32) - inner[:, BLK:]
             if block == 0:
-                carried_ref[tokens, lanes] = through
-                local_ref[tokens, lanes] = inner[:, :BLK].astype(local_ref.dtype)
+                carried, local = through, inner[:, :BLK]
             else:
-                passed = dot(through, prior_ref[head, block - 1])
-                carried_ref[tokens, lanes] = passed[:, :BLK].astype(carried_ref.dtype)
-                local_ref[tokens, lanes] = (inner[:, :BLK] + passed[:, BLK:]).astype(
-                    local_ref.dtype
-                )
-
-
-def finish_side(weight_ref, gain_ref, z_ref, carried_ref, local_ref, *rest):
-    state_refs, out_ref = rest[:-1], rest[-1]
+                passed = dot(through.astype(BF), prior_ref[head, block - 1])
+                carried, local = passed[:, :BLK], inner[:, :BLK] + passed[:, BLK:]
+            scaled = [
+                (carried * turned_w[tokens, first + level : first + level + 1]).astype(BF)
+                for level in range(1, per_head)
+            ]
+            base_ref[tokens, lanes] = turned_w[tokens, first : first + 1] * local + dot(
+                scaled[0], near
+            )
+            begin = head * (levels - 1) * BLK
+            scaled_ref[tokens, begin : begin + (levels - 1) * BLK] = jnp.concatenate(
+                scaled[1:], axis=1
+            )
+
+
+def finish_side(
+    core_ref, gain_ref, z_ref, base_ref, scaled_ref, near_ref, own_ref, other_ref, out_ref
+):
     step = pl.program_id(0)
-    levels = len(state_refs)
-    per_head = levels + 1
-    width = weight_ref.shape[1]
+    core = core_ref[0]
     length = z_ref.shape[0]
     blocks = length // BLK
-    stride = HEADS_PER_STEP * per_head
+    levels = own_ref.shape[2] // BLK
+    mine = step // (pl.num_programs(0) // 2) == core
+    eye = jnp.where(iota2((BLK, BLK), 0) == iota2((BLK, BLK), 1), 1.0, 0.0).astype(BF)
     for head in range(HEADS_PER_STEP):
         lanes = slice(head * BLK, (head + 1) * BLK)
-        states = jnp.concatenate([ref[head] for ref in state_refs], axis=0)
+        reach = jnp.where(core == 1, near_ref[head], eye)
+        seen = dot(reach, jnp.where(mine, own_ref[head], other_ref[head])).astype(BF)
+        states = jnp.concatenate(
+            [seen[:, level * BLK : (level + 1) * BLK] for level in range(levels)], axis=0
+        )
+        begin = head * levels * BLK
         for block in range(blocks):
             tokens = slice(block * BLK, (block + 1) * BLK)
-            weights = pltpu.roll(weight_ref[tokens, :], width - stride * step, 1)
-            first = head * per_head
-            carried = carried_ref[tokens, lanes].astype(F32)
-            scaled = [
-                (carried * weights[:, first + level : first + level + 1]).astype(BF)
-                for level in range(1, per_head)
-            ]
-            far = dot(jnp.concatenate(scaled, axis=1), states)
-            opened = weights[:, first : first + 1] * local_ref[tokens, lanes].astype(F32) + far
+            opened = base_ref[tokens, lanes] + dot(
+                scaled_ref[tokens, begin : begin + levels * BLK], states
+            )
             square = jnp.sum(opened * opened, axis=-1, keepdims=True) * (1.0 / BLK)
             normed = opened * lax.rsqrt(square + EPS) * gain_ref[...]
             gate = z_ref[tokens, lanes].astype(F32)
             out_ref[tokens, lanes] = (normed * silu(gate)).astype(BF)
 
 
-def combine_side(upper_ref, pair_ref, far_ref, reach_ref, next_ref, sent_ref, state_ref, new_reach_ref):
-    heads = pair_ref.shape[0]
+def merged(left, right_a, right_b):
+    moved = dot(right_a.astype(BF), left.astype(BF))
+    return jnp.concatenate([moved[:, :BLK], moved[:, BLK:] + right_b.astype(F32)], axis=1)
+
+
+def join_near(core_ref, pair_ref, far_ref, next_ref, sent_ref):
+    @pl.when(core_ref[0] == 1)
+    def _():
+        for head in range(pair_ref.shape[0]):
+            own = pair_ref[head]
+            joined = merged(far_ref[head], own[:, :BLK], own[:, BLK:])
+            next_ref[head] = joined
+            sent_ref[head] = joined.astype(BF)
+
+    @pl.when(core_ref[0] == 0)
+    def _():
+        for head in range(pair_ref.shape[0]):
+            far = far_ref[head]
+            joined = merged(pair_ref[head], far[:, :BLK], far[:, BLK:])
+            next_ref[head] = joined
+            sent_ref[head] = joined.astype(BF)
+
+
+def join_far(upper_ref, pair_ref, far_ref, *rest):
+    next_ref, sent_ref, state_ref, onward_ref = rest[-4:]
+    reach_ref = rest[0] if len(rest) == 5 else None
 
     @pl.when(upper_ref[0] == 1)
     def _():
-        for head in range(heads):
+        for head in range(pair_ref.shape[0]):
             far = far_ref[head]
             own = pair_ref[head]
-            seen = dot(reach_ref[head], far)
-            new_reach_ref[head] = seen[:, :BLK].astype(BF)
-            state_ref[head] = seen[:, BLK:].astype(BF)
-            merged = dot(own[:, :BLK].astype(BF), far)
-            merged = jnp.concatenate([merged[:, :BLK], merged[:, BLK:] + own[:, BLK:]], axis=1)
-            next_ref[head] = merged
-            sent_ref[head] = merged.astype(BF)
+            seen = far if reach_ref is None else dot(reach_ref[head], far).astype(BF)
+            onward_ref[head] = seen[:, :BLK]
+            state_ref[head] = seen[:, BLK:]
+            joined = merged(far, own[:, :BLK], own[:, BLK:])
+            next_ref[head] = joined
+            sent_ref[head] = joined.astype(BF)
 
     @pl.when(upper_ref[0] == 0)
     def _():
-        for head in range(heads):
+        for head in range(pair_ref.shape[0]):
             far = far_ref[head]
-            merged = dot(far[:, :BLK], pair_ref[head].astype(BF))
-            merged = jnp.concatenate(
-                [merged[:, :BLK], merged[:, BLK:] + far[:, BLK:].astype(F32)], axis=1
-            )
-            next_ref[head] = merged
-            sent_ref[head] = merged.astype(BF)
+            joined = merged(pair_ref[head], far[:, :BLK], far[:, BLK:])
+            next_ref[head] = joined
+            sent_ref[head] = joined.astype(BF)
             state_ref[head] = jnp.zeros((BLK, BLK), BF)
-            new_reach_ref[head] = reach_ref[head]
-
-
-def top_side(upper_ref, far_ref, reach_ref, state_ref):
+            if reach_ref is None:
+                row, col = iota2((BLK, BLK), 0), iota2((BLK, BLK), 1)
+                onward_ref[head] = jnp.where(row == col, 1.0, 0.0).astype(BF)
+            else:
+                onward_ref[head] = reach_ref[head]
+
+
+def join_top(upper_ref, far_ref, reach_ref, *rest):
+    state_refs, out_ref = rest[:-1], rest[-1]
+    levels = len(state_refs)
+    for level in range(levels):
+        for head in range(far_ref.shape[0]):
+            out_ref[head, :, level * BLK : (level + 1) * BLK] = state_refs[level][head]
+
     @pl.when(upper_ref[0] == 1)
     def _():
         for head in range(far_ref.shape[0]):
-            state_ref[head] = dot(reach_ref[head], far_ref[head]).astype(BF)
+            out_ref[head, :, levels * BLK :] = dot(reach_ref[head], far_ref[head]).astype(BF)
 
     @pl.when(upper_ref[0] == 0)
     def _():
-        state_ref[...] = jnp.zeros(state_ref.shape, BF)
+        for head in range(far_ref.shape[0]):
+            out_ref[head, :, levels * BLK :] = jnp.zeros((BLK, BLK), BF)
 
 
 def shape_of(shape, dtype):
@@ -302,17 +348,23 @@
     return pl.BlockSpec(shape, lambda i: (0,) * len(shape))
 
 
-def by_head(shape):
-    return pl.BlockSpec((HEADS_PER_STEP,) + shape, lambda i: (i,) + (0,) * len(shape))
-
-
-def by_column(shape):
+def by_head(shape, first=0, lane=0):
+    tail = (0,) * (len(shape) - 1) + (lane,)
+    return pl.BlockSpec((HEADS_PER_STEP,) + shape, lambda i: (i + first,) + tail)
+
+
+def by_column(shape, first=0):
     lead = len(shape) - 1
-    return pl.BlockSpec(shape, lambda i: (0,) * lead + (i,))
-
-
-VMEM = pl.BlockSpec(memory_space=pltpu.VMEM)
+    return pl.BlockSpec(shape, lambda i: (0,) * lead + (i + first,))
+
+
+ANY = pl.BlockSpec(memory_space=pl.ANY)
 SMEM = pl.BlockSpec(memory_space=pltpu.SMEM)
+JOIN_STEPS = 2
+
+
+def bit(position, level):
+    return (position // 2**level % 2).astype(jnp.int32).reshape(1)
 
 
 def per_device(q_in, k_in, v_in, z_in, log_gate, beta, level_weight, conv_weight, norm_gain):
@@ -320,6 +372,7 @@
     blocks = length // BLK
     width = HEADS_PER_STEP * BLK
     steps = heads // HEADS_PER_STEP
+    half = heads // 2
     ctx = lax.axis_size("ctx")
     levels = ctx.bit_length() - 1
     position = lax.axis_index("ctx")
@@ -331,8 +384,10 @@
     rows = jnp.stack([g.T, beta.T], axis=1)
     weights = level_weight[:, :, : levels + 1].reshape(length, heads * (levels + 1))
     weights = jnp.pad(weights, ((0, 0), (0, -weights.shape[1] % BLK)))
+    core = bit(position, 0)
 
     params = pltpu.CompilerParams(dimension_semantics=("arbitrary",), vmem_limit_bytes=60 << 20)
+    cost = pl.CostEstimate(flops=10**10, bytes_accessed=2 * 10**7, transcendentals=10**7)
     kt, uw, pair, sent, prior = pl.pallas_call(
         key_side,
         grid=(steps,),
@@ -354,70 +409,104 @@
             pltpu.VMEM((6, BLK, BLK), BF),
         ],
         compiler_params=params,
-        cost_estimate=pl.CostEstimate(flops=10**10, bytes_accessed=2 * 10**7, transcendentals=10**7),
+        cost_estimate=cost,
         name="key_side",
     )(rows, g_pad, conv_weight, halo, k_in, v_in)
-
-    carried, local = pl.pallas_call(
-        query_side,
-        grid=(steps,),
-        in_specs=[
-            by_head((2, length)), whole(g_pad.shape), by_column((3, 4, width)),
-            by_column((3, 4, width)), by_column((length, width)), by_head((BLK, length)),
-            by_head((length, 2 * BLK)), by_head((blocks - 1, BLK, 2 * BLK)),
-        ],
-        out_specs=[by_column((length, width)), by_column((length, width))],
-        out_shape=[shape_of(q_in.shape, BF), shape_of(q_in.shape, BF)],
-        scratch_shapes=[pltpu.VMEM((HEADS_PER_STEP, length + 8, BLK), F32)],
-        compiler_params=params,
-        cost_estimate=pl.CostEstimate(flops=10**10, bytes_accessed=2 * 10**7, transcendentals=10**7),
-        name="query_side",
-    )(rows, g_pad, conv_weight, halo, q_in, kt, uw, prior)
-
-    reach = jnp.broadcast_to(jnp.eye(BLK, dtype=BF), (heads, BLK, BLK))
-    states = []
-    square = (heads, BLK, BLK)
-    for level in range(levels - 1):
+    near = lax.ppermute(sent, "ctx", [(i, i ^ 1) for i in range(ctx)])
+
+    def queries_of(first, queries, previous):
+        count = len(previous)
+        scaled_width = width * (levels - 1)
+        return pl.pallas_call(
+            functools.partial(query_side, first_step=first),
+            grid=(steps // 2,),
+            in_specs=[
+                SMEM, by_head((2, length), first), whole(g_pad.shape), whole(weights.shape),
+                by_column((3, 4, width), first), by_column((3, 4, width), first),
+                by_column((length, width), first), by_head((BLK, length), first),
+                by_head((length, 2 * BLK), first), by_head((blocks - 1, BLK, 2 * BLK), first),
+                by_head((BLK, BLK), first, 1),
+            ]
+            + [ANY] * count,
+            out_specs=[by_column((length, scaled_width), first), by_column((length, width), first)],
+            out_shape=[
+                shape_of((length, heads * (levels - 1) * BLK), BF), shape_of(q_in.shape, F32)
+            ],
+            scratch_shapes=[pltpu.VMEM((HEADS_PER_STEP, length + 8, BLK), F32)],
+            input_output_aliases={11 + i: i for i in range(count)},
+            compiler_params=params,
+            cost_estimate=cost,
+            name="query_side",
+        )(
+            core, rows, g_pad, weights, conv_weight, halo, queries, kt, uw, prior, near, *previous
+        )
+
+    group = half // JOIN_STEPS
+    joined_shapes = [
+        shape_of((half, BLK, 2 * BLK), F32), shape_of((half, BLK, 2 * BLK), BF),
+    ]
+
+    def part(lanes):
+        return pl.BlockSpec((group, BLK, lanes), lambda i, *_: (i, 0, 0))
+
+    chosen = pl.BlockSpec((group, BLK, 2 * BLK), lambda i, which: (which[0] * JOIN_STEPS + i, 0, 0))
+    pair, sent = pl.pallas_call(
+        join_near,
+        grid_spec=pltpu.PrefetchScalarGridSpec(
+            num_scalar_prefetch=1, grid=(JOIN_STEPS,), in_specs=[chosen, chosen],
+            out_specs=[part(2 * BLK)] * 2,
+        ),
+        out_shape=joined_shapes,
+        name="join_near",
+    )(core, pair, near)
+
+    square = shape_of((half, BLK, BLK), BF)
+    reach, states, parts = None, [], ()
+    for level in range(1, levels - 1):
         far = lax.ppermute(sent, "ctx", [(i, i ^ 2**level) for i in range(ctx)])
-        upper = (position // 2**level % 2).astype(jnp.int32).reshape(1)
+        if level == 1:
+            parts = queries_of(0, q_in, ())
+            far, *parts = lax.optimization_barrier((far, *parts))
+        given = (pair, far) if reach is None else (pair, far, reach)
         pair, sent, state, reach = pl.pallas_call(
-            combine_side,
-            in_specs=[SMEM, VMEM, VMEM, VMEM],
-            out_specs=[VMEM] * 4,
-            out_shape=[
-                shape_of(pair.shape, F32), shape_of(pair.shape, BF), shape_of(square, BF),
-                shape_of(square, BF),
-            ],
-            name="combine",
-        )(upper, pair, far, reach)
+            join_far,
+            grid=(JOIN_STEPS,),
+            in_specs=[SMEM, part(2 * BLK), part(2 * BLK)] + [part(BLK)] * (len(given) - 2),
+            out_specs=[part(2 * BLK), part(2 * BLK), part(BLK), part(BLK)],
+            out_shape=joined_shapes + [square, square],
+            name="join_far",
+        )(bit(position, level), *given)
         states.append(state)
     top = levels - 1
-    far = lax.ppermute(
-        sent[:, :, BLK:], "ctx", [(i, i + 2**top) for i in range(ctx - 2**top)]
-    )
-    upper = (position // 2**top % 2).astype(jnp.int32).reshape(1)
-    states.append(
-        pl.pallas_call(
-            top_side,
-            in_specs=[SMEM, VMEM, VMEM],
-            out_specs=VMEM,
-            out_shape=shape_of(square, BF),
-            name="top",
-        )(upper, far, reach)
+    sent_b, later_q = lax.optimization_barrier((sent[:, :, BLK:], q_in))
+    far = lax.ppermute(sent_b, "ctx", [(i, i + 2**top) for i in range(ctx - 2**top)])
+    parts = queries_of(steps // 2, later_q, parts)
+    far, scaled, base = lax.optimization_barrier((far, *parts))
+    own = pl.pallas_call(
+        join_top,
+        grid=(JOIN_STEPS,),
+        in_specs=[SMEM] + [part(BLK)] * (2 + len(states)),
+        out_specs=part((levels - 1) * BLK),
+        out_shape=shape_of((half, BLK, (levels - 1) * BLK), BF),
+        name="join_top",
+    )(bit(position, top), far, reach, *states)
+    other = lax.ppermute(own, "ctx", [(i, i ^ 1) for i in range(ctx)])
+    fold = steps // 2
+    from_half = pl.BlockSpec(
+        (HEADS_PER_STEP, BLK, (levels - 1) * BLK), lambda i: (i % fold, 0, 0)
     )
     return pl.pallas_call(
         finish_side,
         grid=(steps,),
         in_specs=[
-            whole(weights.shape), whole((1, BLK)), by_column((length, width)),
-            by_column((length, width)), by_column((length, width)),
-        ]
-        + [by_head((BLK, BLK))] * levels,
+            SMEM, whole((1, BLK)), by_column((length, width)), by_column((length, width)),
+            by_column((length, width * (levels - 1))), by_head((BLK, BLK)), from_half, from_half,
+        ],
         out_specs=by_column((length, width)),
         out_shape=shape_of(z_in.shape, BF),
         compiler_params=params,
         name="finish_side",
-    )(weights, norm_gain.reshape(1, BLK), z_in, carried, local, *states)
+    )(core, norm_gain.reshape(1, BLK), z_in, base, scaled, near, own, other)
 
 
 def solution(mesh):

time: 130 us -> 98.3 us (0.76)
  the two profiles are of different devices: /device:TPU:24 before, /device:TPU:0 now
where the time goes in v1:
time: 98.3 us; the launch traced here: 97.6 us
  Pallas kernels  72 us (73%)
  starting transfers between devices  10.9 us (11%)
  local copies, waits for them, and re-layouts  10.7 us (11%)
  waiting for transfers between devices  3.62 us (4%)
    pallas_call x1, Pallas kernels, per_device(): pl.pallas_call(key_side, grid=(steps,), in_specs=[by_head((2, length)), w...  27.9 us
    pallas_call x2, Pallas kernels, queries_of(): pl.pallas_call(functools.partial(query_side, first_step=first), grid=(ste...  26.3 us
    pallas_call x1, Pallas kernels, per_device(): pl.pallas_call(finish_side, grid=(steps,), in_specs=[SMEM, whole((1, BLK)...  10.6 us
    unnamed x11, local copies, waits for them, and re-layouts  4.78 us
    ppermute x1, starting transfers between devices, per_device(): lax.ppermute(sent_b, 'ctx', [(i, i + 2 ** top) for i in range(ctx - 2 **...  4.2 us
    ppermute x1, starting transfers between devices, per_device(): near = lax.ppermute(sent, 'ctx', [(i, i ^ 1) for i in range(ctx)])  2.67 us
    pallas_call x1, Pallas kernels, per_device(): pl.pallas_call(join_far, grid=(JOIN_STEPS,), in_specs=[SMEM, part(2 * BLK...  2.67 us
    pallas_call x1, Pallas kernels, per_device(): pl.pallas_call(join_near, grid_spec=pltpu.PrefetchScalarGridSpec(num_scal...  2.5 us
  transfers between devices with their start and end apart: 5, of which 2 were waited for; matrix products, arithmetic and copies ran while one was open for 5% of the time, Pallas kernels for 27%

profile of v1, /device:TPU:0, one launch (start us, length us, event | category | flops | bytes accessed | tf_op | source)
XLA Modules:
  0.0 97.6 jit_solution(13065158697547599830)
XLA Ops:
  0.0 0.8 slice_bitcast_fusion.2
  0.8 0.8 slice_bitcast_fusion
  1.6 2.4 %collective-permute-start = (bf16[3,4,2048]{2,1,0:T(4,128)(2,1)S(1)}, bf16[3,4,2048]{2,1,0:T(4,128)(2,1)S(1)}, u32[]{:S(2)}, u32[]{:S(2)}) collective-permute-start(bf16[3,4,2048]{2,1,0:T(4,128)(2,1)S(1)} %pad_maximum_fusion.1), channel_id=1, source_target_pairs={{0,1},{1,2},{2,3},{3,4},{4,5},{5,6},{6,7},{8,9},{9,10},{10,11},{11... | collective-permute-start | bytes 147464 | tf_op jit(solution)/shard_map/ppermute | solution.py:380
  4.0 0.9 copy.39
  4.9 0.9 copy.33
  5.8 0.3 reduce_window_sum.11
  6.1 0.7 pad.8.g_ref
  6.8 0.8 copy.34.rows_ref
  7.6 0.0 slice-start
  7.6 0.0 collective-permute-done.halo_ref
  7.6 0.0 copy-start.4
  7.6 0.6 copy-done.4
  8.2 27.9 %key_side.1 = (bf16[16,128,512]{2,1,0:T(8,128)(2,1)}, bf16[16,512,256]{2,1,0:T(8,128)(2,1)}, f32[16,128,256]{2,1,0:T(8,128)}, bf16[16,128,256]{2,1,0:T(8,128)(2,1)}, bf16[16,3,128,256]{3,2,1,0:T(8,128)(2,1)}) custom-call(f32[16,2,512]{2,1,0:T(2,128)} %copy.34.rows_ref, f32[512,128]{1,0:T(8,128)} %pad.8.g_ref, f32[3,4,2048]{2,1,0:T(4,128)} %taps_ref.5, ...), custom_call_target="tpu_custom_call" | custom-call | flops 10000000000 | bytes 20000000 | tf_op jit(solution)/shard_map/key_side/pallas_call | solution.py:391
  36.1 2.7 %collective-permute-start.1 = (bf16[16,128,256]{2,1,0:T(8,128)(2,1)}, bf16[16,128,256]{2,1,0:T(8,128)(2,1)S(1)}, u32[]{:S(2)}, u32[]{:S(2)}) collective-permute-start(bf16[16,128,256]{2,1,0:T(8,128)(2,1)} %get-tuple-element.28), channel_id=1, source_target_pairs={{0,1},{1,0},{2,3},{3,2},{4,5},{5,4},{6,7},{7,6},{8,9},{9,8},{10,11... | collective-permute-start | bytes 3145736 | tf_op jit(solution)/shard_map/ppermute | solution.py:415
  38.8 0.0 slice-done
  38.8 0.1 copy.35
  38.9 0.1 copy.36
  39.1 0.7 pad.9.weight_ref
  39.8 1.5 %collective-permute-done.1.far_ref.near_ref = bf16[16,128,256]{2,1,0:T(8,128)(2,1)S(1)} collective-permute-done((bf16[16,128,256]{2,1,0:T(8,128)(2,1)}, bf16[16,128,256]{2,1,0:T(8,128)(2,1)S(1)}, u32[]{:S(2)}, u32[]{:S(2)}) %collective-permute-start.1) | collective-permute-done | bytes 1048608 | tf_op jit(solution)/shard_map/ppermute | solution.py:415
  41.3 0.0 copy-start
  41.3 1.0 %copy-done = bf16[16,128,256]{2,1,0:T(8,128)(2,1)} copy-done((bf16[16,128,256]{2,1,0:T(8,128)(2,1)}, bf16[16,128,256]{2,1,0:T(8,128)(2,1)S(1)}, u32[]{:S(2)}) %copy-start) | copy-done | bytes 1048600
  42.3 2.5 %join_near.1 = (f32[8,128,256]{2,1,0:T(8,128)}, bf16[8,128,256]{2,1,0:T(8,128)(2,1)}) custom-call(s32[1]{0:T(128)} %bitcast.core_ref.odd_ref, f32[16,128,256]{2,1,0:T(8,128)} %get-tuple-element.27.pair_ref, bf16[16,128,256]{2,1,0:T(8,128)(2,1)} %copy-done), custom_call_target="tpu_custom_call" | custom-call | tf_op jit(solution)/shard_map/join_near/pallas_call | solution.py:453
  44.8 1.6 %collective-permute-start.2 = (bf16[8,128,256]{2,1,0:T(8,128)(2,1)}, bf16[8,128,256]{2,1,0:T(8,128)(2,1)S(1)}, u32[]{:S(2)}, u32[]{:S(2)}) collective-permute-start(bf16[8,128,256]{2,1,0:T(8,128)(2,1)} %get-tuple-element.30), channel_id=1, source_target_pairs={{0,2},{1,3},{2,0},{3,1},{4,6},{5,7},{6,4},{7,5},{8,10},{9,11},{10,... | collective-permute-start | bytes 1572872 | tf_op jit(solution)/shard_map/ppermute | solution.py:466
  46.3 13.1 %query_side.2 = (bf16[512,4096]{1,0:T(8,128)(2,1)}, f32[512,2048]{1,0:T(8,128)}) custom-call(s32[1]{0:T(128)} %bitcast.core_ref.odd_ref, f32[16,2,512]{2,1,0:T(2,128)} %copy.34.rows_ref, f32[512,128]{1,0:T(8,128)} %pad.8.g_ref, f32[512,128]{1,0:T(8,128)} %pad.9.weight_ref, f32[3,4,2048]{2,1,0:T(4,128)} %taps_ref.5, bf16[3,4,2048]{2,1,0:T(4,128)(2,1)} %copy-done.4, ...), custom_call_target="tpu_custom_call" | custom-call | flops 10000000000 | bytes 20000000 | tf_op jit(solution)/shard_map/query_side/pallas_call | solution.py:420
  59.5 0.0 collective-permute-done.2.far_ref
  59.5 0.0 copy-start.1
  59.5 0.8 copy-done.1
  60.3 2.7 %join_far.1 = (f32[8,128,256]{2,1,0:T(8,128)}, bf16[8,128,256]{2,1,0:T(8,128)(2,1)}, bf16[8,128,128]{2,1,0:T(8,128)(2,1)}, bf16[8,128,128]{2,1,0:T(8,128)(2,1)}) custom-call(s32[1]{0:T(128)} %bitcast.2.upper_ref, f32[8,128,256]{2,1,0:T(8,128)} %get-tuple-element.29.pair_ref, bf16[8,128,256]{2,1,0:T(8,128)(2,1)} %copy-done.1), custom_call_target="tpu_custom_call" | custom-call | tf_op jit(solution)/shard_map/join_far/pallas_call | solution.py:471
  63.0 1.0 slice.19
  63.9 4.2 %collective-permute-start.3 = (bf16[8,128,128]{2,1,0:T(8,128)(2,1)S(1)}, bf16[8,128,128]{2,1,0:T(8,128)(2,1)S(1)}, u32[]{:S(2)}, u32[]{:S(2)}) collective-permute-start(bf16[8,128,128]{2,1,0:T(8,128)(2,1)S(1)} %slice.19), channel_id=1, source_target_pairs={{0,4},{1,5},{2,6},{3,7},{8,12},{9,13},{10,14},{11,15},{16,20},{17,... | collective-permute-start | bytes 786440 | tf_op jit(solution)/shard_map/ppermute | solution.py:482
  68.1 13.2 %query_side.3 = (bf16[512,4096]{1,0:T(8,128)(2,1)}, f32[512,2048]{1,0:T(8,128)}) custom-call(s32[1]{0:T(128)} %bitcast.core_ref.odd_ref, f32[16,2,512]{2,1,0:T(2,128)} %copy.34.rows_ref, f32[512,128]{1,0:T(8,128)} %pad.8.g_ref, f32[512,128]{1,0:T(8,128)} %pad.9.weight_ref, f32[3,4,2048]{2,1,0:T(4,128)} %taps_ref.5, ...), custom_call_target="tpu_custom_call", output_to_operand_aliasing={{0}: (11, {}), {1}: (12, {})} | custom-call | flops 10000000000 | bytes 20000000 | tf_op jit(solution)/shard_map/query_side/pallas_call | solution.py:420
  81.3 0.0 collective-permute-done.3.far_ref
  81.3 0.0 copy-start.3
  81.3 0.7 copy-done.3
  82.0 2.0 %join_top.1.own_ref = bf16[8,128,256]{2,1,0:T(8,128)(2,1)} custom-call(s32[1]{0:T(128)} %bitcast.12.upper_ref, bf16[8,128,128]{2,1,0:T(8,128)(2,1)} %copy-done.3, bf16[8,128,128]{2,1,0:T(8,128)(2,1)} %get-tuple-element.47.reach_ref, bf16[8,128,128]{2,1,0:T(8,128)(2,1)} %get-tuple-element.48.rest_0_), custom_call_target="tpu_custom_call" | custom-call | tf_op jit(solution)/shard_map/join_top/pallas_call | solution.py:485
  84.0 0.0 collective-permute-start.4
  84.0 2.1 %collective-permute-done.4.other_ref = bf16[8,128,256]{2,1,0:T(8,128)(2,1)S(1)} collective-permute-done((bf16[8,128,256]{2,1,0:T(8,128)(2,1)}, bf16[8,128,256]{2,1,0:T(8,128)(2,1)S(1)}, u32[]{:S(2)}, u32[]{:S(2)}) %collective-permute-start.4) | collective-permute-done | bytes 524320 | tf_op jit(solution)/shard_map/ppermute | solution.py:493
  86.1 0.0 copy-start.2
  86.1 0.8 copy-done.2
  86.9 10.6 %finish_side.1 = bf16[512,2048]{1,0:T(8,128)(2,1)} custom-call(s32[1]{0:T(128)} %bitcast.core_ref.odd_ref, f32[1,128]{1,0:T(1,128)} %bitcast.25, bf16[512,2048]{1,0:T(8,128)(2,1)} %z_ref.1, f32[512,2048]{1,0:T(8,128)} %get-tuple-element.44.base_ref, bf16[512,4096]{1,0:T(8,128)(2,1)} %get-tuple-element.45.scaled_ref, bf16[16,128,256]{2,1,0:T(8,128)(2,1)} %copy-done, ...), custom_call_target="tpu_custom_call" | custom-call | tf_op jit(solution)/shard_map/finish_side/pallas_call | solution.py:498
  (3 shorter events, 0.1 us)
Async XLA Ops:
  1.6 6.0 %collective-permute-start = (bf16[3,4,2048]{2,1,0:T(4,128)(2,1)S(1)}, bf16[3,4,2048]{2,1,0:T(4,128)(2,1)S(1)}, u32[]{:S(2)}, u32[]{:S(2)}) collective-permute-start(bf16[3,4,2048]{2,1,0:T(4,128)(2,1)S(1)} %pad_maximum_fusion.1), channel_id=1, source_target_pairs={{0,1},{1,2},{2,3},{3,4},{4,5},{5,6},{6,7},{8,9},{9,10},{10,11},{11... | collective-permute-start | bytes 147464 | tf_op jit(solution)/shard_map/ppermute | solution.py:380
  7.6 31.2 %slice-start = ((f32[512,16,6]{0,1,2:T(8,128)}), f32[512,16,4]{0,1,2:T(8,128)S(1)}, s32[]{:S(2)}) async-start(f32[512,16,6]{0,1,2:T(8,128)} %param.15), calls=%async_computation | async-start | bytes 262144 | tf_op jit(solution)/shard_map/slice | solution.py:385
  7.6 0.6 copy-start.4
  36.1 5.2 %collective-permute-start.1 = (bf16[16,128,256]{2,1,0:T(8,128)(2,1)}, bf16[16,128,256]{2,1,0:T(8,128)(2,1)S(1)}, u32[]{:S(2)}, u32[]{:S(2)}) collective-permute-start(bf16[16,128,256]{2,1,0:T(8,128)(2,1)} %get-tuple-element.28), channel_id=1, source_target_pairs={{0,1},{1,0},{2,3},{3,2},{4,5},{5,4},{6,7},{7,6},{8,9},{9,8},{10,11... | collective-permute-start | bytes 3145736 | tf_op jit(solution)/shard_map/ppermute | solution.py:415
  41.3 1.0 %copy-start = (bf16[16,128,256]{2,1,0:T(8,128)(2,1)}, bf16[16,128,256]{2,1,0:T(8,128)(2,1)S(1)}, u32[]{:S(2)}) copy-start(bf16[16,128,256]{2,1,0:T(8,128)(2,1)S(1)} %collective-permute-done.1.far_ref.near_ref) | copy-start | bytes 3145732
  44.8 14.7 %collective-permute-start.2 = (bf16[8,128,256]{2,1,0:T(8,128)(2,1)}, bf16[8,128,256]{2,1,0:T(8,128)(2,1)S(1)}, u32[]{:S(2)}, u32[]{:S(2)}) collective-permute-start(bf16[8,128,256]{2,1,0:T(8,128)(2,1)} %get-tuple-element.30), channel_id=1, source_target_pairs={{0,2},{1,3},{2,0},{3,1},{4,6},{5,7},{6,4},{7,5},{8,10},{9,11},{10,... | collective-permute-start | bytes 1572872 | tf_op jit(solution)/shard_map/ppermute | solution.py:466
  59.5 0.8 copy-start.1
  63.9 17.4 %collective-permute-start.3 = (bf16[8,128,128]{2,1,0:T(8,128)(2,1)S(1)}, bf16[8,128,128]{2,1,0:T(8,128)(2,1)S(1)}, u32[]{:S(2)}, u32[]{:S(2)}) collective-permute-start(bf16[8,128,128]{2,1,0:T(8,128)(2,1)S(1)} %slice.19), channel_id=1, source_target_pairs={{0,4},{1,5},{2,6},{3,7},{8,12},{9,13},{10,14},{11,15},{16,20},{17,... | collective-permute-start | bytes 786440 | tf_op jit(solution)/shard_map/ppermute | solution.py:482
  81.3 0.7 copy-start.3
  84.0 2.1 %collective-permute-start.4 = (bf16[8,128,256]{2,1,0:T(8,128)(2,1)}, bf16[8,128,256]{2,1,0:T(8,128)(2,1)S(1)}, u32[]{:S(2)}, u32[]{:S(2)}) collective-permute-start(bf16[8,128,256]{2,1,0:T(8,128)(2,1)} %join_top.1.own_ref), channel_id=1, source_target_pairs={{0,1},{1,0},{2,3},{3,2},{4,5},{5,4},{6,7},{7,6},{8,9},{9,8},{10,11... | collective-permute-start | bytes 1572872 | tf_op jit(solution)/shard_map/ppermute | solution.py:493
  86.1 0.8 copy-start.2

commit v2 on v1

--- a/solution.py
+++ b/solution.py
@@ -9,7 +9,9 @@
 
 BLK = 128
 SUB = 16
-HEADS_PER_STEP = 2
+KEY_HEADS = 4
+QUERY_HEADS = 2
+FINISH_HEADS = 4
 EPS = 1e-06
 BF = jnp.bfloat16
 F32 = jnp.float32
@@ -129,7 +131,7 @@
 
 def key_side(
     rows_ref, g_ref, taps_ref, halo_ref, k_ref, v_ref,
-    kt_ref, uw_ref, pair_ref, sent_ref, prior_ref, pad_ref, mask_ref,
+    kt_ref, uw_ref, pair_ref, prior_ref, pad_ref, mask_ref,
 ):
     step = pl.program_id(0)
 
@@ -139,9 +141,9 @@
 
     length = k_ref.shape[0]
     blocks = length // BLK
-    turned_g = pltpu.roll(g_ref[...], BLK - HEADS_PER_STEP * step, 1)
+    turned_g = pltpu.roll(g_ref[...], BLK - KEY_HEADS * step, 1)
     lowers, rights, tails, lasts = [], [], [], []
-    for head in range(HEADS_PER_STEP):
+    for head in range(KEY_HEADS):
         lanes = slice(head * BLK, (head + 1) * BLK)
         fill_padded(pad_ref, 2 * head, k_ref, halo_ref[1, :, lanes], lanes)
         fill_padded(pad_ref, 2 * head + 1, v_ref, halo_ref[2, :, lanes], lanes)
@@ -166,14 +168,14 @@
             lasts.append(jnp.exp(g_last))
     solved = inverses(lowers, mask_ref)
     maps = []
-    for head in range(HEADS_PER_STEP):
+    for head in range(KEY_HEADS):
         for block in range(blocks):
             i = head * blocks + block
             fresh = dot(solved[i].astype(BF), rights[i]).astype(BF)
             uw_ref[head, block * BLK : (block + 1) * BLK, :] = fresh
             maps.append(dot(tails[i], fresh))
     eye = jnp.where(iota2((BLK, BLK), 0) == iota2((BLK, BLK), 1), 1.0, 0.0).astype(F32)
-    for head in range(HEADS_PER_STEP):
+    for head in range(KEY_HEADS):
         i = head * blocks
         state_a = lasts[i] * eye - maps[i][:, BLK:]
         state_b = maps[i][:, :BLK]
@@ -186,8 +188,7 @@
             state_a = state[:, :BLK]
             state_b = state[:, BLK:] + maps[i][:, :BLK]
         state = jnp.concatenate([state_a, state_b], axis=1)
-        pair_ref[head] = state
-        sent_ref[head] = state.astype(BF)
+        pair_ref[head] = state.astype(BF)
 
 
 def query_side(
@@ -198,13 +199,13 @@
     step = pl.program_id(0) + first_step
     length = q_ref.shape[0]
     blocks = length // BLK
-    levels = scaled_ref.shape[1] // (HEADS_PER_STEP * BLK) + 1
+    levels = scaled_ref.shape[1] // (QUERY_HEADS * BLK) + 1
     per_head = levels + 1
     width = weight_ref.shape[1]
     odd = odd_ref[0].astype(F32)
-    turned_g = pltpu.roll(g_ref[...], BLK - HEADS_PER_STEP * step, 1)
-    turned_w = pltpu.roll(weight_ref[...], width - HEADS_PER_STEP * per_head * step, 1)
-    for head in range(HEADS_PER_STEP):
+    turned_g = pltpu.roll(g_ref[...], BLK - QUERY_HEADS * step, 1)
+    turned_w = pltpu.roll(weight_ref[...], width - QUERY_HEADS * per_head * step, 1)
+    for head in range(QUERY_HEADS):
         lanes = slice(head * BLK, (head + 1) * BLK)
         fill_padded(pad_ref, head, q_ref, halo_ref[0, :, lanes], lanes)
         near = near_ref[head] * odd.astype(BF)
@@ -240,19 +241,27 @@
 
 
 def finish_side(
-    core_ref, gain_ref, z_ref, base_ref, scaled_ref, near_ref, own_ref, other_ref, out_ref
+    core_ref, gain_ref, z_ref, base_ref, scaled_ref, near_ref, own_ref, far_ref, out_ref,
+    other_ref, sem,
 ):
     step = pl.program_id(0)
     core = core_ref[0]
     length = z_ref.shape[0]
     blocks = length // BLK
     levels = own_ref.shape[2] // BLK
-    mine = step // (pl.num_programs(0) // 2) == core
+    fold = pl.num_programs(0) // 2
+    mine = step // fold == core
+    begin_head = step % fold * FINISH_HEADS
+
+    @pl.when(step == 0)
+    def _():
+        fetch([(far_ref, other_ref)], sem)
+
     eye = jnp.where(iota2((BLK, BLK), 0) == iota2((BLK, BLK), 1), 1.0, 0.0).astype(BF)
-    for head in range(HEADS_PER_STEP):
+    for head in range(FINISH_HEADS):
         lanes = slice(head * BLK, (head + 1) * BLK)
         reach = jnp.where(core == 1, near_ref[head], eye)
-        seen = dot(reach, jnp.where(mine, own_ref[head], other_ref[head])).astype(BF)
+        seen = dot(reach, jnp.where(mine, own_ref[head], other_ref[begin_head + head])).astype(BF)
         states = jnp.concatenate(
             [seen[:, level * BLK : (level + 1) * BLK] for level in range(levels)], axis=0
         )
@@ -273,70 +282,77 @@
     return jnp.concatenate([moved[:, :BLK], moved[:, BLK:] + right_b.astype(F32)], axis=1)
 
 
-def join_near(core_ref, pair_ref, far_ref, next_ref, sent_ref):
-    @pl.when(core_ref[0] == 1)
-    def _():
-        for head in range(pair_ref.shape[0]):
-            own = pair_ref[head]
-            joined = merged(far_ref[head], own[:, :BLK], own[:, BLK:])
-            next_ref[head] = joined
-            sent_ref[head] = joined.astype(BF)
-
-    @pl.when(core_ref[0] == 0)
-    def _():
-        for head in range(pair_ref.shape[0]):
-            far = far_ref[head]
-            joined = merged(pair_ref[head], far[:, :BLK], far[:, BLK:])
-            next_ref[head] = joined
-            sent_ref[head] = joined.astype(BF)
+def fetch(pairs, sem):
+    copies = [
+        pltpu.make_async_copy(source, target, sem.at[i])
+        for i, (source, target) in enumerate(pairs)
+    ]
+    for copy in copies:
+        copy.start()
+    for copy in copies:
+        copy.wait()
+
+
+def join_near(core_ref, pair_ref, far_ref, next_ref, own, far, sem):
+    core = core_ref[0]
+    half = pl.ds(core * own.shape[0], own.shape[0])
+    fetch([(pair_ref.at[half], own), (far_ref.at[half], far)], sem)
+
+    @pl.when(core == 1)
+    def _():
+        for head in range(own.shape[0]):
+            next_ref[head] = merged(far[head], own[head, :, :BLK], own[head, :, BLK:]).astype(BF)
+
+    @pl.when(core == 0)
+    def _():
+        for head in range(own.shape[0]):
+            next_ref[head] = merged(own[head], far[head, :, :BLK], far[head, :, BLK:]).astype(BF)
 
 
 def join_far(upper_ref, pair_ref, far_ref, *rest):
-    next_ref, sent_ref, state_ref, onward_ref = rest[-4:]
-    reach_ref = rest[0] if len(rest) == 5 else None
+    next_ref, state_ref, onward_ref, own, far, sem = rest[-6:]
+    reach_ref = rest[0] if len(rest) == 7 else None
+    lanes = slice(2 * BLK - next_ref.shape[2], 2 * BLK)
+    fetch([(pair_ref, own), (far_ref, far)], sem)
 
     @pl.when(upper_ref[0] == 1)
     def _():
-        for head in range(pair_ref.shape[0]):
-            far = far_ref[head]
-            own = pair_ref[head]
-            seen = far if reach_ref is None else dot(reach_ref[head], far).astype(BF)
+        for head in range(own.shape[0]):
+            seen = far[head] if reach_ref is None else dot(reach_ref[head], far[head]).astype(BF)
             onward_ref[head] = seen[:, :BLK]
             state_ref[head] = seen[:, BLK:]
-            joined = merged(far, own[:, :BLK], own[:, BLK:])
-            next_ref[head] = joined
-            sent_ref[head] = joined.astype(BF)
+            joined = merged(far[head], own[head, :, :BLK], own[head, :, BLK:]).astype(BF)
+            next_ref[head] = joined[:, lanes]
 
     @pl.when(upper_ref[0] == 0)
     def _():
-        for head in range(pair_ref.shape[0]):
-            far = far_ref[head]
-            joined = merged(pair_ref[head], far[:, :BLK], far[:, BLK:])
-            next_ref[head] = joined
-            sent_ref[head] = joined.astype(BF)
+        row, col = iota2((BLK, BLK), 0), iota2((BLK, BLK), 1)
+        for head in range(own.shape[0]):
+            joined = merged(own[head], far[head, :, :BLK], far[head, :, BLK:]).astype(BF)
+            next_ref[head] = joined[:, lanes]
             state_ref[head] = jnp.zeros((BLK, BLK), BF)
             if reach_ref is None:
-                row, col = iota2((BLK, BLK), 0), iota2((BLK, BLK), 1)
                 onward_ref[head] = jnp.where(row == col, 1.0, 0.0).astype(BF)
             else:
                 onward_ref[head] = reach_ref[head]
 
 
 def join_top(upper_ref, far_ref, reach_ref, *rest):
-    state_refs, out_ref = rest[:-1], rest[-1]
+    state_refs, (out_ref, far, sem) = rest[:-3], rest[-3:]
     levels = len(state_refs)
+    fetch([(far_ref, far)], sem)
     for level in range(levels):
-        for head in range(far_ref.shape[0]):
+        for head in range(far.shape[0]):
             out_ref[head, :, level * BLK : (level + 1) * BLK] = state_refs[level][head]
 
     @pl.when(upper_ref[0] == 1)
     def _():
-        for head in range(far_ref.shape[0]):
-            out_ref[head, :, levels * BLK :] = dot(reach_ref[head], far_ref[head]).astype(BF)
+        for head in range(far.shape[0]):
+            out_ref[head, :, levels * BLK :] = dot(reach_ref[head], far[head]).astype(BF)
 
     @pl.when(upper_ref[0] == 0)
     def _():
-        for head in range(far_ref.shape[0]):
+        for head in range(far.shape[0]):
             out_ref[head, :, levels * BLK :] = jnp.zeros((BLK, BLK), BF)
 
 
@@ -348,9 +364,9 @@
     return pl.BlockSpec(shape, lambda i: (0,) * len(shape))
 
 
-def by_head(shape, first=0, lane=0):
+def by_head(count, shape, first=0, lane=0):
     tail = (0,) * (len(shape) - 1) + (lane,)
-    return pl.BlockSpec((HEADS_PER_STEP,) + shape, lambda i: (i + first,) + tail)
+    return pl.BlockSpec((count,) + shape, lambda i: (i + first,) + tail)
 
 
 def by_column(shape, first=0):
@@ -360,19 +376,144 @@
 
 ANY = pl.BlockSpec(memory_space=pl.ANY)
 SMEM = pl.BlockSpec(memory_space=pltpu.SMEM)
-JOIN_STEPS = 2
+VMEM = pl.BlockSpec(memory_space=pltpu.VMEM)
+COST = pl.CostEstimate(flops=10**10, bytes_accessed=2 * 10**7, transcendentals=10**7)
+PARAMS = pltpu.CompilerParams(dimension_semantics=("arbitrary",), vmem_limit_bytes=62 << 20)
+
+SMALL = pltpu.CompilerParams(vmem_limit_bytes=8 << 20)
 
 
 def bit(position, level):
     return (position // 2**level % 2).astype(jnp.int32).reshape(1)
+
+
+def keys_of(rows, g_pad, conv_weight, halo, k_in, v_in):
+    heads, _, length = rows.shape
+    blocks = length // BLK
+    width = KEY_HEADS * BLK
+    return pl.pallas_call(
+        key_side,
+        grid=(heads // KEY_HEADS,),
+        in_specs=[
+            by_head(KEY_HEADS, (2, length)), whole(g_pad.shape), by_column((3, 4, width)),
+            by_column((3, 4, width)), by_column((length, width)), by_column((length, width)),
+        ],
+        out_specs=[
+            by_head(KEY_HEADS, (BLK, length)), by_head(KEY_HEADS, (length, 2 * BLK)),
+            by_head(KEY_HEADS, (BLK, 2 * BLK)), by_head(KEY_HEADS, (blocks - 1, BLK, 2 * BLK)),
+        ],
+        out_shape=[
+            shape_of((heads, BLK, length), BF), shape_of((heads, length, 2 * BLK), BF),
+            shape_of((heads, BLK, 2 * BLK), BF), shape_of((heads, blocks - 1, BLK, 2 * BLK), BF),
+        ],
+        scratch_shapes=[
+            pltpu.VMEM((2 * KEY_HEADS, length + 8, BLK), F32),
+            pltpu.VMEM((6, BLK, BLK), BF),
+        ],
+        compiler_params=PARAMS,
+        cost_estimate=COST,
+        name="key_side",
+    )(rows, g_pad, conv_weight, halo, k_in, v_in)
+
+
+def queries_of(second, levels, core, rows, g_pad, weights, taps, halo, q_in, kt, uw, prior, near, previous):
+    heads, _, length = rows.shape
+    blocks = length // BLK
+    steps = heads // QUERY_HEADS // 2
+    first = steps if second else 0
+    width = QUERY_HEADS * BLK
+    scaled_width = width * (levels - 1)
+    count = len(previous)
+    return pl.pallas_call(
+        functools.partial(query_side, first_step=first),
+        grid=(steps,),
+        in_specs=[
+            SMEM, by_head(QUERY_HEADS, (2, length), first), whole(g_pad.shape),
+            whole(weights.shape), by_column((3, 4, width), first), by_column((3, 4, width), first),
+            by_column((length, width), first), by_head(QUERY_HEADS, (BLK, length), first),
+            by_head(QUERY_HEADS, (length, 2 * BLK), first),
+            by_head(QUERY_HEADS, (blocks - 1, BLK, 2 * BLK), first),
+            by_head(QUERY_HEADS, (BLK, BLK), first, 1),
+        ]
+        + [ANY] * count,
+        out_specs=[by_column((length, scaled_width), first), by_column((length, width), first)],
+        out_shape=[shape_of((length, heads * (levels - 1) * BLK), BF), shape_of(q_in.shape, F32)],
+        scratch_shapes=[pltpu.VMEM((QUERY_HEADS, length + 8, BLK), F32)],
+        input_output_aliases={11 + i: i for i in range(count)},
+        compiler_params=PARAMS,
+        cost_estimate=COST,
+        name="query_side",
+    )(core, rows, g_pad, weights, taps, halo, q_in, kt, uw, prior, near, *previous)
+
+
+def finished(core, gain, z_in, base, scaled, near, own, other):
+    length = z_in.shape[0]
+    heads, levels = near.shape[0], own.shape[2] // BLK
+    width = FINISH_HEADS * BLK
+    fold = heads // FINISH_HEADS // 2
+    return pl.pallas_call(
+        finish_side,
+        grid=(2 * fold,),
+        in_specs=[
+            SMEM, whole(gain.shape), by_column((length, width)), by_column((length, width)),
+            by_column((length, width * levels)), by_head(FINISH_HEADS, (BLK, BLK)),
+            pl.BlockSpec((FINISH_HEADS, BLK, levels * BLK), lambda i: (i % fold, 0, 0)), ANY,
+        ],
+        out_specs=by_column((length, width)),
+        out_shape=shape_of(z_in.shape, BF),
+        scratch_shapes=[pltpu.VMEM(other.shape, BF), pltpu.SemaphoreType.DMA((1,))],
+        compiler_params=PARAMS,
+        name="finish_side",
+    )(core, gain, z_in, base, scaled, near, own, other)
+
+
+def joined_near(core, pair, near):
+    shape = (pair.shape[0] // 2,) + pair.shape[1:]
+    return pl.pallas_call(
+        join_near,
+        in_specs=[SMEM, ANY, ANY],
+        out_specs=VMEM,
+        out_shape=shape_of(shape, BF),
+        scratch_shapes=[
+            pltpu.VMEM(shape, BF), pltpu.VMEM(shape, BF), pltpu.SemaphoreType.DMA((2,)),
+        ],
+        compiler_params=SMALL,
+        name="join_near",
+    )(core, pair, near)
+
+
+def joined_far(upper, pair, far, reach, last):
+    square = (pair.shape[0], BLK, BLK)
+    given = () if reach is None else (reach,)
+    return pl.pallas_call(
+        join_far,
+        in_specs=[SMEM, ANY, ANY] + [VMEM] * len(given),
+        out_specs=[VMEM] * 3,
+        out_shape=[shape_of(square if last else pair.shape, BF)] + [shape_of(square, BF)] * 2,
+        scratch_shapes=[
+            pltpu.VMEM(pair.shape, BF), pltpu.VMEM(pair.shape, BF), pltpu.SemaphoreType.DMA((2,)),
+        ],
+        compiler_params=SMALL,
+        name="join_far",
+    )(upper, pair, far, *given)
+
+
+def joined_top(upper, far, reach, states):
+    shape = (far.shape[0], BLK, (len(states) + 1) * BLK)
+    return pl.pallas_call(
+        join_top,
+        in_specs=[SMEM, ANY] + [VMEM] * (1 + len(states)),
+        out_specs=VMEM,
+        out_shape=shape_of(shape, BF),
+        scratch_shapes=[pltpu.VMEM(far.shape, BF), pltpu.SemaphoreType.DMA((1,))],
+        compiler_params=SMALL,
+        name="join_top",
+    )(upper, far, reach, *states)
 
 
 def per_device(q_in, k_in, v_in, z_in, log_gate, beta, level_weight, conv_weight, norm_gain):
     length, heads = log_gate.shape
     blocks = length // BLK
-    width = HEADS_PER_STEP * BLK
-    steps = heads // HEADS_PER_STEP
-    half = heads // 2
     ctx = lax.axis_size("ctx")
     levels = ctx.bit_length() - 1
     position = lax.axis_index("ctx")
@@ -386,127 +527,32 @@
     weights = jnp.pad(weights, ((0, 0), (0, -weights.shape[1] % BLK)))
     core = bit(position, 0)
 
-    params = pltpu.CompilerParams(dimension_semantics=("arbitrary",), vmem_limit_bytes=60 << 20)
-    cost = pl.CostEstimate(flops=10**10, bytes_accessed=2 * 10**7, transcendentals=10**7)
-    kt, uw, pair, sent, prior = pl.pallas_call(
-        key_side,
-        grid=(steps,),
-        in_specs=[
-            by_head((2, length)), whole(g_pad.shape), by_column((3, 4, width)),
-            by_column((3, 4, width)), by_column((length, width)), by_column((length, width)),
-        ],
-        out_specs=[
-            by_head((BLK, length)), by_head((length, 2 * BLK)), by_head((BLK, 2 * BLK)),
-            by_head((BLK, 2 * BLK)), by_head((blocks - 1, BLK, 2 * BLK)),
-        ],
-        out_shape=[
-            shape_of((heads, BLK, length), BF), shape_of((heads, length, 2 * BLK), BF),
-            shape_of((heads, BLK, 2 * BLK), F32), shape_of((heads, BLK, 2 * BLK), BF),
-            shape_of((heads, blocks - 1, BLK, 2 * BLK), BF),
-        ],
-        scratch_shapes=[
-            pltpu.VMEM((2 * HEADS_PER_STEP, length + 8, BLK), F32),
-            pltpu.VMEM((6, BLK, BLK), BF),
-        ],
-        compiler_params=params,
-        cost_estimate=cost,
-        name="key_side",
-    )(rows, g_pad, conv_weight, halo, k_in, v_in)
-    near = lax.ppermute(sent, "ctx", [(i, i ^ 1) for i in range(ctx)])
-
-    def queries_of(first, queries, previous):
-        count = len(previous)
-        scaled_width = width * (levels - 1)
-        return pl.pallas_call(
-            functools.partial(query_side, first_step=first),
-            grid=(steps // 2,),
-            in_specs=[
-                SMEM, by_head((2, length), first), whole(g_pad.shape), whole(weights.shape),
-                by_column((3, 4, width), first), by_column((3, 4, width), first),
-                by_column((length, width), first), by_head((BLK, length), first),
-                by_head((length, 2 * BLK), first), by_head((blocks - 1, BLK, 2 * BLK), first),
-                by_head((BLK, BLK), first, 1),
-            ]
-            + [ANY] * count,
-            out_specs=[by_column((length, scaled_width), first), by_column((length, width), first)],
-            out_shape=[
-                shape_of((length, heads * (levels - 1) * BLK), BF), shape_of(q_in.shape, F32)
-            ],
-            scratch_shapes=[pltpu.VMEM((HEADS_PER_STEP, length + 8, BLK), F32)],
-            input_output_aliases={11 + i: i for i in range(count)},
-            compiler_params=params,
-            cost_estimate=cost,
-            name="query_side",
-        )(
-            core, rows, g_pad, weights, conv_weight, halo, queries, kt, uw, prior, near, *previous
+    kt, uw, pair, prior = keys_of(rows, g_pad, conv_weight, halo, k_in, v_in)
+    near = lax.ppermute(pair, "ctx", [(i, i ^ 1) for i in range(ctx)])
+    pair = joined_near(core, pair, near)
+
+    def queries(second, q_in, previous):
+        return queries_of(
+            second, levels, core, rows, g_pad, weights, conv_weight, halo, q_in, kt, uw, prior,
+            near, previous,
         )
 
-    group = half // JOIN_STEPS
-    joined_shapes = [
-        shape_of((half, BLK, 2 * BLK), F32), shape_of((half, BLK, 2 * BLK), BF),
-    ]
-
-    def part(lanes):
-        return pl.BlockSpec((group, BLK, lanes), lambda i, *_: (i, 0, 0))
-
-    chosen = pl.BlockSpec((group, BLK, 2 * BLK), lambda i, which: (which[0] * JOIN_STEPS + i, 0, 0))
-    pair, sent = pl.pallas_call(
-        join_near,
-        grid_spec=pltpu.PrefetchScalarGridSpec(
-            num_scalar_prefetch=1, grid=(JOIN_STEPS,), in_specs=[chosen, chosen],
-            out_specs=[part(2 * BLK)] * 2,
-        ),
-        out_shape=joined_shapes,
-        name="join_near",
-    )(core, pair, near)
-
-    square = shape_of((half, BLK, BLK), BF)
     reach, states, parts = None, [], ()
     for level in range(1, levels - 1):
-        far = lax.ppermute(sent, "ctx", [(i, i ^ 2**level) for i in range(ctx)])
+        far = lax.ppermute(pair, "ctx", [(i, i ^ 2**level) for i in range(ctx)])
         if level == 1:
-            parts = queries_of(0, q_in, ())
+            parts = queries(False, q_in, ())
             far, *parts = lax.optimization_barrier((far, *parts))
-        given = (pair, far) if reach is None else (pair, far, reach)
-        pair, sent, state, reach = pl.pallas_call(
-            join_far,
-            grid=(JOIN_STEPS,),
-            in_specs=[SMEM, part(2 * BLK), part(2 * BLK)] + [part(BLK)] * (len(given) - 2),
-            out_specs=[part(2 * BLK), part(2 * BLK), part(BLK), part(BLK)],
-            out_shape=joined_shapes + [square, square],
-            name="join_far",
-        )(bit(position, level), *given)
+        pair, state, reach = joined_far(bit(position, level), pair, far, reach, level == levels - 2)
         states.append(state)
     top = levels - 1
-    sent_b, later_q = lax.optimization_barrier((sent[:, :, BLK:], q_in))
-    far = lax.ppermute(sent_b, "ctx", [(i, i + 2**top) for i in range(ctx - 2**top)])
-    parts = queries_of(steps // 2, later_q, parts)
+    pair, later_q = lax.optimization_barrier((pair, q_in))
+    far = lax.ppermute(pair, "ctx", [(i, i + 2**top) for i in range(ctx - 2**top)])
+    parts = queries(True, later_q, parts)
     far, scaled, base = lax.optimization_barrier((far, *parts))
-    own = pl.pallas_call(
-        join_top,
-        grid=(JOIN_STEPS,),
-        in_specs=[SMEM] + [part(BLK)] * (2 + len(states)),
-        out_specs=part((levels - 1) * BLK),
-        out_shape=shape_of((half, BLK, (levels - 1) * BLK), BF),
-        name="join_top",
-    )(bit(position, top), far, reach, *states)
+    own = joined_top(bit(position, top), far, reach, states)
     other = lax.ppermute(own, "ctx", [(i, i ^ 1) for i in range(ctx)])
-    fold = steps // 2
-    from_half = pl.BlockSpec(
-        (HEADS_PER_STEP, BLK, (levels - 1) * BLK), lambda i: (i % fold, 0, 0)
-    )
-    return pl.pallas_call(
-        finish_side,
-        grid=(steps,),
-        in_specs=[
-            SMEM, whole((1, BLK)), by_column((length, width)), by_column((length, width)),
-            by_column((length, width * (levels - 1))), by_head((BLK, BLK)), from_half, from_half,
-        ],
-        out_specs=by_column((length, width)),
-        out_shape=shape_of(z_in.shape, BF),
-        compiler_params=params,
-        name="finish_side",
-    )(core, norm_gain.reshape(1, BLK), z_in, base, scaled, near, own, other)
+    return finished(core, norm_gain.reshape(1, BLK), z_in, base, scaled, near, own, other)
 
 
 def solution(mesh):

time: 98.3 us -> 82.6 us (0.84)
  Pallas kernels: 72 us -> 59.9 us
  local copies, waits for them, and re-layouts: 10.7 us -> 7.3 us
    pallas_call x5, Pallas kernels: 45.6 us -> 33.6 us  [the longest x1 20.9 us: keys_of(): pl.pallas_call(key_side, grid=(heads // KEY_HEADS,), in_specs=[by_head(KE...]
    unnamed x11, local copies, waits for them, and re-layouts: 4.78 us -> 2.31 us
  transfers between devices with their start and end apart: 5 -> 5, of which waited for: 2 -> 2; matrix products, arithmetic and copies ran while one was open for 5% -> 6% of each run, Pallas kernels for 27% -> 32%
where the time goes in v2:
time: 82.6 us; the launch traced here: 81.9 us
  Pallas kernels  59.9 us (73%)
  starting transfers between devices  10.9 us (13%)
  local copies, waits for them, and re-layouts  7.3 us (9%)
  waiting for transfers between devices  3.38 us (4%)
    pallas_call x2, Pallas kernels, queries_of(): pl.pallas_call(functools.partial(query_side, first_step=first), grid=(ste...  26.3 us
    pallas_call x1, Pallas kernels, keys_of(): pl.pallas_call(key_side, grid=(heads // KEY_HEADS,), in_specs=[by_head(KE...  20.9 us
    pallas_call x1, Pallas kernels, finished(): pl.pallas_call(finish_side, grid=(2 * fold,), in_specs=[SMEM, whole(gain....  10 us
    ppermute x1, starting transfers between devices, per_device(): lax.ppermute(pair, 'ctx', [(i, i + 2 ** top) for i in range(ctx - 2 ** to...  4.07 us
    ppermute x1, starting transfers between devices, per_device(): near = lax.ppermute(pair, 'ctx', [(i, i ^ 1) for i in range(ctx)])  2.74 us
    ppermute x1, starting transfers between devices, per_device(): halo = lax.ppermute(edge, 'ctx', [(i, i + 1) for i in range(ctx - 1)])  2.4 us
    unnamed x11, local copies, waits for them, and re-layouts  2.31 us
    pallas_call x1, Pallas kernels, joined_far(): pl.pallas_call(join_far, in_specs=[SMEM, ANY, ANY] + [VMEM] * len(given),...  2.11 us
  transfers between devices with their start and end apart: 5, of which 2 were waited for; matrix products, arithmetic and copies ran while one was open for 6% of the time, Pallas kernels for 32%

profile of v2, /device:TPU:0, one launch (start us, length us, event | category | flops | bytes accessed | tf_op | source)
XLA Modules:
  0.0 81.9 jit_solution(2081807511379036533)
XLA Ops:
  0.0 0.8 slice_bitcast_fusion.2
  0.8 0.8 slice_bitcast_fusion
  1.6 2.4 %collective-permute-start = (bf16[3,4,2048]{2,1,0:T(4,128)(2,1)S(1)}, bf16[3,4,2048]{2,1,0:T(4,128)(2,1)S(1)}, u32[]{:S(2)}, u32[]{:S(2)}) collective-permute-start(bf16[3,4,2048]{2,1,0:T(4,128)(2,1)S(1)} %pad_maximum_fusion.1), channel_id=1, source_target_pairs={{0,1},{1,2},{2,3},{3,4},{4,5},{5,6},{6,7},{8,9},{9,10},{10,11},{11... | collective-permute-start | bytes 147464 | tf_op jit(solution)/shard_map/ppermute | solution.py:521
  4.0 0.9 %copy.39 = f32[512,16]{1,0:T(8,128)S(1)} copy(f32[512,16]{0,1:T(8,128)} %param.13) | data formatting | bytes 65536 | tf_op jit(solution)/shard_map/reshape | solution.py:523
  4.9 0.9 %copy.33 = f32[512,16]{1,0:T(8,128)S(1)} copy(f32[512,16]{0,1:T(8,128)} %param.14) | data formatting | bytes 65536 | tf_op args[5]
  5.8 0.3 reduce_window_sum.11
  6.1 0.7 pad.8.g_ref
  6.9 0.8 copy.34.rows_ref
  7.7 0.0 slice-start
  7.7 0.0 collective-permute-done.halo_ref
  7.7 0.0 copy-start.4
  7.7 0.6 copy-done.4
  8.3 20.9 %key_side.1 = (bf16[16,128,512]{2,1,0:T(8,128)(2,1)}, bf16[16,512,256]{2,1,0:T(8,128)(2,1)}, bf16[16,128,256]{2,1,0:T(8,128)(2,1)}, bf16[16,3,128,256]{3,2,1,0:T(8,128)(2,1)}) custom-call(f32[16,2,512]{2,1,0:T(2,128)} %copy.34.rows_ref, f32[512,128]{1,0:T(8,128)} %pad.8.g_ref, f32[3,4,2048]{2,1,0:T(4,128)} %taps_ref.5, bf16[3,4,2048]{2,1,0:T(4,128)(2,1)} %copy-done.4, ...), custom_call_target="tpu_custom_call" | custom-call | flops 10000000000 | bytes 20000000 | tf_op jit(solution)/shard_map/key_side/pallas_call | solution.py:394
  29.2 0.0 copy-start.2
  29.2 2.7 %collective-permute-start.1 = (bf16[16,128,256]{2,1,0:T(8,128)(2,1)}, bf16[16,128,256]{2,1,0:T(8,128)(2,1)S(1)}, u32[]{:S(2)}, u32[]{:S(2)}) collective-permute-start(bf16[16,128,256]{2,1,0:T(8,128)(2,1)} %get-tuple-element.24.pair_ref), channel_id=1, source_target_pairs={{0,1},{1,0},{2,3},{3,2},{4,5},{5,4},{6,7},{7,6},{8,9},{9,8},{10,11... | collective-permute-start | bytes 3145736 | tf_op jit(solution)/shard_map/ppermute | solution.py:531
  31.9 0.0 slice-done
  31.9 0.1 copy.35
  32.1 0.1 copy.36
  32.2 0.7 pad.9.weight_ref
  33.0 1.5 %collective-permute-done.1.far_ref.near_ref = bf16[16,128,256]{2,1,0:T(8,128)(2,1)S(1)} collective-permute-done((bf16[16,128,256]{2,1,0:T(8,128)(2,1)}, bf16[16,128,256]{2,1,0:T(8,128)(2,1)S(1)}, u32[]{:S(2)}, u32[]{:S(2)}) %collective-permute-start.1) | collective-permute-done | bytes 1048608 | tf_op jit(solution)/shard_map/ppermute | solution.py:531
  34.4 0.0 copy-start
  34.4 0.0 copy-done.2
  34.4 0.4 join_near.1.pair_ref
  34.8 1.6 %collective-permute-start.2 = (bf16[8,128,256]{2,1,0:T(8,128)(2,1)S(1)}, bf16[8,128,256]{2,1,0:T(8,128)(2,1)}, u32[]{:S(2)}, u32[]{:S(2)}) collective-permute-start(bf16[8,128,256]{2,1,0:T(8,128)(2,1)S(1)} %join_near.1.pair_ref), channel_id=1, source_target_pairs={{0,2},{1,3},{2,0},{3,1},{4,6},{5,7},{6,4},{7,5},{8,10},{9,11},{10,... | collective-permute-start | bytes 1572872 | tf_op jit(solution)/shard_map/ppermute | solution.py:542
  36.5 0.0 copy-done
  36.5 13.2 %query_side.2 = (bf16[512,4096]{1,0:T(8,128)(2,1)}, f32[512,2048]{1,0:T(8,128)}) custom-call(s32[1]{0:T(128)} %bitcast.core_ref.odd_ref, f32[16,2,512]{2,1,0:T(2,128)} %copy.34.rows_ref, f32[512,128]{1,0:T(8,128)} %pad.8.g_ref, f32[512,128]{1,0:T(8,128)} %pad.9.weight_ref, f32[3,4,2048]{2,1,0:T(4,128)} %taps_ref.5, bf16[3,4,2048]{2,1,0:T(4,128)(2,1)} %copy-done.4, ...), custom_call_target="tpu_custom_call" | custom-call | flops 10000000000 | bytes 20000000 | tf_op jit(solution)/shard_map/query_side/pallas_call | solution.py:427
  49.6 0.0 collective-permute-done.2.far_ref
  49.6 2.1 %join_far.1 = (bf16[8,128,128]{2,1,0:T(8,128)(2,1)}, bf16[8,128,128]{2,1,0:T(8,128)(2,1)S(1)}, bf16[8,128,128]{2,1,0:T(8,128)(2,1)S(1)}) custom-call(s32[1]{0:T(128)} %bitcast.2.upper_ref, bf16[8,128,256]{2,1,0:T(8,128)(2,1)S(1)} %join_near.1.pair_ref, bf16[8,128,256]{2,1,0:T(8,128)(2,1)} %collective-permute-done.2.far_ref), custom_call_target="tpu_custom_call" | custom-call | tf_op jit(solution)/shard_map/join_far/pallas_call | solution.py:488
  51.7 4.1 %collective-permute-start.3 = (bf16[8,128,128]{2,1,0:T(8,128)(2,1)}, bf16[8,128,128]{2,1,0:T(8,128)(2,1)S(1)}, u32[]{:S(2)}, u32[]{:S(2)}) collective-permute-start(bf16[8,128,128]{2,1,0:T(8,128)(2,1)} %get-tuple-element.32), channel_id=1, source_target_pairs={{0,4},{1,5},{2,6},{3,7},{8,12},{9,13},{10,14},{11,15},{16,20},{17,... | collective-permute-start | bytes 786440 | tf_op jit(solution)/shard_map/ppermute | solution.py:550
  55.8 13.1 %query_side.3 = (bf16[512,4096]{1,0:T(8,128)(2,1)}, f32[512,2048]{1,0:T(8,128)}) custom-call(s32[1]{0:T(128)} %bitcast.core_ref.odd_ref, f32[16,2,512]{2,1,0:T(2,128)} %copy.34.rows_ref, f32[512,128]{1,0:T(8,128)} %pad.8.g_ref, f32[512,128]{1,0:T(8,128)} %pad.9.weight_ref, f32[3,4,2048]{2,1,0:T(4,128)} %taps_ref.5, ...), custom_call_target="tpu_custom_call", output_to_operand_aliasing={{0}: (11, {}), {1}: (12, {})} | custom-call | flops 10000000000 | bytes 20000000 | tf_op jit(solution)/shard_map/query_side/pallas_call | solution.py:427
  69.0 0.0 collective-permute-done.3.far_ref
  69.0 0.1 join_top.1.own_ref
  69.1 0.0 copy-start.1
  69.1 0.1 collective-permute-start.4
  69.2 1.9 %collective-permute-done.4.far_ref = bf16[8,128,256]{2,1,0:T(8,128)(2,1)S(1)} collective-permute-done((bf16[8,128,256]{2,1,0:T(8,128)(2,1)S(1)}, bf16[8,128,256]{2,1,0:T(8,128)(2,1)S(1)}, u32[]{:S(2)}, u32[]{:S(2)}) %collective-permute-start.4) | collective-permute-done | bytes 524320 | tf_op jit(solution)/shard_map/ppermute | solution.py:554
  71.1 0.0 copy-start.3
  71.1 0.0 copy-done.1
  71.1 0.8 copy-done.3
  71.9 10.0 %finish_side.1 = bf16[512,2048]{1,0:T(8,128)(2,1)} custom-call(s32[1]{0:T(128)} %bitcast.core_ref.odd_ref, f32[1,128]{1,0:T(1,128)} %bitcast.25, bf16[512,2048]{1,0:T(8,128)(2,1)} %z_ref.1, f32[512,2048]{1,0:T(8,128)} %get-tuple-element.38.base_ref, bf16[512,4096]{1,0:T(8,128)(2,1)} %get-tuple-element.39.scaled_ref, bf16[16,128,256]{2,1,0:T(8,128)(2,1)} %copy-done, ...), custom_call_target="tpu_custom_call" | custom-call | tf_op jit(solution)/shard_map/finish_side/pallas_call | solution.py:454
  (3 shorter events, 0.1 us)
Async XLA Ops:
  1.6 6.0 %collective-permute-start = (bf16[3,4,2048]{2,1,0:T(4,128)(2,1)S(1)}, bf16[3,4,2048]{2,1,0:T(4,128)(2,1)S(1)}, u32[]{:S(2)}, u32[]{:S(2)}) collective-permute-start(bf16[3,4,2048]{2,1,0:T(4,128)(2,1)S(1)} %pad_maximum_fusion.1), channel_id=1, source_target_pairs={{0,1},{1,2},{2,3},{3,4},{4,5},{5,6},{6,7},{8,9},{9,10},{10,11},{11... | collective-permute-start | bytes 147464 | tf_op jit(solution)/shard_map/ppermute | solution.py:521
  7.7 24.3 %slice-start = ((f32[512,16,6]{0,1,2:T(8,128)}), f32[512,16,4]{0,1,2:T(8,128)S(1)}, s32[]{:S(2)}) async-start(f32[512,16,6]{0,1,2:T(8,128)} %param.15), calls=%async_computation | async-start | bytes 262144 | tf_op jit(solution)/shard_map/slice | solution.py:526
  7.7 0.6 copy-start.4
  29.2 5.2 %copy-start.2 = (bf16[16,128,256]{2,1,0:T(8,128)(2,1)S(1)}, bf16[16,128,256]{2,1,0:T(8,128)(2,1)}, u32[]{:S(2)}) copy-start(bf16[16,128,256]{2,1,0:T(8,128)(2,1)} %get-tuple-element.24.pair_ref) | copy-start | bytes 3145732
  29.2 5.2 %collective-permute-start.1 = (bf16[16,128,256]{2,1,0:T(8,128)(2,1)}, bf16[16,128,256]{2,1,0:T(8,128)(2,1)S(1)}, u32[]{:S(2)}, u32[]{:S(2)}) collective-permute-start(bf16[16,128,256]{2,1,0:T(8,128)(2,1)} %get-tuple-element.24.pair_ref), channel_id=1, source_target_pairs={{0,1},{1,0},{2,3},{3,2},{4,5},{5,4},{6,7},{7,6},{8,9},{9,8},{10,11... | collective-permute-start | bytes 3145736 | tf_op jit(solution)/shard_map/ppermute | solution.py:531
  34.4 2.0 %copy-start = (bf16[16,128,256]{2,1,0:T(8,128)(2,1)}, bf16[16,128,256]{2,1,0:T(8,128)(2,1)S(1)}, u32[]{:S(2)}) copy-start(bf16[16,128,256]{2,1,0:T(8,128)(2,1)S(1)} %collective-permute-done.1.far_ref.near_ref) | copy-start | bytes 3145732
  34.8 14.8 %collective-permute-start.2 = (bf16[8,128,256]{2,1,0:T(8,128)(2,1)S(1)}, bf16[8,128,256]{2,1,0:T(8,128)(2,1)}, u32[]{:S(2)}, u32[]{:S(2)}) collective-permute-start(bf16[8,128,256]{2,1,0:T(8,128)(2,1)S(1)} %join_near.1.pair_ref), channel_id=1, source_target_pairs={{0,2},{1,3},{2,0},{3,1},{4,6},{5,7},{6,4},{7,5},{8,10},{9,11},{10,... | collective-permute-start | bytes 1572872 | tf_op jit(solution)/shard_map/ppermute | solution.py:542
  51.7 17.2 %collective-permute-start.3 = (bf16[8,128,128]{2,1,0:T(8,128)(2,1)}, bf16[8,128,128]{2,1,0:T(8,128)(2,1)S(1)}, u32[]{:S(2)}, u32[]{:S(2)}) collective-permute-start(bf16[8,128,128]{2,1,0:T(8,128)(2,1)} %get-tuple-element.32), channel_id=1, source_target_pairs={{0,4},{1,5},{2,6},{3,7},{8,12},{9,13},{10,14},{11,15},{16,20},{17,... | collective-permute-start | bytes 786440 | tf_op jit(solution)/shard_map/ppermute | solution.py:550
  69.1 2.0 %copy-start.1 = (bf16[8,128,256]{2,1,0:T(8,128)(2,1)}, bf16[8,128,256]{2,1,0:T(8,128)(2,1)S(1)}, u32[]{:S(2)}) copy-start(bf16[8,128,256]{2,1,0:T(8,128)(2,1)S(1)} %join_top.1.own_ref) | copy-start | bytes 1572868
  69.1 2.0 %collective-permute-start.4 = (bf16[8,128,256]{2,1,0:T(8,128)(2,1)S(1)}, bf16[8,128,256]{2,1,0:T(8,128)(2,1)S(1)}, u32[]{:S(2)}, u32[]{:S(2)}) collective-permute-start(bf16[8,128,256]{2,1,0:T(8,128)(2,1)S(1)} %join_top.1.own_ref), channel_id=1, source_target_pairs={{0,1},{1,0},{2,3},{3,2},{4,5},{5,4},{6,7},{7,6},{8,9},{9,8},{10,11... | collective-permute-start | bytes 1572872 | tf_op jit(solution)/shard_map/ppermute | solution.py:554
  71.1 0.8 copy-start.3

commit v3 on v2

--- a/solution.py
+++ b/solution.py
@@ -360,6 +360,14 @@
     return jax.ShapeDtypeStruct(shape, dtype)
 
 
+def in_vmem(*arrays):
+    return [pltpu.with_memory_space_constraint(x, pltpu.VMEM) for x in arrays]
+
+
+def in_hbm(*arrays):
+    return [pltpu.with_memory_space_constraint(x, pltpu.HBM) for x in arrays]
+
+
 def whole(shape):
     return pl.BlockSpec(shape, lambda i: (0,) * len(shape))
 
@@ -378,7 +386,7 @@
 SMEM = pl.BlockSpec(memory_space=pltpu.SMEM)
 VMEM = pl.BlockSpec(memory_space=pltpu.VMEM)
 COST = pl.CostEstimate(flops=10**10, bytes_accessed=2 * 10**7, transcendentals=10**7)
-PARAMS = pltpu.CompilerParams(dimension_semantics=("arbitrary",), vmem_limit_bytes=62 << 20)
+PARAMS = pltpu.CompilerParams(dimension_semantics=("arbitrary",), vmem_limit_bytes=22 << 20)
 
 SMALL = pltpu.CompilerParams(vmem_limit_bytes=8 << 20)
 
@@ -403,8 +411,9 @@
             by_head(KEY_HEADS, (BLK, 2 * BLK)), by_head(KEY_HEADS, (blocks - 1, BLK, 2 * BLK)),
         ],
         out_shape=[
-            shape_of((heads, BLK, length), BF), shape_of((heads, length, 2 * BLK), BF),
-            shape_of((heads, BLK, 2 * BLK), BF), shape_of((heads, blocks - 1, BLK, 2 * BLK), BF),
+            pltpu.VMEM((heads, BLK, length), BF), pltpu.VMEM((heads, length, 2 * BLK), BF),
+            pltpu.VMEM((heads, BLK, 2 * BLK), BF),
+            pltpu.VMEM((heads, blocks - 1, BLK, 2 * BLK), BF),
         ],
         scratch_shapes=[
             pltpu.VMEM((2 * KEY_HEADS, length + 8, BLK), F32),
@@ -413,7 +422,7 @@
         compiler_params=PARAMS,
         cost_estimate=COST,
         name="key_side",
-    )(rows, g_pad, conv_weight, halo, k_in, v_in)
+    )(rows, g_pad, conv_weight, halo, *in_hbm(k_in, v_in))
 
 
 def queries_of(second, levels, core, rows, g_pad, weights, taps, halo, q_in, kt, uw, prior, near, previous):
@@ -437,13 +446,18 @@
         ]
         + [ANY] * count,
         out_specs=[by_column((length, scaled_width), first), by_column((length, width), first)],
-        out_shape=[shape_of((length, heads * (levels - 1) * BLK), BF), shape_of(q_in.shape, F32)],
+        out_shape=[
+            pltpu.VMEM((length, heads * (levels - 1) * BLK), BF), pltpu.VMEM(q_in.shape, F32)
+        ],
         scratch_shapes=[pltpu.VMEM((QUERY_HEADS, length + 8, BLK), F32)],
         input_output_aliases={11 + i: i for i in range(count)},
         compiler_params=PARAMS,
         cost_estimate=COST,
         name="query_side",
-    )(core, rows, g_pad, weights, taps, halo, q_in, kt, uw, prior, near, *previous)
+    )(
+        core, rows, g_pad, weights, taps, halo, *in_hbm(q_in), *in_vmem(kt, uw, prior, near),
+        *in_vmem(*previous),
+    )
 
 
 def finished(core, gain, z_in, base, scaled, near, own, other):
@@ -464,7 +478,7 @@
         scratch_shapes=[pltpu.VMEM(other.shape, BF), pltpu.SemaphoreType.DMA((1,))],
         compiler_params=PARAMS,
         name="finish_side",
-    )(core, gain, z_in, base, scaled, near, own, other)
+    )(core, gain, *in_hbm(z_in), *in_vmem(base, scaled, near, own, other))
 
 
 def joined_near(core, pair, near):
@@ -525,7 +539,11 @@
     rows = jnp.stack([g.T, beta.T], axis=1)
     weights = level_weight[:, :, : levels + 1].reshape(length, heads * (levels + 1))
     weights = jnp.pad(weights, ((0, 0), (0, -weights.shape[1] % BLK)))
-    core = bit(position, 0)
+    bits = [bit(position, level) for level in range(levels)]
+    halo, rows, g_pad, weights, *bits = lax.optimization_barrier(
+        (halo, rows, g_pad, weights, *bits)
+    )
+    core = bits[0]
 
     kt, uw, pair, prior = keys_of(rows, g_pad, conv_weight, halo, k_in, v_in)
     near = lax.ppermute(pair, "ctx", [(i, i ^ 1) for i in range(ctx)])
@@ -543,14 +561,14 @@
         if level == 1:
             parts = queries(False, q_in, ())
             far, *parts = lax.optimization_barrier((far, *parts))
-        pair, state, reach = joined_far(bit(position, level), pair, far, reach, level == levels - 2)
+        pair, state, reach = joined_far(bits[level], pair, far, reach, level == levels - 2)
         states.append(state)
     top = levels - 1
     pair, later_q = lax.optimization_barrier((pair, q_in))
     far = lax.ppermute(pair, "ctx", [(i, i + 2**top) for i in range(ctx - 2**top)])
     parts = queries(True, later_q, parts)
     far, scaled, base = lax.optimization_barrier((far, *parts))
-    own = joined_top(bit(position, top), far, reach, states)
+    own = joined_top(bits[top], far, reach, states)
     other = lax.ppermute(own, "ctx", [(i, i ^ 1) for i in range(ctx)])
     return finished(core, norm_gain.reshape(1, BLK), z_in, base, scaled, near, own, other)
 

time: 82.6 us -> 73.3 us (0.89)
  Pallas kernels: 59.9 us -> 51.1 us
  local copies, waits for them, and re-layouts: 7.3 us -> 3.86 us
  waiting for transfers between devices: 3.38 us -> 5.25 us
    pallas_call x2, Pallas kernels: 26.3 us -> 23.1 us  [queries_of(): pl.pallas_call(functools.partial(query_side, first_step=first), grid=(ste...]
    pallas_call x1, Pallas kernels: 10 us -> 7.29 us  [finished(): pl.pallas_call(finish_side, grid=(2 * fold,), in_specs=[SMEM, whole(gain....]
    unnamed x11 -> x4, local copies, waits for them, and re-layouts: 2.31 us -> 0.01 us
    pallas_call x1, Pallas kernels: 2.11 us -> 0.39 us  [joined_far(): pl.pallas_call(join_far, in_specs=[SMEM, ANY, ANY] + [VMEM] * len(given),...]
    pallas_call x1, Pallas kernels: 20.9 us -> 19.7 us  [keys_of(): pl.pallas_call(key_side, grid=(heads // KEY_HEADS,), in_specs=[by_head(KE...]
    ppermute x1, waiting for transfers between devices: 0.01 us -> 1.06 us  [per_device(): far = lax.ppermute(pair, 'ctx', [(i, i ^ 2 ** level) for i in range(ctx)])]
    slice x3 -> x2, local copies, waits for them, and re-layouts: 0.09 us -> 1 us  [per_device(): level_weight[:, :, :levels + 1].reshape(length, heads * (levels + 1))]
  transfers between devices with their start and end apart: 5 -> 5, of which waited for: 2 -> 3; matrix products, arithmetic and copies ran while one was open for 6% -> 4% of each run, Pallas kernels for 32% -> 32%
where the time goes in v3:
time: 73.3 us; the launch traced here: 72.8 us
  Pallas kernels  51.1 us (70%)
  starting transfers between devices  11.4 us (16%)
  waiting for transfers between devices  5.25 us (7%)
  local copies, waits for them, and re-layouts  3.86 us (5%)
  other arithmetic  1.08 us (1%)
    pallas_call x2, Pallas kernels, queries_of(): pl.pallas_call(functools.partial(query_side, first_step=first), grid=(ste...  23.1 us
    pallas_call x1, Pallas kernels, keys_of(): pl.pallas_call(key_side, grid=(heads // KEY_HEADS,), in_specs=[by_head(KE...  19.7 us
    pallas_call x1, Pallas kernels, finished(): pl.pallas_call(finish_side, grid=(2 * fold,), in_specs=[SMEM, whole(gain....  7.29 us
    ppermute x1, starting transfers between devices, per_device(): lax.ppermute(pair, 'ctx', [(i, i + 2 ** top) for i in range(ctx - 2 ** to...  4.5 us
    ppermute x1, starting transfers between devices, per_device(): near = lax.ppermute(pair, 'ctx', [(i, i ^ 1) for i in range(ctx)])  2.75 us
    ppermute x1, starting transfers between devices, per_device(): halo = lax.ppermute(edge, 'ctx', [(i, i + 1) for i in range(ctx - 1)])  2.4 us
    ppermute x1, waiting for transfers between devices, per_device(): near = lax.ppermute(pair, 'ctx', [(i, i ^ 1) for i in range(ctx)])  2.29 us
    ppermute x1, waiting for transfers between devices, per_device(): other = lax.ppermute(own, 'ctx', [(i, i ^ 1) for i in range(ctx)])  1.9 us
  transfers between devices with their start and end apart: 5, of which 3 were waited for; matrix products, arithmetic and copies ran while one was open for 4% of the time, Pallas kernels for 32%

profile of v3, /device:TPU:0, one launch (start us, length us, event | category | flops | bytes accessed | tf_op | source)
XLA Modules:
  0.0 72.8 jit_solution(12313064394147081698)
XLA Ops:
  0.0 0.0 copy-start.1
  0.0 0.8 %slice_bitcast_fusion.2 = bf16[1,4,2048]{2,1,0:T(4,128)(2,1)S(1)} fusion(bf16[512,2048]{1,0:T(8,128)(2,1)} %q_ref.2), kind=kLoop, calls=%fused_computation.4 | loop fusion | bytes 32768 | tf_op jit(solution)/shard_map/stack | solution.py:534
  0.8 0.8 %slice_bitcast_fusion = (bf16[1,4,2048]{2,1,0:T(4,128)(2,1)S(1)}, bf16[1,4,2048]{2,1,0:T(4,128)(2,1)S(1)}) fusion(bf16[512,2048]{1,0:T(8,128)(2,1)} %v_ref.1, bf16[512,2048]{1,0:T(8,128)(2,1)} %k_ref.1), kind=kLoop, calls=%fused_computation.2 | loop fusion | bytes 65536 | tf_op jit(solution)/shard_map/stack | solution.py:534
  1.7 2.4 %collective-permute-start = (bf16[3,4,2048]{2,1,0:T(4,128)(2,1)S(1)}, bf16[3,4,2048]{2,1,0:T(4,128)(2,1)S(1)}, u32[]{:S(2)}, u32[]{:S(2)}) collective-permute-start(bf16[3,4,2048]{2,1,0:T(4,128)(2,1)S(1)} %pad_maximum_fusion.1), channel_id=1, source_target_pairs={{0,1},{1,2},{2,3},{3,4},{4,5},{5,6},{6,7},{8,9},{9,10},{10,11},{11... | collective-permute-start | bytes 147464 | tf_op jit(solution)/shard_map/ppermute | solution.py:535
  4.1 0.9 %copy.32 = f32[512,16]{1,0:T(8,128)S(1)} copy(f32[512,16]{0,1:T(8,128)} %param.13) | data formatting | bytes 65536 | tf_op jit(solution)/shard_map/reshape | solution.py:537
  5.0 0.3 reduce_window_sum.11
  5.2 0.1 copy.26
  5.3 0.8 %pad_maximum_fusion = f32[16,2,512]{2,0,1:T(8,128)S(1)} fusion(f32[16,1,512]{2,0,1:T(8,128)} %bitcast.25, f32[16,1,512]{2,0,1:T(8,128)S(1)} %copy.26), kind=kLoop, calls=%fused_computation | loop fusion | flops 16384 | bytes 131072 | tf_op jit(solution)/shard_map/stack | solution.py:539
  6.1 0.9 %slice.15 = f32[512,16,4]{0,1,2:T(8,128)S(1)} slice(f32[512,16,6]{0,1,2:T(8,128)} %param.15), slice={[0:512], [0:16], [0:4]} | slice | bytes 262144 | tf_op jit(solution)/shard_map/slice | solution.py:540
  7.0 0.1 copy.27
  7.2 0.1 copy.28
  7.4 0.0 collective-permute-done.halo_ref
  7.4 0.1 copy.29.rows_ref
  7.4 0.0 copy-done.1
  7.5 19.7 %key_side.1 = (bf16[16,128,512]{2,1,0:T(8,128)(2,1)S(1)}, bf16[16,512,256]{2,1,0:T(8,128)(2,1)S(1)}, bf16[16,128,256]{2,1,0:T(8,128)(2,1)S(1)}, bf16[16,3,128,256]{3,2,1,0:T(8,128)(2,1)S(1)}) custom-call(f32[16,2,512]{2,1,0:T(2,128)S(1)} %copy.29.rows_ref, f32[512,128]{1,0:T(8,128)S(1)} %pad.8.g_ref, f32[3,4,2048]{2,1,0:T(4,128)S(1)} %copy-done.1, ...), custom_call_target="tpu_custom_call" | custom-call | flops 10000000000 | bytes 20000000 | tf_op jit(solution)/shard_map/key_side/pallas_call | solution.py:402
  27.2 2.7 %collective-permute-start.1 = (bf16[16,128,256]{2,1,0:T(8,128)(2,1)S(1)}, bf16[16,128,256]{2,1,0:T(8,128)(2,1)S(1)}, u32[]{:S(2)}, u32[]{:S(2)}) collective-permute-start(bf16[16,128,256]{2,1,0:T(8,128)(2,1)S(1)} %get-tuple-element.36.pair_ref), channel_id=1, source_target_pairs={{0,1},{1,0},{2,3},{3,2},{4,5},{5,4},{6,7},{7,6},{8,9},{9,8},{10,11... | collective-permute-start | bytes 3145736 | tf_op jit(solution)/shard_map/ppermute | solution.py:549
  30.0 2.3 %collective-permute-done.1.far_ref.near_ref = bf16[16,128,256]{2,1,0:T(8,128)(2,1)S(1)} collective-permute-done((bf16[16,128,256]{2,1,0:T(8,128)(2,1)S(1)}, bf16[16,128,256]{2,1,0:T(8,128)(2,1)S(1)}, u32[]{:S(2)}, u32[]{:S(2)}) %collective-permute-start.1) | collective-permute-done | bytes 1048608 | tf_op jit(solution)/shard_map/ppermute | solution.py:549
  32.2 0.4 join_near.1.pair_ref
  32.6 1.6 %collective-permute-start.2 = (bf16[8,128,256]{2,1,0:T(8,128)(2,1)S(1)}, bf16[8,128,256]{2,1,0:T(8,128)(2,1)S(1)}, u32[]{:S(2)}, u32[]{:S(2)}) collective-permute-start(bf16[8,128,256]{2,1,0:T(8,128)(2,1)S(1)} %join_near.1.pair_ref), channel_id=1, source_target_pairs={{0,2},{1,3},{2,0},{3,1},{4,6},{5,7},{6,4},{7,5},{8,10},{9,11},{10,... | collective-permute-start | bytes 1572872 | tf_op jit(solution)/shard_map/ppermute | solution.py:560
  34.3 11.6 %query_side.2 = (bf16[512,4096]{1,0:T(8,128)(2,1)S(1)}, f32[512,2048]{1,0:T(8,128)S(1)}) custom-call(s32[1]{0:T(128)} %bitcast.9.core_ref.odd_ref, f32[16,2,512]{2,1,0:T(2,128)S(1)} %copy.29.rows_ref, f32[512,128]{1,0:T(8,128)S(1)} %pad.8.g_ref, f32[512,128]{1,0:T(8,128)S(1)} %pad.9.weight_ref, f32[3,4,2048]{2,1,0:T(4,128)S(1)} %copy-done.1, ...), custom_call_target="tpu_custom_call" | custom-call | flops 10000000000 | bytes 20000000 | tf_op jit(solution)/shard_map/query_side/pallas_call | solution.py:436
  45.8 1.1 %collective-permute-done.2.far_ref = bf16[8,128,256]{2,1,0:T(8,128)(2,1)S(1)} collective-permute-done((bf16[8,128,256]{2,1,0:T(8,128)(2,1)S(1)}, bf16[8,128,256]{2,1,0:T(8,128)(2,1)S(1)}, u32[]{:S(2)}, u32[]{:S(2)}) %collective-permute-start.2) | collective-permute-done | bytes 524320 | tf_op jit(solution)/shard_map/ppermute | solution.py:560
  46.9 0.4 join_far.1
  47.3 0.0 copy-start
  47.3 4.5 %collective-permute-start.3 = (bf16[8,128,128]{2,1,0:T(8,128)(2,1)S(1)}, bf16[8,128,128]{2,1,0:T(8,128)(2,1)S(1)}, u32[]{:S(2)}, u32[]{:S(2)}) collective-permute-start(bf16[8,128,128]{2,1,0:T(8,128)(2,1)S(1)} %get-tuple-element.45), channel_id=1, source_target_pairs={{0,4},{1,5},{2,6},{3,7},{8,12},{9,13},{10,14},{11,15},{16,20},{17,... | collective-permute-start | bytes 786440 | tf_op jit(solution)/shard_map/ppermute | solution.py:568
  51.8 11.6 %query_side.3 = (bf16[512,4096]{1,0:T(8,128)(2,1)S(1)}, f32[512,2048]{1,0:T(8,128)S(1)}) custom-call(s32[1]{0:T(128)} %bitcast.9.core_ref.odd_ref, f32[16,2,512]{2,1,0:T(2,128)S(1)} %copy.29.rows_ref, f32[512,128]{1,0:T(8,128)S(1)} %pad.8.g_ref, f32[512,128]{1,0:T(8,128)S(1)} %pad.9.weight_ref, ...), custom_call_target="tpu_custom_call", output_to_operand_aliasing={{0}: (11, {}), {1}: (12, {})} | custom-call | flops 10000000000 | bytes 20000000 | tf_op jit(solution)/shard_map/query_side/pallas_call | solution.py:436
  63.4 0.0 collective-permute-done.3.far_ref
  63.4 0.1 join_top.1.own_ref
  63.6 0.1 collective-permute-start.4
  63.6 1.9 %collective-permute-done.4.far_ref = bf16[8,128,256]{2,1,0:T(8,128)(2,1)S(1)} collective-permute-done((bf16[8,128,256]{2,1,0:T(8,128)(2,1)S(1)}, bf16[8,128,256]{2,1,0:T(8,128)(2,1)S(1)}, u32[]{:S(2)}, u32[]{:S(2)}) %collective-permute-start.4) | collective-permute-done | bytes 524320 | tf_op jit(solution)/shard_map/ppermute | solution.py:572
  65.5 0.0 copy-done
  65.5 7.3 %finish_side.1 = bf16[512,2048]{1,0:T(8,128)(2,1)} custom-call(s32[1]{0:T(128)} %bitcast.9.core_ref.odd_ref, f32[1,128]{1,0:T(1,128)S(1)} %bitcast.21, bf16[512,2048]{1,0:T(8,128)(2,1)} %z_ref.1, f32[512,2048]{1,0:T(8,128)S(1)} %get-tuple-element.51.base_ref, bf16[512,4096]{1,0:T(8,128)(2,1)S(1)} %get-tuple-element.52.scaled_ref, ...), custom_call_target="tpu_custom_call" | custom-call | tf_op jit(solution)/shard_map/finish_side/pallas_call | solution.py:468
  (4 shorter events, 0.1 us)
Async XLA Ops:
  0.0 7.4 %copy-start.1 = (f32[3,4,2048]{2,1,0:T(4,128)S(1)}, f32[3,4,2048]{2,1,0:T(4,128)}, u32[]{:S(2)}) copy-start(f32[3,4,2048]{2,1,0:T(4,128)} %taps_ref.5) | copy-start | bytes 294916
  1.7 5.7 %collective-permute-start = (bf16[3,4,2048]{2,1,0:T(4,128)(2,1)S(1)}, bf16[3,4,2048]{2,1,0:T(4,128)(2,1)S(1)}, u32[]{:S(2)}, u32[]{:S(2)}) collective-permute-start(bf16[3,4,2048]{2,1,0:T(4,128)(2,1)S(1)} %pad_maximum_fusion.1), channel_id=1, source_target_pairs={{0,1},{1,2},{2,3},{3,4},{4,5},{5,6},{6,7},{8,9},{9,10},{10,11},{11... | collective-permute-start | bytes 147464 | tf_op jit(solution)/shard_map/ppermute | solution.py:535
  27.2 5.0 %collective-permute-start.1 = (bf16[16,128,256]{2,1,0:T(8,128)(2,1)S(1)}, bf16[16,128,256]{2,1,0:T(8,128)(2,1)S(1)}, u32[]{:S(2)}, u32[]{:S(2)}) collective-permute-start(bf16[16,128,256]{2,1,0:T(8,128)(2,1)S(1)} %get-tuple-element.36.pair_ref), channel_id=1, source_target_pairs={{0,1},{1,0},{2,3},{3,2},{4,5},{5,4},{6,7},{7,6},{8,9},{9,8},{10,11... | collective-permute-start | bytes 3145736 | tf_op jit(solution)/shard_map/ppermute | solution.py:549
  32.6 14.3 %collective-permute-start.2 = (bf16[8,128,256]{2,1,0:T(8,128)(2,1)S(1)}, bf16[8,128,256]{2,1,0:T(8,128)(2,1)S(1)}, u32[]{:S(2)}, u32[]{:S(2)}) collective-permute-start(bf16[8,128,256]{2,1,0:T(8,128)(2,1)S(1)} %join_near.1.pair_ref), channel_id=1, source_target_pairs={{0,2},{1,3},{2,0},{3,1},{4,6},{5,7},{6,4},{7,5},{8,10},{9,11},{10,... | collective-permute-start | bytes 1572872 | tf_op jit(solution)/shard_map/ppermute | solution.py:560
  47.3 18.2 %copy-start = (f32[128]{0:T(128)S(1)}, f32[128]{0:T(128)}, u32[]{:S(2)}) copy-start(f32[128]{0:T(128)} %param.17) | copy-start | bytes 1540
  47.3 16.1 %collective-permute-start.3 = (bf16[8,128,128]{2,1,0:T(8,128)(2,1)S(1)}, bf16[8,128,128]{2,1,0:T(8,128)(2,1)S(1)}, u32[]{:S(2)}, u32[]{:S(2)}) collective-permute-start(bf16[8,128,128]{2,1,0:T(8,128)(2,1)S(1)} %get-tuple-element.45), channel_id=1, source_target_pairs={{0,4},{1,5},{2,6},{3,7},{8,12},{9,13},{10,14},{11,15},{16,20},{17,... | collective-permute-start | bytes 786440 | tf_op jit(solution)/shard_map/ppermute | solution.py:568
  63.6 2.0 %collective-permute-start.4 = (bf16[8,128,256]{2,1,0:T(8,128)(2,1)S(1)}, bf16[8,128,256]{2,1,0:T(8,128)(2,1)S(1)}, u32[]{:S(2)}, u32[]{:S(2)}) collective-permute-start(bf16[8,128,256]{2,1,0:T(8,128)(2,1)S(1)} %join_top.1.own_ref), channel_id=1, source_target_pairs={{0,1},{1,0},{2,3},{3,2},{4,5},{5,4},{6,7},{7,6},{8,9},{9,8},{10,11... | collective-permute-start | bytes 1572872 | tf_op jit(solution)/shard_map/ppermute | solution.py:572

commit v4 on v3

--- a/solution.py
+++ b/solution.py
@@ -13,6 +13,7 @@
 QUERY_HEADS = 2
 FINISH_HEADS = 4
 EPS = 1e-06
+LOG2_E = 1.4426950408889634
 BF = jnp.bfloat16
 F32 = jnp.float32
 
@@ -52,7 +53,7 @@
 def decay_matrix(g_col, g_row, beta_row):
     size = g_col.shape[0]
     causal = iota2((size, BLK), 1) <= iota2((size, BLK), 0)
-    return jnp.exp(jnp.where(causal, g_col - g_row, -1e30)) * beta_row
+    return jnp.exp2(jnp.where(causal, g_col - g_row, -1e30)) * beta_row
 
 
 def make_masks(mask_ref):
@@ -83,17 +84,17 @@
     return out
 
 
-def inverses(lowers, mask_ref):
-    count = len(lowers)
-    every = range(count)
+def inverses(lowers, mask_ref, results):
+    every = range(len(lowers))
     row, col = iota2((SUB, BLK), 0), iota2((SUB, BLK), 1) % SUB
     eye = jnp.where(row == col, 1.0, 0.0).astype(F32)
     strict = col < row
     same = mask_ref[0]
     times = BLK // SUB
     powers = [jnp.where(strict, -picked(lower, SUB, None), 0.0) for lower in lowers]
-    results = [eye + power for power in powers]
+    results[:] = [eye + power for power in powers]
     powers = [dot(p.astype(BF), tiled(p, times, same)) for p in powers]
+    yield
     reach = 2
     while reach < SUB // 2:
         both = [
@@ -103,30 +104,46 @@
             )
             for i in every
         ]
-        powers = [b[:SUB] for b in both]
-        results = [results[i] + both[i][SUB:] for i in every]
+        yield
+        powers = [x[:SUB] for x in both]
+        results[:] = [results[i] + both[i][SUB:] for i in every]
         reach *= 2
-    results = [
+    results[:] = [
         results[i] + dot(results[i].astype(BF), tiled(powers[i], times, same)) for i in every
     ]
+    yield
     size, index = SUB, 0
     while size < BLK:
         times = BLK // size
         low = iota2((size, BLK), 1) // size % 2 == 0
         cross = [picked(lower, size, size).astype(BF) for lower in lowers]
         moved = [dot(cross[i], tiled(results[i], times, mask_ref[index])) for i in every]
+        yield
         turned = [
             dot(results[i].astype(BF), tiled(moved[i], times, mask_ref[index + 1]))
             for i in every
         ]
-        results = [
+        yield
+        results[:] = [
             jnp.concatenate(
                 [jnp.where(low, results[i], 0.0), jnp.where(low, -turned[i], results[i])], axis=0
             )
             for i in every
         ]
         size, index = size * 2, index + 2
-    return results
+
+
+def chained(first, second):
+    yield from first
+    yield from second
+
+
+def together(first, second):
+    live = [first, second]
+    while live:
+        for stages in list(live):
+            if next(stages, live) is live:
+                live.remove(stages)
 
 
 def key_side(
@@ -141,65 +158,101 @@
 
     length = k_ref.shape[0]
     blocks = length // BLK
+    base = KEY_HEADS * step
     turned_g = pltpu.roll(g_ref[...], BLK - KEY_HEADS * step, 1)
-    lowers, rights, tails, lasts = [], [], [], []
-    for head in range(KEY_HEADS):
-        lanes = slice(head * BLK, (head + 1) * BLK)
-        fill_padded(pad_ref, 2 * head, k_ref, halo_ref[1, :, lanes], lanes)
-        fill_padded(pad_ref, 2 * head + 1, v_ref, halo_ref[2, :, lanes], lanes)
-        for block in range(blocks):
-            start = block * BLK
-            tokens = slice(start, start + BLK)
-            keys = unit(conv_rows(pad_ref, 2 * head, taps_ref[1, :, lanes], start, BLK)).astype(BF)
-            values = conv_rows(pad_ref, 2 * head + 1, taps_ref[2, :, lanes], start, BLK).astype(BF)
-            keys_f = keys.astype(F32)
-            turned = keys_f.T
-            turned_b = turned.astype(BF)
-            kt_ref[head, :, tokens] = turned_b
-            g_col = jnp.broadcast_to(turned_g[tokens, head : head + 1], (BLK, BLK))
-            g_row = rows_ref[head, 0:1, tokens]
-            beta_row = rows_ref[head, 1:2, tokens]
-            g_last = g_row[:, BLK - 1 : BLK]
-            lowers.append(decay_matrix(g_col, g_row, beta_row) * dot(keys, turned_b))
-            rights.append(
-                jnp.concatenate([values, (jnp.exp(g_col) * keys_f).astype(BF)], axis=1)
+    eye = jnp.where(iota2((BLK, BLK), 0) == iota2((BLK, BLK), 1), 1.0, 0.0).astype(F32)
+
+    def front(heads, lowers, others):
+        for head in heads:
+            lanes = slice(head * BLK, (head + 1) * BLK)
+            fill_padded(pad_ref, 2 * head, k_ref, halo_ref[1, :, lanes], lanes)
+            fill_padded(pad_ref, 2 * head + 1, v_ref, halo_ref[2, :, lanes], lanes)
+            for block in range(blocks):
+                start = block * BLK
+                tokens = slice(start, start + BLK)
+                keys = unit(conv_rows(pad_ref, 2 * head, taps_ref[1, :, lanes], start, BLK))
+                keys = keys.astype(BF)
+                values = conv_rows(pad_ref, 2 * head + 1, taps_ref[2, :, lanes], start, BLK)
+                keys_f = keys.astype(F32)
+                turned = keys_f.T
+                turned_b = turned.astype(BF)
+                kt_ref[base + head, :, tokens] = turned_b
+                g_col = jnp.broadcast_to(turned_g[tokens, head : head + 1], (BLK, BLK))
+                g_row = rows_ref[head, 0:1, tokens]
+                beta_row = rows_ref[head, 1:2, tokens]
+                g_last = g_row[:, BLK - 1 : BLK]
+                lowers.append(decay_matrix(g_col, g_row, beta_row) * dot(keys, turned_b))
+                right = jnp.concatenate(
+                    [values.astype(BF), (jnp.exp2(g_col) * keys_f).astype(BF)], axis=1
+                )
+                tail = (turned * (jnp.exp2(g_last - g_row) * beta_row)).astype(BF)
+                others.append((right, tail, jnp.exp2(g_last)))
+                yield
+
+    def back(heads, solved, others):
+        maps = []
+        for place, head in enumerate(heads):
+            for block in range(blocks):
+                i = place * blocks + block
+                fresh = dot(solved[i].astype(BF), others[i][0]).astype(BF)
+                uw_ref[base + head, block * BLK : (block + 1) * BLK, :] = fresh
+                maps.append(fresh)
+            yield
+        for place, head in enumerate(heads):
+            for block in range(blocks):
+                i = place * blocks + block
+                maps[i] = dot(others[i][1], maps[i])
+            yield
+        states = []
+        for place, head in enumerate(heads):
+            i = place * blocks
+            states.append(
+                jnp.concatenate(
+                    [others[i][2] * eye - maps[i][:, BLK:], maps[i][:, :BLK]], axis=1
+                )
             )
-            tails.append((turned * (jnp.exp(g_last - g_row) * beta_row)).astype(BF))
-            lasts.append(jnp.exp(g_last))
-    solved = inverses(lowers, mask_ref)
-    maps = []
-    for head in range(KEY_HEADS):
-        for block in range(blocks):
-            i = head * blocks + block
-            fresh = dot(solved[i].astype(BF), rights[i]).astype(BF)
-            uw_ref[head, block * BLK : (block + 1) * BLK, :] = fresh
-            maps.append(dot(tails[i], fresh))
-    eye = jnp.where(iota2((BLK, BLK), 0) == iota2((BLK, BLK), 1), 1.0, 0.0).astype(F32)
-    for head in range(KEY_HEADS):
-        i = head * blocks
-        state_a = lasts[i] * eye - maps[i][:, BLK:]
-        state_b = maps[i][:, :BLK]
         for block in range(1, blocks):
-            i = head * blocks + block
-            state = jnp.concatenate([state_a, state_b], axis=1)
-            low = state.astype(BF)
-            prior_ref[head, block - 1] = low
-            state = lasts[i] * state - dot(maps[i][:, BLK:].astype(BF), low)
-            state_a = state[:, :BLK]
-            state_b = state[:, BLK:] + maps[i][:, :BLK]
-        state = jnp.concatenate([state_a, state_b], axis=1)
-        pair_ref[head] = state.astype(BF)
+            for place, head in enumerate(heads):
+                i = place * blocks + block
+                low = states[place].astype(BF)
+                prior_ref[base + head, block - 1] = low
+                state = others[i][2] * states[place] - dot(maps[i][:, BLK:].astype(BF), low)
+                states[place] = jnp.concatenate(
+                    [state[:, :BLK], state[:, BLK:] + maps[i][:, :BLK]], axis=1
+                )
+            yield
+        for place, head in enumerate(heads):
+            pair_ref[base + head] = states[place].astype(BF)
+
+    groups = [range(i, i + 2) for i in range(0, KEY_HEADS, 2)]
+    lowers, others, solved = [], [], []
+    for _ in front(groups[0], lowers, others):
+        pass
+    ending = iter(())
+    for place in range(len(groups)):
+        solved = []
+        later, later_others = [], []
+        if place + 1 < len(groups):
+            beside = front(groups[place + 1], later, later_others)
+        else:
+            beside = iter(())
+
+        together(inverses(lowers, mask_ref, solved), chained(ending, beside))
+        ending = back(groups[place], solved, others)
+        lowers, others = later, later_others
+    for _ in ending:
+        pass
 
 
 def query_side(
     odd_ref, rows_ref, g_ref, weight_ref, taps_ref, halo_ref, q_ref, kt_ref, uw_ref, prior_ref,
-    near_ref, *rest, first_step,
+    near_ref, scaled_ref, base_ref, pad_ref, *, first_step,
 ):
-    scaled_ref, base_ref, pad_ref = rest[-3:]
-    step = pl.program_id(0) + first_step
+    local_step = pl.program_id(0)
+    step = local_step + first_step
     length = q_ref.shape[0]
     blocks = length // BLK
-    levels = scaled_ref.shape[1] // (QUERY_HEADS * BLK) + 1
+    levels = scaled_ref.shape[2] // BLK + 1
     per_head = levels + 1
     width = weight_ref.shape[1]
     odd = odd_ref[0].astype(F32)
@@ -208,7 +261,9 @@
     for head in range(QUERY_HEADS):
         lanes = slice(head * BLK, (head + 1) * BLK)
         fill_padded(pad_ref, head, q_ref, halo_ref[0, :, lanes], lanes)
-        near = near_ref[head] * odd.astype(BF)
+        where = QUERY_HEADS * step + head
+        out = QUERY_HEADS * local_step + head
+        near = near_ref[where, :, BLK:] * odd.astype(BF)
         first = head * per_head
         for block in range(blocks):
             start = block * BLK
@@ -218,31 +273,28 @@
             g_row = rows_ref[head, 0:1, tokens]
             beta_row = rows_ref[head, 1:2, tokens]
             mixing = (
-                decay_matrix(g_col, g_row, beta_row) * dot(queries, kt_ref[head, :, tokens])
+                decay_matrix(g_col, g_row, beta_row) * dot(queries, kt_ref[where, :, tokens])
             ).astype(BF)
-            inner = dot(mixing, uw_ref[head, tokens, :])
-            through = jnp.exp(g_col) * queries.astype(F32) - inner[:, BLK:]
+            inner = dot(mixing, uw_ref[where, tokens, :])
+            through = jnp.exp2(g_col) * queries.astype(F32) - inner[:, BLK:]
             if block == 0:
                 carried, local = through, inner[:, :BLK]
             else:
-                passed = dot(through.astype(BF), prior_ref[head, block - 1])
+                passed = dot(through.astype(BF), prior_ref[where, block - 1])
                 carried, local = passed[:, :BLK], inner[:, :BLK] + passed[:, BLK:]
             scaled = [
                 (carried * turned_w[tokens, first + level : first + level + 1]).astype(BF)
                 for level in range(1, per_head)
             ]
-            base_ref[tokens, lanes] = turned_w[tokens, first : first + 1] * local + dot(
+            base_ref[out, tokens, :] = turned_w[tokens, first : first + 1] * local + dot(
                 scaled[0], near
             )
-            begin = head * (levels - 1) * BLK
-            scaled_ref[tokens, begin : begin + (levels - 1) * BLK] = jnp.concatenate(
-                scaled[1:], axis=1
-            )
+            scaled_ref[out, tokens, :] = jnp.concatenate(scaled[1:], axis=1)
 
 
 def finish_side(
-    core_ref, gain_ref, z_ref, base_ref, scaled_ref, near_ref, own_ref, far_ref, out_ref,
-    other_ref, sem,
+    core_ref, gain_ref, z_ref, near_ref, own_ref, other_ref, base_0, scaled_0, base_1, scaled_1,
+    out_ref,
 ):
     step = pl.program_id(0)
     core = core_ref[0]
@@ -250,31 +302,33 @@
     blocks = length // BLK
     levels = own_ref.shape[2] // BLK
     fold = pl.num_programs(0) // 2
-    mine = step // fold == core
-    begin_head = step % fold * FINISH_HEADS
-
-    @pl.when(step == 0)
-    def _():
-        fetch([(far_ref, other_ref)], sem)
-
     eye = jnp.where(iota2((BLK, BLK), 0) == iota2((BLK, BLK), 1), 1.0, 0.0).astype(BF)
-    for head in range(FINISH_HEADS):
-        lanes = slice(head * BLK, (head + 1) * BLK)
-        reach = jnp.where(core == 1, near_ref[head], eye)
-        seen = dot(reach, jnp.where(mine, own_ref[head], other_ref[begin_head + head])).astype(BF)
-        states = jnp.concatenate(
-            [seen[:, level * BLK : (level + 1) * BLK] for level in range(levels)], axis=0
-        )
-        begin = head * levels * BLK
-        for block in range(blocks):
-            tokens = slice(block * BLK, (block + 1) * BLK)
-            opened = base_ref[tokens, lanes] + dot(
-                scaled_ref[tokens, begin : begin + levels * BLK], states
+
+    def part(second, base_ref, scaled_ref):
+        mine = core == second
+        for head in range(FINISH_HEADS):
+            lanes = slice(head * BLK, (head + 1) * BLK)
+            place = step % fold * FINISH_HEADS + head
+            reach = jnp.where(core == 1, near_ref[step * FINISH_HEADS + head, :, :BLK], eye)
+            seen = dot(reach, jnp.where(mine, own_ref[place], other_ref[place])).astype(BF)
+            states = jnp.concatenate(
+                [seen[:, level * BLK : (level + 1) * BLK] for level in range(levels)], axis=0
             )
-            square = jnp.sum(opened * opened, axis=-1, keepdims=True) * (1.0 / BLK)
-            normed = opened * lax.rsqrt(square + EPS) * gain_ref[...]
-            gate = z_ref[tokens, lanes].astype(F32)
-            out_ref[tokens, lanes] = (normed * silu(gate)).astype(BF)
+            for block in range(blocks):
+                tokens = slice(block * BLK, (block + 1) * BLK)
+                opened = base_ref[place, tokens, :] + dot(scaled_ref[place, tokens, :], states)
+                square = jnp.sum(opened * opened, axis=-1, keepdims=True) * (1.0 / BLK)
+                normed = opened * lax.rsqrt(square + EPS) * gain_ref[...]
+                gate = z_ref[tokens, lanes].astype(F32)
+                out_ref[tokens, lanes] = (normed * silu(gate)).astype(BF)
+
+    @pl.when(step < fold)
+    def _():
+        part(0, base_0, scaled_0)
+
+    @pl.when(step >= fold)
+    def _():
+        part(1, base_1, scaled_1)
 
 
 def merged(left, right_a, right_b):
@@ -406,10 +460,7 @@
             by_head(KEY_HEADS, (2, length)), whole(g_pad.shape), by_column((3, 4, width)),
             by_column((3, 4, width)), by_column((length, width)), by_column((length, width)),
         ],
-        out_specs=[
-            by_head(KEY_HEADS, (BLK, length)), by_head(KEY_HEADS, (length, 2 * BLK)),
-            by_head(KEY_HEADS, (BLK, 2 * BLK)), by_head(KEY_HEADS, (blocks - 1, BLK, 2 * BLK)),
-        ],
+        out_specs=[VMEM] * 4,
         out_shape=[
             pltpu.VMEM((heads, BLK, length), BF), pltpu.VMEM((heads, length, 2 * BLK), BF),
             pltpu.VMEM((heads, BLK, 2 * BLK), BF),
@@ -425,60 +476,47 @@
     )(rows, g_pad, conv_weight, halo, *in_hbm(k_in, v_in))
 
 
-def queries_of(second, levels, core, rows, g_pad, weights, taps, halo, q_in, kt, uw, prior, near, previous):
+def queries_of(second, levels, core, rows, g_pad, weights, taps, halo, q_in, kt, uw, prior, near):
     heads, _, length = rows.shape
-    blocks = length // BLK
     steps = heads // QUERY_HEADS // 2
     first = steps if second else 0
     width = QUERY_HEADS * BLK
-    scaled_width = width * (levels - 1)
-    count = len(previous)
     return pl.pallas_call(
         functools.partial(query_side, first_step=first),
         grid=(steps,),
         in_specs=[
             SMEM, by_head(QUERY_HEADS, (2, length), first), whole(g_pad.shape),
             whole(weights.shape), by_column((3, 4, width), first), by_column((3, 4, width), first),
-            by_column((length, width), first), by_head(QUERY_HEADS, (BLK, length), first),
-            by_head(QUERY_HEADS, (length, 2 * BLK), first),
-            by_head(QUERY_HEADS, (blocks - 1, BLK, 2 * BLK), first),
-            by_head(QUERY_HEADS, (BLK, BLK), first, 1),
+            by_column((length, width), first),
         ]
-        + [ANY] * count,
-        out_specs=[by_column((length, scaled_width), first), by_column((length, width), first)],
+        + [VMEM] * 4,
+        out_specs=[VMEM] * 2,
         out_shape=[
-            pltpu.VMEM((length, heads * (levels - 1) * BLK), BF), pltpu.VMEM(q_in.shape, F32)
+            pltpu.VMEM((heads // 2, length, (levels - 1) * BLK), BF),
+            pltpu.VMEM((heads // 2, length, BLK), F32),
         ],
         scratch_shapes=[pltpu.VMEM((QUERY_HEADS, length + 8, BLK), F32)],
-        input_output_aliases={11 + i: i for i in range(count)},
         compiler_params=PARAMS,
         cost_estimate=COST,
         name="query_side",
-    )(
-        core, rows, g_pad, weights, taps, halo, *in_hbm(q_in), *in_vmem(kt, uw, prior, near),
-        *in_vmem(*previous),
-    )
-
-
-def finished(core, gain, z_in, base, scaled, near, own, other):
+    )(core, rows, g_pad, weights, taps, halo, *in_hbm(q_in), *in_vmem(kt, uw, prior, near))
+
+
+def finished(core, gain, z_in, near, own, other, base_0, scaled_0, base_1, scaled_1):
     length = z_in.shape[0]
-    heads, levels = near.shape[0], own.shape[2] // BLK
     width = FINISH_HEADS * BLK
-    fold = heads // FINISH_HEADS // 2
     return pl.pallas_call(
         finish_side,
-        grid=(2 * fold,),
-        in_specs=[
-            SMEM, whole(gain.shape), by_column((length, width)), by_column((length, width)),
-            by_column((length, width * levels)), by_head(FINISH_HEADS, (BLK, BLK)),
-            pl.BlockSpec((FINISH_HEADS, BLK, levels * BLK), lambda i: (i % fold, 0, 0)), ANY,
-        ],
+        grid=(near.shape[0] // FINISH_HEADS,),
+        in_specs=[SMEM, whole(gain.shape), by_column((length, width))] + [VMEM] * 7,
         out_specs=by_column((length, width)),
         out_shape=shape_of(z_in.shape, BF),
-        scratch_shapes=[pltpu.VMEM(other.shape, BF), pltpu.SemaphoreType.DMA((1,))],
         compiler_params=PARAMS,
         name="finish_side",
-    )(core, gain, *in_hbm(z_in), *in_vmem(base, scaled, near, own, other))
+    )(
+        core, gain, *in_hbm(z_in),
+        *in_vmem(near, own, other, base_0, scaled_0, base_1, scaled_1),
+    )
 
 
 def joined_near(core, pair, near):
@@ -534,7 +572,7 @@
     edge = jnp.stack([x[length - 4 :] for x in (q_in, k_in, v_in)], axis=0)
     halo = lax.ppermute(edge, "ctx", [(i, i + 1) for i in range(ctx - 1)])
 
-    g = jnp.cumsum(log_gate.reshape(blocks, BLK, heads), axis=1).reshape(length, heads)
+    g = jnp.cumsum(log_gate.reshape(blocks, BLK, heads), axis=1).reshape(length, heads) * LOG2_E
     g_pad = jnp.pad(g, ((0, 0), (0, BLK - heads)))
     rows = jnp.stack([g.T, beta.T], axis=1)
     weights = level_weight[:, :, : levels + 1].reshape(length, heads * (levels + 1))
@@ -549,28 +587,27 @@
     near = lax.ppermute(pair, "ctx", [(i, i ^ 1) for i in range(ctx)])
     pair = joined_near(core, pair, near)
 
-    def queries(second, q_in, previous):
+    def queries(second, q_in):
         return queries_of(
-            second, levels, core, rows, g_pad, weights, conv_weight, halo, q_in, kt, uw, prior,
-            near, previous,
+            second, levels, core, rows, g_pad, weights, conv_weight, halo, q_in, kt, uw, prior, near
         )
 
-    reach, states, parts = None, [], ()
+    reach, states = None, []
     for level in range(1, levels - 1):
         far = lax.ppermute(pair, "ctx", [(i, i ^ 2**level) for i in range(ctx)])
         if level == 1:
-            parts = queries(False, q_in, ())
-            far, *parts = lax.optimization_barrier((far, *parts))
+            far, scaled_0, base_0 = lax.optimization_barrier((far, *queries(False, q_in)))
         pair, state, reach = joined_far(bits[level], pair, far, reach, level == levels - 2)
         states.append(state)
     top = levels - 1
     pair, later_q = lax.optimization_barrier((pair, q_in))
-    far = lax.ppermute(pair, "ctx", [(i, i + 2**top) for i in range(ctx - 2**top)])
-    parts = queries(True, later_q, parts)
-    far, scaled, base = lax.optimization_barrier((far, *parts))
+    far = lax.ppermute(pair, "ctx", [(i, i ^ 2**top) for i in range(ctx)])
+    far, scaled_1, base_1 = lax.optimization_barrier((far, *queries(True, later_q)))
     own = joined_top(bits[top], far, reach, states)
     other = lax.ppermute(own, "ctx", [(i, i ^ 1) for i in range(ctx)])
-    return finished(core, norm_gain.reshape(1, BLK), z_in, base, scaled, near, own, other)
+    return finished(
+        core, norm_gain.reshape(1, BLK), z_in, near, own, other, base_0, scaled_0, base_1, scaled_1
+    )
 
 
 def solution(mesh):

time: 73.3 us -> 70.6 us (0.963)
  starting transfers between devices: 11.4 us -> 9.64 us
  local copies, waits for them, and re-layouts: 3.86 us -> 2.95 us
    ppermute x1, starting transfers between devices: 4.5 us -> 2.65 us  [per_device(): far = lax.ppermute(pair, 'ctx', [(i, i ^ 2 ** top) for i in range(ctx)])]
    slice x2 -> x3, local copies, waits for them, and re-layouts: 1 us -> 0.09 us  [per_device(): level_weight[:, :, :levels + 1].reshape(length, heads * (levels + 1))]
  transfers between devices with their start and end apart: 5 -> 5, of which waited for: 3 -> 4; matrix products, arithmetic and copies ran while one was open for 4% -> 3% of each run, Pallas kernels for 32% -> 32%
where the time goes in v4:
time: 70.6 us; the launch traced here: 70.1 us
  Pallas kernels  50.4 us (71%)
  starting transfers between devices  9.64 us (14%)
  waiting for transfers between devices  5.82 us (8%)
  local copies, waits for them, and re-layouts  2.95 us (4%)
  other arithmetic  1.1 us (2%)
    pallas_call x2, Pallas kernels, queries_of(): pl.pallas_call(functools.partial(query_side, first_step=first), grid=(ste...  22.6 us
    pallas_call x1, Pallas kernels, keys_of(): pl.pallas_call(key_side, grid=(heads // KEY_HEADS,), in_specs=[by_head(KE...  20 us
    pallas_call x1, Pallas kernels, finished(): pl.pallas_call(finish_side, grid=(near.shape[0] // FINISH_HEADS,), in_spe...  6.91 us
    ppermute x1, starting transfers between devices, per_device(): near = lax.ppermute(pair, 'ctx', [(i, i ^ 1) for i in range(ctx)])  2.74 us
    ppermute x1, starting transfers between devices, per_device(): far = lax.ppermute(pair, 'ctx', [(i, i ^ 2 ** top) for i in range(ctx)])  2.65 us
    ppermute x1, starting transfers between devices, per_device(): halo = lax.ppermute(edge, 'ctx', [(i, i + 1) for i in range(ctx - 1)])  2.53 us
    ppermute x1, waiting for transfers between devices, per_device(): near = lax.ppermute(pair, 'ctx', [(i, i ^ 1) for i in range(ctx)])  2.29 us
    ppermute x1, waiting for transfers between devices, per_device(): other = lax.ppermute(own, 'ctx', [(i, i ^ 1) for i in range(ctx)])  1.9 us
  transfers between devices with their start and end apart: 5, of which 4 were waited for; matrix products, arithmetic and copies ran while one was open for 3% of the time, Pallas kernels for 32%

profile of v4, /device:TPU:0, one launch (start us, length us, event | category | flops | bytes accessed | tf_op | source)
XLA Modules:
  0.0 70.1 jit_solution(11770311462132536383)
XLA Ops:
  0.0 0.0 slice-start
  0.0 0.8 %slice_bitcast_fusion.2 = bf16[1,4,2048]{2,1,0:T(4,128)(2,1)S(1)} fusion(bf16[512,2048]{1,0:T(8,128)(2,1)} %q_ref.2), kind=kLoop, calls=%fused_computation.5 | loop fusion | bytes 32768 | tf_op jit(solution)/shard_map/stack | solution.py:572
  0.8 0.8 %slice_bitcast_fusion = (bf16[1,4,2048]{2,1,0:T(4,128)(2,1)S(1)}, bf16[1,4,2048]{2,1,0:T(4,128)(2,1)S(1)}) fusion(bf16[512,2048]{1,0:T(8,128)(2,1)} %v_ref.1, bf16[512,2048]{1,0:T(8,128)(2,1)} %k_ref.1), kind=kLoop, calls=%fused_computation.3 | loop fusion | bytes 65536 | tf_op jit(solution)/shard_map/stack | solution.py:572
  1.7 0.0 copy-start.1
  1.7 2.5 %collective-permute-start = (bf16[3,4,2048]{2,1,0:T(4,128)(2,1)S(1)}, bf16[3,4,2048]{2,1,0:T(4,128)(2,1)S(1)}, u32[]{:S(2)}, u32[]{:S(2)}) collective-permute-start(bf16[3,4,2048]{2,1,0:T(4,128)(2,1)S(1)} %pad_maximum_fusion.1), channel_id=1, source_target_pairs={{0,1},{1,2},{2,3},{3,4},{4,5},{5,6},{6,7},{8,9},{9,10},{10,11},{11... | collective-permute-start | bytes 147464 | tf_op jit(solution)/shard_map/ppermute | solution.py:573
  4.2 0.9 %copy.30 = f32[512,16]{1,0:T(8,128)S(1)} copy(f32[512,16]{0,1:T(8,128)} %param.13) | data formatting | bytes 65536 | tf_op jit(solution)/shard_map/reshape | solution.py:575
  5.1 0.3 reduce_window_sum.11
  5.4 0.1 copy.24
  5.5 0.8 %pad_maximum_fusion = f32[16,2,512]{2,0,1:T(8,128)S(1)} fusion(f32[16,1,512]{2,0,1:T(8,128)} %bitcast.25, f32[16,1,512]{2,0,1:T(8,128)S(1)} %copy.24), kind=kLoop, calls=%fused_computation.1 | loop fusion | flops 16384 | bytes 131072 | tf_op jit(solution)/shard_map/stack | solution.py:577
  6.3 0.0 slice-done
  6.3 0.1 copy.25
  6.4 0.1 copy.26
  6.6 0.0 collective-permute-done.halo_ref
  6.6 0.1 copy.27.rows_ref
  6.7 0.0 copy-done.1
  6.7 20.0 %key_side.1 = (bf16[16,128,512]{2,1,0:T(8,128)(2,1)S(1)}, bf16[16,512,256]{2,1,0:T(8,128)(2,1)S(1)}, bf16[16,128,256]{2,1,0:T(8,128)(2,1)S(1)}, bf16[16,3,128,256]{3,2,1,0:T(8,128)(2,1)S(1)}) custom-call(f32[16,2,512]{2,1,0:T(2,128)S(1)} %copy.27.rows_ref, f32[512,128]{1,0:T(8,128)S(1)} %pad.8.g_ref, f32[3,4,2048]{2,1,0:T(4,128)S(1)} %copy-done.1, ...), custom_call_target="tpu_custom_call" | custom-call | flops 10000000000 | bytes 20000000 | tf_op jit(solution)/shard_map/key_side/pallas_call | solution.py:456
  26.7 2.7 %collective-permute-start.1 = (bf16[16,128,256]{2,1,0:T(8,128)(2,1)S(1)}, bf16[16,128,256]{2,1,0:T(8,128)(2,1)S(1)}, u32[]{:S(2)}, u32[]{:S(2)}) collective-permute-start(bf16[16,128,256]{2,1,0:T(8,128)(2,1)S(1)} %get-tuple-element.35.pair_ref), channel_id=1, source_target_pairs={{0,1},{1,0},{2,3},{3,2},{4,5},{5,4},{6,7},{7,6},{8,9},{9,8},{10,11... | collective-permute-start | bytes 3145736 | tf_op jit(solution)/shard_map/ppermute | solution.py:587
  29.4 2.3 %collective-permute-done.1.far_ref.near_ref = bf16[16,128,256]{2,1,0:T(8,128)(2,1)S(1)} collective-permute-done((bf16[16,128,256]{2,1,0:T(8,128)(2,1)S(1)}, bf16[16,128,256]{2,1,0:T(8,128)(2,1)S(1)}, u32[]{:S(2)}, u32[]{:S(2)}) %collective-permute-start.1) | collective-permute-done | bytes 1048608 | tf_op jit(solution)/shard_map/ppermute | solution.py:587
  31.7 0.4 join_near.1.pair_ref
  32.1 1.6 %collective-permute-start.2 = (bf16[8,128,256]{2,1,0:T(8,128)(2,1)S(1)}, bf16[8,128,256]{2,1,0:T(8,128)(2,1)S(1)}, u32[]{:S(2)}, u32[]{:S(2)}) collective-permute-start(bf16[8,128,256]{2,1,0:T(8,128)(2,1)S(1)} %join_near.1.pair_ref), channel_id=1, source_target_pairs={{0,2},{1,3},{2,0},{3,1},{4,6},{5,7},{6,4},{7,5},{8,10},{9,11},{10,... | collective-permute-start | bytes 1572872 | tf_op jit(solution)/shard_map/ppermute | solution.py:597
  33.7 11.3 %query_side.2 = (bf16[8,512,256]{2,1,0:T(8,128)(2,1)S(1)}, f32[8,512,128]{2,1,0:T(8,128)S(1)}) custom-call(s32[1]{0:T(128)} %bitcast.9.core_ref.odd_ref, f32[16,2,512]{2,1,0:T(2,128)S(1)} %copy.27.rows_ref, f32[512,128]{1,0:T(8,128)S(1)} %pad.8.g_ref, f32[512,128]{1,0:T(8,128)S(1)} %pad.9.weight_ref, f32[3,4,2048]{2,1,0:T(4,128)S(1)} %copy-done.1, ...), custom_call_target="tpu_custom_call" | custom-call | flops 10000000000 | bytes 20000000 | tf_op jit(solution)/shard_map/query_side/pallas_call | solution.py:484
  45.1 1.3 %collective-permute-done.2.far_ref = bf16[8,128,256]{2,1,0:T(8,128)(2,1)S(1)} collective-permute-done((bf16[8,128,256]{2,1,0:T(8,128)(2,1)S(1)}, bf16[8,128,256]{2,1,0:T(8,128)(2,1)S(1)}, u32[]{:S(2)}, u32[]{:S(2)}) %collective-permute-start.2) | collective-permute-done | bytes 524320 | tf_op jit(solution)/shard_map/ppermute | solution.py:597
  46.4 0.4 join_far.1
  46.8 0.0 copy-start
  46.8 2.7 %collective-permute-start.3 = (bf16[8,128,128]{2,1,0:T(8,128)(2,1)S(1)}, bf16[8,128,128]{2,1,0:T(8,128)(2,1)S(1)}, u32[]{:S(2)}, u32[]{:S(2)}) collective-permute-start(bf16[8,128,128]{2,1,0:T(8,128)(2,1)S(1)} %get-tuple-element.46), channel_id=1, source_target_pairs={{0,4},{1,5},{2,6},{3,7},{4,0},{5,1},{6,2},{7,3},{8,12},{9,13},{10,... | collective-permute-start | bytes 786440 | tf_op jit(solution)/shard_map/ppermute | solution.py:604
  49.4 11.3 %query_side.3 = (bf16[8,512,256]{2,1,0:T(8,128)(2,1)S(1)}, f32[8,512,128]{2,1,0:T(8,128)S(1)}) custom-call(s32[1]{0:T(128)} %bitcast.9.core_ref.odd_ref, f32[16,2,512]{2,1,0:T(2,128)S(1)} %copy.27.rows_ref, f32[512,128]{1,0:T(8,128)S(1)} %pad.8.g_ref, f32[512,128]{1,0:T(8,128)S(1)} %pad.9.weight_ref, f32[3,4,2048]{2,1,0:T(4,128)S(1)} %copy-done.1, ...), custom_call_target="tpu_custom_call" | custom-call | flops 10000000000 | bytes 20000000 | tf_op jit(solution)/shard_map/query_side/pallas_call | solution.py:484
  60.7 0.3 collective-permute-done.3.far_ref
  61.1 0.1 join_top.1.own_ref
  61.2 0.1 collective-permute-start.4
  61.3 1.9 %collective-permute-done.4.other_ref = bf16[8,128,256]{2,1,0:T(8,128)(2,1)S(1)} collective-permute-done((bf16[8,128,256]{2,1,0:T(8,128)(2,1)S(1)}, bf16[8,128,256]{2,1,0:T(8,128)(2,1)S(1)}, u32[]{:S(2)}, u32[]{:S(2)}) %collective-permute-start.4) | collective-permute-done | bytes 524320 | tf_op jit(solution)/shard_map/ppermute | solution.py:607
  63.2 0.0 copy-done
  63.2 6.9 %finish_side.1 = bf16[512,2048]{1,0:T(8,128)(2,1)} custom-call(s32[1]{0:T(128)} %bitcast.9.core_ref.odd_ref, f32[1,128]{1,0:T(1,128)S(1)} %bitcast.21, bf16[512,2048]{1,0:T(8,128)(2,1)} %z_ref.1, bf16[16,128,256]{2,1,0:T(8,128)(2,1)S(1)} %collective-permute-done.1.far_ref.near_ref, bf16[8,128,256]{2,1,0:T(8,128)(2,1)S(1)} %join_top.1.own_ref, ...), custom_call_target="tpu_custom_call" | custom-call | tf_op jit(solution)/shard_map/finish_side/pallas_call | solution.py:508
  (5 shorter events, 0.2 us)
Async XLA Ops:
  0.0 6.3 %slice-start = ((f32[512,16,6]{0,1,2:T(8,128)}), f32[512,16,4]{0,1,2:T(8,128)S(1)}, s32[]{:S(2)}) async-start(f32[512,16,6]{0,1,2:T(8,128)} %param.15), calls=%async_computation | async-start | bytes 262144 | tf_op jit(solution)/shard_map/slice | solution.py:578
  1.7 5.0 %copy-start.1 = (f32[3,4,2048]{2,1,0:T(4,128)S(1)}, f32[3,4,2048]{2,1,0:T(4,128)}, u32[]{:S(2)}) copy-start(f32[3,4,2048]{2,1,0:T(4,128)} %taps_ref.5) | copy-start | bytes 294916
  1.7 5.0 %collective-permute-start = (bf16[3,4,2048]{2,1,0:T(4,128)(2,1)S(1)}, bf16[3,4,2048]{2,1,0:T(4,128)(2,1)S(1)}, u32[]{:S(2)}, u32[]{:S(2)}) collective-permute-start(bf16[3,4,2048]{2,1,0:T(4,128)(2,1)S(1)} %pad_maximum_fusion.1), channel_id=1, source_target_pairs={{0,1},{1,2},{2,3},{3,4},{4,5},{5,6},{6,7},{8,9},{9,10},{10,11},{11... | collective-permute-start | bytes 147464 | tf_op jit(solution)/shard_map/ppermute | solution.py:573
  26.7 5.0 %collective-permute-start.1 = (bf16[16,128,256]{2,1,0:T(8,128)(2,1)S(1)}, bf16[16,128,256]{2,1,0:T(8,128)(2,1)S(1)}, u32[]{:S(2)}, u32[]{:S(2)}) collective-permute-start(bf16[16,128,256]{2,1,0:T(8,128)(2,1)S(1)} %get-tuple-element.35.pair_ref), channel_id=1, source_target_pairs={{0,1},{1,0},{2,3},{3,2},{4,5},{5,4},{6,7},{7,6},{8,9},{9,8},{10,11... | collective-permute-start | bytes 3145736 | tf_op jit(solution)/shard_map/ppermute | solution.py:587
  32.1 14.3 %collective-permute-start.2 = (bf16[8,128,256]{2,1,0:T(8,128)(2,1)S(1)}, bf16[8,128,256]{2,1,0:T(8,128)(2,1)S(1)}, u32[]{:S(2)}, u32[]{:S(2)}) collective-permute-start(bf16[8,128,256]{2,1,0:T(8,128)(2,1)S(1)} %join_near.1.pair_ref), channel_id=1, source_target_pairs={{0,2},{1,3},{2,0},{3,1},{4,6},{5,7},{6,4},{7,5},{8,10},{9,11},{10,... | collective-permute-start | bytes 1572872 | tf_op jit(solution)/shard_map/ppermute | solution.py:597
  46.8 16.4 %copy-start = (f32[128]{0:T(128)S(1)}, f32[128]{0:T(128)}, u32[]{:S(2)}) copy-start(f32[128]{0:T(128)} %param.17) | copy-start | bytes 1540
  46.8 14.3 %collective-permute-start.3 = (bf16[8,128,128]{2,1,0:T(8,128)(2,1)S(1)}, bf16[8,128,128]{2,1,0:T(8,128)(2,1)S(1)}, u32[]{:S(2)}, u32[]{:S(2)}) collective-permute-start(bf16[8,128,128]{2,1,0:T(8,128)(2,1)S(1)} %get-tuple-element.46), channel_id=1, source_target_pairs={{0,4},{1,5},{2,6},{3,7},{4,0},{5,1},{6,2},{7,3},{8,12},{9,13},{10,... | collective-permute-start | bytes 786440 | tf_op jit(solution)/shard_map/ppermute | solution.py:604
  61.2 2.0 %collective-permute-start.4 = (bf16[8,128,256]{2,1,0:T(8,128)(2,1)S(1)}, bf16[8,128,256]{2,1,0:T(8,128)(2,1)S(1)}, u32[]{:S(2)}, u32[]{:S(2)}) collective-permute-start(bf16[8,128,256]{2,1,0:T(8,128)(2,1)S(1)} %join_top.1.own_ref), channel_id=1, source_target_pairs={{0,1},{1,0},{2,3},{3,2},{4,5},{5,4},{6,7},{7,6},{8,9},{9,8},{10,11... | collective-permute-start | bytes 1572872 | tf_op jit(solution)/shard_map/ppermute | solution.py:607

commit v5 on v4

--- a/solution.py
+++ b/solution.py
@@ -9,8 +9,8 @@
 
 BLK = 128
 SUB = 16
-KEY_HEADS = 4
-QUERY_HEADS = 2
+PAIR = 4
+QUERY_HEADS = 4
 FINISH_HEADS = 4
 EPS = 1e-06
 LOG2_E = 1.4426950408889634
@@ -133,11 +133,6 @@
         size, index = size * 2, index + 2
 
 
-def chained(first, second):
-    yield from first
-    yield from second
-
-
 def together(first, second):
     live = [first, second]
     while live:
@@ -147,106 +142,105 @@
 
 
 def key_side(
-    rows_ref, g_ref, taps_ref, halo_ref, k_ref, v_ref,
-    kt_ref, uw_ref, pair_ref, prior_ref, pad_ref, mask_ref,
+    rows_ref, g_ref, taps_ref, halo_ref, k_first, v_first, k_next, v_next,
+    kt_ref, uw_ref, pair_ref, prior_ref, pad_ref, low_ref, right_ref, tail_ref, mask_ref,
 ):
     step = pl.program_id(0)
-
-    @pl.when(step == 0)
-    def _():
-        make_masks(mask_ref)
-
-    length = k_ref.shape[0]
+    length = k_first.shape[0]
     blocks = length // BLK
-    base = KEY_HEADS * step
-    turned_g = pltpu.roll(g_ref[...], BLK - KEY_HEADS * step, 1)
+    last = kt_ref.shape[0] // PAIR - 1
     eye = jnp.where(iota2((BLK, BLK), 0) == iota2((BLK, BLK), 1), 1.0, 0.0).astype(F32)
 
-    def front(heads, lowers, others):
-        for head in heads:
-            lanes = slice(head * BLK, (head + 1) * BLK)
-            fill_padded(pad_ref, 2 * head, k_ref, halo_ref[1, :, lanes], lanes)
-            fill_padded(pad_ref, 2 * head + 1, v_ref, halo_ref[2, :, lanes], lanes)
+    def front(pair, k_ref, v_ref, slot):
+        turned_g = pltpu.roll(g_ref[...], BLK - PAIR * pair, 1)
+        for place in range(PAIR):
+            head = PAIR * pair + place
+            lanes = slice(place * BLK, (place + 1) * BLK)
+            columns = pl.ds(pl.multiple_of(head * BLK, BLK), BLK)
+            pad = 2 * (PAIR * slot + place)
+            fill_padded(pad_ref, pad, k_ref, halo_ref[1, :, columns], lanes)
+            fill_padded(pad_ref, pad + 1, v_ref, halo_ref[2, :, columns], lanes)
+            key_taps, value_taps = taps_ref[1, :, columns], taps_ref[2, :, columns]
             for block in range(blocks):
+                i = place * blocks + block
                 start = block * BLK
                 tokens = slice(start, start + BLK)
-                keys = unit(conv_rows(pad_ref, 2 * head, taps_ref[1, :, lanes], start, BLK))
-                keys = keys.astype(BF)
-                values = conv_rows(pad_ref, 2 * head + 1, taps_ref[2, :, lanes], start, BLK)
+                keys = unit(conv_rows(pad_ref, pad, key_taps, start, BLK)).astype(BF)
+                values = conv_rows(pad_ref, pad + 1, value_taps, start, BLK)
                 keys_f = keys.astype(F32)
                 turned = keys_f.T
                 turned_b = turned.astype(BF)
-                kt_ref[base + head, :, tokens] = turned_b
-                g_col = jnp.broadcast_to(turned_g[tokens, head : head + 1], (BLK, BLK))
+                kt_ref[head, :, tokens] = turned_b
+                right_ref[slot, i, :, :BLK] = values.astype(BF)
+                yield
+                g_col = jnp.broadcast_to(turned_g[tokens, place : place + 1], (BLK, BLK))
                 g_row = rows_ref[head, 0:1, tokens]
                 beta_row = rows_ref[head, 1:2, tokens]
                 g_last = g_row[:, BLK - 1 : BLK]
-                lowers.append(decay_matrix(g_col, g_row, beta_row) * dot(keys, turned_b))
-                right = jnp.concatenate(
-                    [values.astype(BF), (jnp.exp2(g_col) * keys_f).astype(BF)], axis=1
-                )
-                tail = (turned * (jnp.exp2(g_last - g_row) * beta_row)).astype(BF)
-                others.append((right, tail, jnp.exp2(g_last)))
+                low_ref[slot, i] = decay_matrix(g_col, g_row, beta_row) * dot(keys, turned_b)
+                right_ref[slot, i, :, BLK:] = (jnp.exp2(g_col) * keys_f).astype(BF)
+                tail_ref[slot, i] = (turned * (jnp.exp2(g_last - g_row) * beta_row)).astype(BF)
                 yield
 
-    def back(heads, solved, others):
+    def back(pair, slot):
+        solved = []
+        yield from inverses(
+            [low_ref.at[slot, i] for i in range(PAIR * blocks)], mask_ref, solved
+        )
         maps = []
-        for place, head in enumerate(heads):
-            for block in range(blocks):
-                i = place * blocks + block
-                fresh = dot(solved[i].astype(BF), others[i][0]).astype(BF)
-                uw_ref[base + head, block * BLK : (block + 1) * BLK, :] = fresh
-                maps.append(fresh)
-            yield
-        for place, head in enumerate(heads):
-            for block in range(blocks):
-                i = place * blocks + block
-                maps[i] = dot(others[i][1], maps[i])
-            yield
-        states = []
-        for place, head in enumerate(heads):
+        for i in range(PAIR * blocks):
+            fresh = dot(solved[i].astype(BF), right_ref[slot, i]).astype(BF)
+            tokens = slice(i % blocks * BLK, (i % blocks + 1) * BLK)
+            uw_ref[PAIR * pair + i // blocks, tokens, :] = fresh
+            maps.append(fresh)
+        yield
+        maps = [dot(tail_ref[slot, i], maps[i]) for i in range(PAIR * blocks)]
+        yield
+        states, falls = [], []
+        for i in range(PAIR * blocks):
+            end = (i % blocks + 1) * BLK
+            falls.append(
+                jnp.exp2(rows_ref[PAIR * pair + i // blocks, 0:1, end - 1 : end])
+            )
+        for place in range(PAIR):
             i = place * blocks
             states.append(
-                jnp.concatenate(
-                    [others[i][2] * eye - maps[i][:, BLK:], maps[i][:, :BLK]], axis=1
-                )
+                jnp.concatenate([falls[i] * eye - maps[i][:, BLK:], maps[i][:, :BLK]], axis=1)
             )
         for block in range(1, blocks):
-            for place, head in enumerate(heads):
+            for place in range(PAIR):
                 i = place * blocks + block
                 low = states[place].astype(BF)
-                prior_ref[base + head, block - 1] = low
-                state = others[i][2] * states[place] - dot(maps[i][:, BLK:].astype(BF), low)
+                prior_ref[PAIR * pair + place, block - 1] = low
+                state = falls[i] * states[place] - dot(maps[i][:, BLK:].astype(BF), low)
                 states[place] = jnp.concatenate(
                     [state[:, :BLK], state[:, BLK:] + maps[i][:, :BLK]], axis=1
                 )
             yield
-        for place, head in enumerate(heads):
-            pair_ref[base + head] = states[place].astype(BF)
-
-    groups = [range(i, i + 2) for i in range(0, KEY_HEADS, 2)]
-    lowers, others, solved = [], [], []
-    for _ in front(groups[0], lowers, others):
-        pass
-    ending = iter(())
-    for place in range(len(groups)):
-        solved = []
-        later, later_others = [], []
-        if place + 1 < len(groups):
-            beside = front(groups[place + 1], later, later_others)
-        else:
-            beside = iter(())
-
-        together(inverses(lowers, mask_ref, solved), chained(ending, beside))
-        ending = back(groups[place], solved, others)
-        lowers, others = later, later_others
-    for _ in ending:
-        pass
+        for place in range(PAIR):
+            pair_ref[PAIR * pair + place] = states[place].astype(BF)
+
+    @pl.when(step == 0)
+    def _():
+        make_masks(mask_ref)
+        for _ in front(0, k_first, v_first, 0):
+            pass
+
+    for slot in range(2):
+
+        @pl.when((step % 2 == slot) & (step < last))
+        def _():
+            together(back(step, slot), front(step + 1, k_next, v_next, 1 - slot))
+
+    @pl.when(step == last)
+    def _():
+        for _ in back(last, last % 2):
+            pass
 
 
 def query_side(
-    odd_ref, rows_ref, g_ref, weight_ref, taps_ref, halo_ref, q_ref, kt_ref, uw_ref, prior_ref,
-    near_ref, scaled_ref, base_ref, pad_ref, *, first_step,
+    odd_ref, rows_ref, g_ref, weight_ref, taps_ref, halo_ref, gain_ref, q_ref, z_ref, kt_ref,
+    uw_ref, prior_ref, near_ref, scaled_ref, base_ref, gate_ref, pad_ref, *, first_step,
 ):
     local_step = pl.program_id(0)
     step = local_step + first_step
@@ -290,21 +284,22 @@
                 scaled[0], near
             )
             scaled_ref[out, tokens, :] = jnp.concatenate(scaled[1:], axis=1)
+            gate_ref[out, tokens, :] = silu(z_ref[tokens, lanes].astype(F32)) * gain_ref[...]
 
 
 def finish_side(
-    core_ref, gain_ref, z_ref, near_ref, own_ref, other_ref, base_0, scaled_0, base_1, scaled_1,
+    core_ref, near_ref, own_ref, other_ref, scaled_0, base_0, gate_0, scaled_1, base_1, gate_1,
     out_ref,
 ):
     step = pl.program_id(0)
     core = core_ref[0]
-    length = z_ref.shape[0]
+    length = out_ref.shape[0]
     blocks = length // BLK
     levels = own_ref.shape[2] // BLK
     fold = pl.num_programs(0) // 2
     eye = jnp.where(iota2((BLK, BLK), 0) == iota2((BLK, BLK), 1), 1.0, 0.0).astype(BF)
 
-    def part(second, base_ref, scaled_ref):
+    def part(second, scaled_ref, base_ref, gate_ref):
         mine = core == second
         for head in range(FINISH_HEADS):
             lanes = slice(head * BLK, (head + 1) * BLK)
@@ -318,17 +313,16 @@
                 tokens = slice(block * BLK, (block + 1) * BLK)
                 opened = base_ref[place, tokens, :] + dot(scaled_ref[place, tokens, :], states)
                 square = jnp.sum(opened * opened, axis=-1, keepdims=True) * (1.0 / BLK)
-                normed = opened * lax.rsqrt(square + EPS) * gain_ref[...]
-                gate = z_ref[tokens, lanes].astype(F32)
-                out_ref[tokens, lanes] = (normed * silu(gate)).astype(BF)
+                normed = opened * lax.rsqrt(square + EPS)
+                out_ref[tokens, lanes] = (normed * gate_ref[place, tokens, :]).astype(BF)
 
     @pl.when(step < fold)
     def _():
-        part(0, base_0, scaled_0)
+        part(0, scaled_0, base_0, gate_0)
 
     @pl.when(step >= fold)
     def _():
-        part(1, base_1, scaled_1)
+        part(1, scaled_1, base_1, gate_1)
 
 
 def merged(left, right_a, right_b):
@@ -452,13 +446,18 @@
 def keys_of(rows, g_pad, conv_weight, halo, k_in, v_in):
     heads, _, length = rows.shape
     blocks = length // BLK
-    width = KEY_HEADS * BLK
+    width = PAIR * BLK
+    steps = heads // PAIR
+    units = PAIR * blocks
+    first = pl.BlockSpec((length, width), lambda i: (0, 0))
+    following = pl.BlockSpec((length, width), lambda i: (0, jnp.minimum(i + 1, steps - 1)))
+    keys, values = in_hbm(k_in, v_in)
     return pl.pallas_call(
         key_side,
-        grid=(heads // KEY_HEADS,),
+        grid=(steps,),
         in_specs=[
-            by_head(KEY_HEADS, (2, length)), whole(g_pad.shape), by_column((3, 4, width)),
-            by_column((3, 4, width)), by_column((length, width)), by_column((length, width)),
+            whole(rows.shape), whole(g_pad.shape), whole(conv_weight.shape), whole(halo.shape),
+            first, first, following, following,
         ],
         out_specs=[VMEM] * 4,
         out_shape=[
@@ -467,16 +466,19 @@
             pltpu.VMEM((heads, blocks - 1, BLK, 2 * BLK), BF),
         ],
         scratch_shapes=[
-            pltpu.VMEM((2 * KEY_HEADS, length + 8, BLK), F32),
+            pltpu.VMEM((4 * PAIR, length + 8, BLK), F32),
+            pltpu.VMEM((2, units, BLK, BLK), F32),
+            pltpu.VMEM((2, units, BLK, 2 * BLK), BF),
+            pltpu.VMEM((2, units, BLK, BLK), BF),
             pltpu.VMEM((6, BLK, BLK), BF),
         ],
         compiler_params=PARAMS,
         cost_estimate=COST,
         name="key_side",
-    )(rows, g_pad, conv_weight, halo, *in_hbm(k_in, v_in))
-
-
-def queries_of(second, levels, core, rows, g_pad, weights, taps, halo, q_in, kt, uw, prior, near):
+    )(rows, g_pad, conv_weight, halo, keys, values, keys, values)
+
+
+def queries_of(second, levels, core, rows, g_pad, weights, taps, halo, gain, q_in, z_in, *kept):
     heads, _, length = rows.shape
     steps = heads // QUERY_HEADS // 2
     first = steps if second else 0
@@ -487,36 +489,54 @@
         in_specs=[
             SMEM, by_head(QUERY_HEADS, (2, length), first), whole(g_pad.shape),
             whole(weights.shape), by_column((3, 4, width), first), by_column((3, 4, width), first),
-            by_column((length, width), first),
+            whole(gain.shape), by_column((length, width), first), by_column((length, width), first),
         ]
         + [VMEM] * 4,
-        out_specs=[VMEM] * 2,
+        out_specs=[VMEM] * 3,
         out_shape=[
             pltpu.VMEM((heads // 2, length, (levels - 1) * BLK), BF),
+            pltpu.VMEM((heads // 2, length, BLK), F32),
             pltpu.VMEM((heads // 2, length, BLK), F32),
         ],
         scratch_shapes=[pltpu.VMEM((QUERY_HEADS, length + 8, BLK), F32)],
         compiler_params=PARAMS,
         cost_estimate=COST,
         name="query_side",
-    )(core, rows, g_pad, weights, taps, halo, *in_hbm(q_in), *in_vmem(kt, uw, prior, near))
-
-
-def finished(core, gain, z_in, near, own, other, base_0, scaled_0, base_1, scaled_1):
-    length = z_in.shape[0]
-    width = FINISH_HEADS * BLK
+    )(core, rows, g_pad, weights, taps, halo, gain, *in_hbm(q_in, z_in), *in_vmem(*kept))
+
+
+def finished(core, near, own, other, *parts):
+    heads, length = near.shape[0], parts[0].shape[1]
     return pl.pallas_call(
         finish_side,
-        grid=(near.shape[0] // FINISH_HEADS,),
-        in_specs=[SMEM, whole(gain.shape), by_column((length, width))] + [VMEM] * 7,
-        out_specs=by_column((length, width)),
-        out_shape=shape_of(z_in.shape, BF),
+        grid=(heads // FINISH_HEADS,),
+        in_specs=[SMEM] + [VMEM] * 9,
+        out_specs=by_column((length, FINISH_HEADS * BLK)),
+        out_shape=shape_of((length, heads * BLK), BF),
         compiler_params=PARAMS,
         name="finish_side",
-    )(
-        core, gain, *in_hbm(z_in),
-        *in_vmem(near, own, other, base_0, scaled_0, base_1, scaled_1),
-    )
+    )(core, *in_vmem(near, own, other, *parts))
+
+
+def cut_edges(q_ref, k_ref, v_ref, out_ref, rows_ref, sem):
+    length = q_ref.shape[0]
+    last = pl.ds(length - 8, 8)
+    fetch([(ref.at[last], rows_ref.at[i]) for i, ref in enumerate((q_ref, k_ref, v_ref))], sem)
+    for i in range(3):
+        out_ref[i] = rows_ref[i, 4:8, :]
+
+
+def edges_of(*arrays):
+    columns = arrays[0].shape[1]
+    return pl.pallas_call(
+        cut_edges,
+        in_specs=[ANY] * 3,
+        out_specs=VMEM,
+        out_shape=pltpu.VMEM((3, 4, columns), BF),
+        scratch_shapes=[pltpu.VMEM((3, 8, columns), BF), pltpu.SemaphoreType.DMA((3,))],
+        compiler_params=SMALL,
+        name="cut_edges",
+    )(*in_hbm(*arrays))
 
 
 def joined_near(core, pair, near):
@@ -569,8 +589,7 @@
     ctx = lax.axis_size("ctx")
     levels = ctx.bit_length() - 1
     position = lax.axis_index("ctx")
-    edge = jnp.stack([x[length - 4 :] for x in (q_in, k_in, v_in)], axis=0)
-    halo = lax.ppermute(edge, "ctx", [(i, i + 1) for i in range(ctx - 1)])
+    halo = lax.ppermute(edges_of(q_in, k_in, v_in), "ctx", [(i, i + 1) for i in range(ctx - 1)])
 
     g = jnp.cumsum(log_gate.reshape(blocks, BLK, heads), axis=1).reshape(length, heads) * LOG2_E
     g_pad = jnp.pad(g, ((0, 0), (0, BLK - heads)))
@@ -587,27 +606,28 @@
     near = lax.ppermute(pair, "ctx", [(i, i ^ 1) for i in range(ctx)])
     pair = joined_near(core, pair, near)
 
+    gain = norm_gain.reshape(1, BLK)
+
     def queries(second, q_in):
         return queries_of(
-            second, levels, core, rows, g_pad, weights, conv_weight, halo, q_in, kt, uw, prior, near
+            second, levels, core, rows, g_pad, weights, conv_weight, halo, gain, q_in, z_in,
+            kt, uw, prior, near,
         )
 
     reach, states = None, []
     for level in range(1, levels - 1):
         far = lax.ppermute(pair, "ctx", [(i, i ^ 2**level) for i in range(ctx)])
         if level == 1:
-            far, scaled_0, base_0 = lax.optimization_barrier((far, *queries(False, q_in)))
+            far, *parts = lax.optimization_barrier((far, *queries(False, q_in)))
         pair, state, reach = joined_far(bits[level], pair, far, reach, level == levels - 2)
         states.append(state)
     top = levels - 1
     pair, later_q = lax.optimization_barrier((pair, q_in))
     far = lax.ppermute(pair, "ctx", [(i, i ^ 2**top) for i in range(ctx)])
-    far, scaled_1, base_1 = lax.optimization_barrier((far, *queries(True, later_q)))
+    far, *more = lax.optimization_barrier((far, *queries(True, later_q)))
     own = joined_top(bits[top], far, reach, states)
     other = lax.ppermute(own, "ctx", [(i, i ^ 1) for i in range(ctx)])
-    return finished(
-        core, norm_gain.reshape(1, BLK), z_in, near, own, other, base_0, scaled_0, base_1, scaled_1
-    )
+    return finished(core, near, own, other, *parts, *more)
 
 
 def solution(mesh):

time: 70.6 us -> 64.8 us (0.918)
  Pallas kernels: 50.4 us -> 47.4 us
  local copies, waits for them, and re-layouts: 2.95 us -> 0.6 us
  starting transfers between devices: 9.64 us -> 11 us
  waiting for transfers between devices: 5.82 us -> 5.02 us
  other arithmetic: 1.1 us -> 0.3 us
    pallas_call x2 -> x3, Pallas kernels: 26.9 us -> 23.6 us  [the longest x1 17 us: keys_of(): pl.pallas_call(key_side, grid=(steps,), in_specs=[whole(rows.shape), whol...]
    another operation x2 -> x0, local copies, waits for them, and re-layouts: 1.6 us -> none  [per_device(): edge = jnp.stack([x[length - 4:] for x in (q_in, k_in, v_in)], axis=0)]
    ppermute x1, starting transfers between devices: 1.64 us -> 2.66 us  [per_device(): far = lax.ppermute(pair, 'ctx', [(i, i ^ 2 ** level) for i in range(ctx)])]
    another operation x1, other arithmetic: 0.77 us -> 0.01 us  [per_device(): rows = jnp.stack([g.T, beta.T], axis=1)]
    reshape x1, local copies, waits for them, and re-layouts: 0.88 us -> 0.12 us  [per_device(): log_gate.reshape(blocks, BLK, heads)]
  transfers between devices with their start and end apart: 5 -> 5, of which waited for: 4 -> 4; matrix products, arithmetic and copies ran while one was open for 3% -> 1% of each run, Pallas kernels for 32% -> 35%
where the time goes in v5:
time: 64.8 us; the launch traced here: 64.6 us
  Pallas kernels  47.4 us (73%)
  starting transfers between devices  11 us (17%)
  waiting for transfers between devices  5.02 us (8%)
    pallas_call x2, Pallas kernels, queries_of(): pl.pallas_call(functools.partial(query_side, first_step=first), grid=(ste...  22.9 us
    pallas_call x1, Pallas kernels, keys_of(): pl.pallas_call(key_side, grid=(steps,), in_specs=[whole(rows.shape), whol...  17 us
    pallas_call x1, Pallas kernels, finished(): pl.pallas_call(finish_side, grid=(heads // FINISH_HEADS,), in_specs=[SMEM...  5.73 us
    ppermute x1, starting transfers between devices, per_device(): near = lax.ppermute(pair, 'ctx', [(i, i ^ 1) for i in range(ctx)])  2.9 us
    ppermute x1, starting transfers between devices, per_device(): far = lax.ppermute(pair, 'ctx', [(i, i ^ 2 ** top) for i in range(ctx)])  2.82 us
    ppermute x1, starting transfers between devices, per_device(): far = lax.ppermute(pair, 'ctx', [(i, i ^ 2 ** level) for i in range(ctx)])  2.66 us
    ppermute x1, starting transfers between devices, per_device(): lax.ppermute(edges_of(q_in, k_in, v_in), 'ctx', [(i, i + 1) for i in rang...  2.53 us
    ppermute x1, waiting for transfers between devices, per_device(): near = lax.ppermute(pair, 'ctx', [(i, i ^ 1) for i in range(ctx)])  2.29 us
  transfers between devices with their start and end apart: 5, of which 4 were waited for; matrix products, arithmetic and copies ran while one was open for 1% of the time, Pallas kernels for 35%

profile of v5, /device:TPU:0, one launch (start us, length us, event | category | flops | bytes accessed | tf_op | source)
XLA Modules:
  0.0 64.6 jit_solution(15091633288872249368)
XLA Ops:
  0.0 0.0 copy-start.2
  0.0 0.0 copy-start.3
  0.0 0.8 %cut_edges.1 = bf16[3,4,2048]{2,1,0:T(4,128)(2,1)S(1)} custom-call(bf16[512,2048]{1,0:T(8,128)(2,1)} %q_ref.4, bf16[512,2048]{1,0:T(8,128)(2,1)} %k_next.1, bf16[512,2048]{1,0:T(8,128)(2,1)} %v_next.1), custom_call_target="tpu_custom_call" | custom-call | tf_op jit(solution)/shard_map/cut_edges/pallas_call | solution.py:531
  0.8 0.0 slice-start
  0.9 0.0 copy-start
  0.9 2.5 %collective-permute-start = (bf16[3,4,2048]{2,1,0:T(4,128)(2,1)S(1)}, bf16[3,4,2048]{2,1,0:T(4,128)(2,1)S(1)}, u32[]{:S(2)}, u32[]{:S(2)}) collective-permute-start(bf16[3,4,2048]{2,1,0:T(4,128)(2,1)S(1)} %cut_edges.1), channel_id=1, source_target_pairs={{0,1},{1,2},{2,3},{3,4},{4,5},{5,6},{6,7},{8,9},{9,10},{10,11},{11... | collective-permute-start | bytes 147464 | tf_op jit(solution)/shard_map/ppermute | solution.py:592
  3.4 0.0 copy-done.2
  3.4 0.1 copy.30
  3.5 0.3 reduce_window_sum.11
  3.8 0.1 copy.24
  3.9 0.0 copy-done.3
  4.0 0.0 slice-done
  4.0 0.1 copy.25
  4.2 0.1 copy.26
  4.4 0.0 collective-permute-done.halo_ref
  4.4 0.1 copy.27.rows_ref
  4.5 0.0 copy-done
  4.5 17.0 %key_side.1 = (bf16[16,128,512]{2,1,0:T(8,128)(2,1)S(1)}, bf16[16,512,256]{2,1,0:T(8,128)(2,1)S(1)}, bf16[16,128,256]{2,1,0:T(8,128)(2,1)S(1)}, bf16[16,3,128,256]{3,2,1,0:T(8,128)(2,1)S(1)}) custom-call(f32[16,2,512]{2,1,0:T(2,128)S(1)} %copy.27.rows_ref, f32[512,128]{1,0:T(8,128)S(1)} %pad.8.g_ref, f32[3,4,2048]{2,1,0:T(4,128)S(1)} %copy-done, ...), custom_call_target="tpu_custom_call" | custom-call | flops 10000000000 | bytes 20000000 | tf_op jit(solution)/shard_map/key_side/pallas_call | solution.py:455
  21.5 0.0 copy-start.1
  21.5 2.9 %collective-permute-start.1 = (bf16[16,128,256]{2,1,0:T(8,128)(2,1)S(1)}, bf16[16,128,256]{2,1,0:T(8,128)(2,1)S(1)}, u32[]{:S(2)}, u32[]{:S(2)}) collective-permute-start(bf16[16,128,256]{2,1,0:T(8,128)(2,1)S(1)} %get-tuple-element.39.pair_ref), channel_id=1, source_target_pairs={{0,1},{1,0},{2,3},{3,2},{4,5},{5,4},{6,7},{7,6},{8,9},{9,8},{10,11... | collective-permute-start | bytes 3145736 | tf_op jit(solution)/shard_map/ppermute | solution.py:606
  24.4 2.3 %collective-permute-done.1.far_ref.near_ref = bf16[16,128,256]{2,1,0:T(8,128)(2,1)S(1)} collective-permute-done((bf16[16,128,256]{2,1,0:T(8,128)(2,1)S(1)}, bf16[16,128,256]{2,1,0:T(8,128)(2,1)S(1)}, u32[]{:S(2)}, u32[]{:S(2)}) %collective-permute-start.1) | collective-permute-done | bytes 1048608 | tf_op jit(solution)/shard_map/ppermute | solution.py:606
  26.7 0.4 join_near.1.pair_ref
  27.1 2.7 %collective-permute-start.2 = (bf16[8,128,256]{2,1,0:T(8,128)(2,1)S(1)}, bf16[8,128,256]{2,1,0:T(8,128)(2,1)S(1)}, u32[]{:S(2)}, u32[]{:S(2)}) collective-permute-start(bf16[8,128,256]{2,1,0:T(8,128)(2,1)S(1)} %join_near.1.pair_ref), channel_id=1, source_target_pairs={{0,2},{1,3},{2,0},{3,1},{4,6},{5,7},{6,4},{7,5},{8,10},{9,11},{10,... | collective-permute-start | bytes 1572872 | tf_op jit(solution)/shard_map/ppermute | solution.py:619
  29.8 0.0 copy-done.1
  29.8 11.5 %query_side.2 = (bf16[8,512,256]{2,1,0:T(8,128)(2,1)S(1)}, f32[8,512,128]{2,1,0:T(8,128)S(1)}, f32[8,512,128]{2,1,0:T(8,128)S(1)}) custom-call(s32[1]{0:T(128)} %bitcast.6.core_ref.odd_ref, f32[16,2,512]{2,1,0:T(2,128)S(1)} %copy.27.rows_ref, f32[512,128]{1,0:T(8,128)S(1)} %pad.8.g_ref, f32[512,128]{1,0:T(8,128)S(1)} %pad.9.weight_ref, ...), custom_call_target="tpu_custom_call" | custom-call | flops 10000000000 | bytes 20000000 | tf_op jit(solution)/shard_map/query_side/pallas_call | solution.py:486
  41.2 0.8 %collective-permute-done.2.far_ref = bf16[8,128,256]{2,1,0:T(8,128)(2,1)S(1)} collective-permute-done((bf16[8,128,256]{2,1,0:T(8,128)(2,1)S(1)}, bf16[8,128,256]{2,1,0:T(8,128)(2,1)S(1)}, u32[]{:S(2)}, u32[]{:S(2)}) %collective-permute-start.2) | collective-permute-done | bytes 524320 | tf_op jit(solution)/shard_map/ppermute | solution.py:619
  42.0 0.4 join_far.1
  42.4 2.8 %collective-permute-start.3 = (bf16[8,128,128]{2,1,0:T(8,128)(2,1)S(1)}, bf16[8,128,128]{2,1,0:T(8,128)(2,1)S(1)}, u32[]{:S(2)}, u32[]{:S(2)}) collective-permute-start(bf16[8,128,128]{2,1,0:T(8,128)(2,1)S(1)} %get-tuple-element.51), channel_id=1, source_target_pairs={{0,4},{1,5},{2,6},{3,7},{4,0},{5,1},{6,2},{7,3},{8,12},{9,13},{10,... | collective-permute-start | bytes 786440 | tf_op jit(solution)/shard_map/ppermute | solution.py:626
  45.2 11.5 %query_side.3 = (bf16[8,512,256]{2,1,0:T(8,128)(2,1)S(1)}, f32[8,512,128]{2,1,0:T(8,128)S(1)}, f32[8,512,128]{2,1,0:T(8,128)S(1)}) custom-call(s32[1]{0:T(128)} %bitcast.6.core_ref.odd_ref, f32[16,2,512]{2,1,0:T(2,128)S(1)} %copy.27.rows_ref, f32[512,128]{1,0:T(8,128)S(1)} %pad.8.g_ref, f32[512,128]{1,0:T(8,128)S(1)} %pad.9.weight_ref, ...), custom_call_target="tpu_custom_call" | custom-call | flops 10000000000 | bytes 20000000 | tf_op jit(solution)/shard_map/query_side/pallas_call | solution.py:486
  56.7 0.1 collective-permute-done.3.far_ref
  56.7 0.1 join_top.1.own_ref
  56.9 0.1 collective-permute-start.4
  56.9 1.9 %collective-permute-done.4.other_ref = bf16[8,128,256]{2,1,0:T(8,128)(2,1)S(1)} collective-permute-done((bf16[8,128,256]{2,1,0:T(8,128)(2,1)S(1)}, bf16[8,128,256]{2,1,0:T(8,128)(2,1)S(1)}, u32[]{:S(2)}, u32[]{:S(2)}) %collective-permute-start.4) | collective-permute-done | bytes 524320 | tf_op jit(solution)/shard_map/ppermute | solution.py:629
  58.8 5.7 %finish_side.1 = bf16[512,2048]{1,0:T(8,128)(2,1)} custom-call(s32[1]{0:T(128)} %bitcast.6.core_ref.odd_ref, bf16[16,128,256]{2,1,0:T(8,128)(2,1)S(1)} %collective-permute-done.1.far_ref.near_ref, bf16[8,128,256]{2,1,0:T(8,128)(2,1)S(1)} %join_top.1.own_ref, bf16[8,128,256]{2,1,0:T(8,128)(2,1)S(1)} %collective-permute-done.4.other_ref, ...), custom_call_target="tpu_custom_call" | custom-call | tf_op jit(solution)/shard_map/finish_side/pallas_call | solution.py:510
  (5 shorter events, 0.1 us)
Async XLA Ops:
  0.0 3.4 %copy-start.2 = (f32[512,16]{0,1:T(8,128)S(1)}, f32[512,16]{0,1:T(8,128)}, u32[]{:S(2)}) copy-start(f32[512,16]{0,1:T(8,128)} %param.13) | copy-start | bytes 98308
  0.0 3.9 %copy-start.3 = (f32[512,16]{0,1:T(8,128)S(1)}, f32[512,16]{0,1:T(8,128)}, u32[]{:S(2)}) copy-start(f32[512,16]{0,1:T(8,128)} %param.14) | copy-start | bytes 98308
  0.8 3.2 %slice-start = ((f32[512,16,6]{0,1,2:T(8,128)}), f32[512,16,4]{0,1,2:T(8,128)S(1)}, s32[]{:S(2)}) async-start(f32[512,16,6]{0,1,2:T(8,128)} %param.15), calls=%async_computation | async-start | bytes 262144 | tf_op jit(solution)/shard_map/slice | solution.py:597
  0.9 3.6 %copy-start = (f32[3,4,2048]{2,1,0:T(4,128)S(1)}, f32[3,4,2048]{2,1,0:T(4,128)}, u32[]{:S(2)}) copy-start(f32[3,4,2048]{2,1,0:T(4,128)} %taps_ref.5) | copy-start | bytes 294916
  0.9 3.5 %collective-permute-start = (bf16[3,4,2048]{2,1,0:T(4,128)(2,1)S(1)}, bf16[3,4,2048]{2,1,0:T(4,128)(2,1)S(1)}, u32[]{:S(2)}, u32[]{:S(2)}) collective-permute-start(bf16[3,4,2048]{2,1,0:T(4,128)(2,1)S(1)} %cut_edges.1), channel_id=1, source_target_pairs={{0,1},{1,2},{2,3},{3,4},{4,5},{5,6},{6,7},{8,9},{9,10},{10,11},{11... | collective-permute-start | bytes 147464 | tf_op jit(solution)/shard_map/ppermute | solution.py:592
  21.5 8.2 %copy-start.1 = (f32[128]{0:T(128)S(1)}, f32[128]{0:T(128)}, u32[]{:S(2)}) copy-start(f32[128]{0:T(128)} %param.17) | copy-start | bytes 1540
  21.5 5.2 %collective-permute-start.1 = (bf16[16,128,256]{2,1,0:T(8,128)(2,1)S(1)}, bf16[16,128,256]{2,1,0:T(8,128)(2,1)S(1)}, u32[]{:S(2)}, u32[]{:S(2)}) collective-permute-start(bf16[16,128,256]{2,1,0:T(8,128)(2,1)S(1)} %get-tuple-element.39.pair_ref), channel_id=1, source_target_pairs={{0,1},{1,0},{2,3},{3,2},{4,5},{5,4},{6,7},{7,6},{8,9},{9,8},{10,11... | collective-permute-start | bytes 3145736 | tf_op jit(solution)/shard_map/ppermute | solution.py:606
  27.1 14.9 %collective-permute-start.2 = (bf16[8,128,256]{2,1,0:T(8,128)(2,1)S(1)}, bf16[8,128,256]{2,1,0:T(8,128)(2,1)S(1)}, u32[]{:S(2)}, u32[]{:S(2)}) collective-permute-start(bf16[8,128,256]{2,1,0:T(8,128)(2,1)S(1)} %join_near.1.pair_ref), channel_id=1, source_target_pairs={{0,2},{1,3},{2,0},{3,1},{4,6},{5,7},{6,4},{7,5},{8,10},{9,11},{10,... | collective-permute-start | bytes 1572872 | tf_op jit(solution)/shard_map/ppermute | solution.py:619
  42.4 14.4 %collective-permute-start.3 = (bf16[8,128,128]{2,1,0:T(8,128)(2,1)S(1)}, bf16[8,128,128]{2,1,0:T(8,128)(2,1)S(1)}, u32[]{:S(2)}, u32[]{:S(2)}) collective-permute-start(bf16[8,128,128]{2,1,0:T(8,128)(2,1)S(1)} %get-tuple-element.51), channel_id=1, source_target_pairs={{0,4},{1,5},{2,6},{3,7},{4,0},{5,1},{6,2},{7,3},{8,12},{9,13},{10,... | collective-permute-start | bytes 786440 | tf_op jit(solution)/shard_map/ppermute | solution.py:626
  56.9 2.0 %collective-permute-start.4 = (bf16[8,128,256]{2,1,0:T(8,128)(2,1)S(1)}, bf16[8,128,256]{2,1,0:T(8,128)(2,1)S(1)}, u32[]{:S(2)}, u32[]{:S(2)}) collective-permute-start(bf16[8,128,256]{2,1,0:T(8,128)(2,1)S(1)} %join_top.1.own_ref), channel_id=1, source_target_pairs={{0,1},{1,0},{2,3},{3,2},{4,5},{5,4},{6,7},{7,6},{8,9},{9,8},{10,11... | collective-permute-start | bytes 1572872 | tf_op jit(solution)/shard_map/ppermute | solution.py:629

commit v6 on v5

--- a/solution.py
+++ b/solution.py
@@ -288,24 +288,23 @@
 
 
 def finish_side(
-    core_ref, near_ref, own_ref, other_ref, scaled_0, base_0, gate_0, scaled_1, base_1, gate_1,
-    out_ref,
+    half_ref, core_ref, near_ref, state_ref, scaled_0, base_0, gate_0, scaled_1, base_1, gate_1,
+    *rest,
 ):
+    out_ref = rest[-1]
     step = pl.program_id(0)
-    core = core_ref[0]
+    half = half_ref[0]
     length = out_ref.shape[0]
     blocks = length // BLK
-    levels = own_ref.shape[2] // BLK
-    fold = pl.num_programs(0) // 2
+    levels = state_ref.shape[2] // BLK
     eye = jnp.where(iota2((BLK, BLK), 0) == iota2((BLK, BLK), 1), 1.0, 0.0).astype(BF)
 
-    def part(second, scaled_ref, base_ref, gate_ref):
-        mine = core == second
+    def part(scaled_ref, base_ref, gate_ref):
         for head in range(FINISH_HEADS):
             lanes = slice(head * BLK, (head + 1) * BLK)
-            place = step % fold * FINISH_HEADS + head
-            reach = jnp.where(core == 1, near_ref[step * FINISH_HEADS + head, :, :BLK], eye)
-            seen = dot(reach, jnp.where(mine, own_ref[place], other_ref[place])).astype(BF)
+            place = step * FINISH_HEADS + head
+            near = near_ref[half * state_ref.shape[0] + place, :, :BLK]
+            seen = dot(jnp.where(core_ref[0] == 1, near, eye), state_ref[place]).astype(BF)
             states = jnp.concatenate(
                 [seen[:, level * BLK : (level + 1) * BLK] for level in range(levels)], axis=0
             )
@@ -316,13 +315,13 @@
                 normed = opened * lax.rsqrt(square + EPS)
                 out_ref[tokens, lanes] = (normed * gate_ref[place, tokens, :]).astype(BF)
 
-    @pl.when(step < fold)
-    def _():
-        part(0, scaled_0, base_0, gate_0)
-
-    @pl.when(step >= fold)
-    def _():
-        part(1, scaled_1, base_1, gate_1)
+    @pl.when(half == 0)
+    def _():
+        part(scaled_0, base_0, gate_0)
+
+    @pl.when(half == 1)
+    def _():
+        part(scaled_1, base_1, gate_1)
 
 
 def merged(left, right_a, right_b):
@@ -505,17 +504,25 @@
     )(core, rows, g_pad, weights, taps, halo, gain, *in_hbm(q_in, z_in), *in_vmem(*kept))
 
 
-def finished(core, near, own, other, *parts):
+def finished(half, core, near, states, parts, previous):
     heads, length = near.shape[0], parts[0].shape[1]
+    steps = heads // FINISH_HEADS // 2
     return pl.pallas_call(
         finish_side,
-        grid=(heads // FINISH_HEADS,),
-        in_specs=[SMEM] + [VMEM] * 9,
-        out_specs=by_column((length, FINISH_HEADS * BLK)),
+        grid_spec=pltpu.PrefetchScalarGridSpec(
+            num_scalar_prefetch=1,
+            grid=(steps,),
+            in_specs=[SMEM] + [VMEM] * 8 + [ANY] * len(previous),
+            out_specs=pl.BlockSpec(
+                (length, FINISH_HEADS * BLK), lambda i, half: (0, half[0] * steps + i)
+            ),
+        ),
         out_shape=shape_of((length, heads * BLK), BF),
+        input_output_aliases={10 + i: i for i in range(len(previous))},
         compiler_params=PARAMS,
+        cost_estimate=COST,
         name="finish_side",
-    )(core, *in_vmem(near, own, other, *parts))
+    )(half, core, *in_vmem(near, states, *parts), *previous)
 
 
 def cut_edges(q_ref, k_ref, v_ref, out_ref, rows_ref, sem):
@@ -596,11 +603,11 @@
     rows = jnp.stack([g.T, beta.T], axis=1)
     weights = level_weight[:, :, : levels + 1].reshape(length, heads * (levels + 1))
     weights = jnp.pad(weights, ((0, 0), (0, -weights.shape[1] % BLK)))
-    bits = [bit(position, level) for level in range(levels)]
+    bits = [bit(position, level) for level in range(levels)] + [1 - bit(position, 0)]
     halo, rows, g_pad, weights, *bits = lax.optimization_barrier(
         (halo, rows, g_pad, weights, *bits)
     )
-    core = bits[0]
+    core, beside = bits[0], bits[-1]
 
     kt, uw, pair, prior = keys_of(rows, g_pad, conv_weight, halo, k_in, v_in)
     near = lax.ppermute(pair, "ctx", [(i, i ^ 1) for i in range(ctx)])
@@ -627,7 +634,10 @@
     far, *more = lax.optimization_barrier((far, *queries(True, later_q)))
     own = joined_top(bits[top], far, reach, states)
     other = lax.ppermute(own, "ctx", [(i, i ^ 1) for i in range(ctx)])
-    return finished(core, near, own, other, *parts, *more)
+    parts = [*parts, *more]
+    out = finished(core, core, near, own, parts, ())
+    other, out = lax.optimization_barrier((other, out))
+    return finished(beside, core, near, other, parts, (out,))
 
 
 def solution(mesh):

time: 64.8 us -> 63.7 us (0.983)
  waiting for transfers between devices: 5.02 us -> 3.1 us
  Pallas kernels: 47.4 us -> 48.2 us
    ppermute x1, waiting for transfers between devices: 1.9 us -> 0.01 us  [per_device(): other = lax.ppermute(own, 'ctx', [(i, i ^ 1) for i in range(ctx)])]
    pallas_call x1 -> x2, Pallas kernels: 5.73 us -> 6.48 us  [finished(): pl.pallas_call(finish_side, grid_spec=pltpu.PrefetchScalarGridSpec(num_sc...]
  transfers between devices with their start and end apart: 5 -> 5, of which waited for: 4 -> 3; matrix products, arithmetic and copies ran while one was open for 1% -> 1% of each run, Pallas kernels for 35% -> 41%
where the time goes in v6:
time: 63.7 us; the launch traced here: 63.4 us
  Pallas kernels  48.2 us (76%)
  starting transfers between devices  11 us (17%)
  waiting for transfers between devices  3.1 us (5%)
    pallas_call x2, Pallas kernels, queries_of(): pl.pallas_call(functools.partial(query_side, first_step=first), grid=(ste...  22.9 us
    pallas_call x1, Pallas kernels, keys_of(): pl.pallas_call(key_side, grid=(steps,), in_specs=[whole(rows.shape), whol...  17 us
    pallas_call x2, Pallas kernels, finished(): pl.pallas_call(finish_side, grid_spec=pltpu.PrefetchScalarGridSpec(num_sc...  6.48 us
    ppermute x1, starting transfers between devices, per_device(): near = lax.ppermute(pair, 'ctx', [(i, i ^ 1) for i in range(ctx)])  2.91 us
    ppermute x1, starting transfers between devices, per_device(): far = lax.ppermute(pair, 'ctx', [(i, i ^ 2 ** top) for i in range(ctx)])  2.83 us
    ppermute x1, starting transfers between devices, per_device(): far = lax.ppermute(pair, 'ctx', [(i, i ^ 2 ** level) for i in range(ctx)])  2.65 us
    ppermute x1, starting transfers between devices, per_device(): lax.ppermute(edges_of(q_in, k_in, v_in), 'ctx', [(i, i + 1) for i in rang...  2.53 us
    ppermute x1, waiting for transfers between devices, per_device(): near = lax.ppermute(pair, 'ctx', [(i, i ^ 1) for i in range(ctx)])  2.29 us
  transfers between devices with their start and end apart: 5, of which 3 were waited for; matrix products, arithmetic and copies ran while one was open for 1% of the time, Pallas kernels for 41%

profile of v6, /device:TPU:0, one launch (start us, length us, event | category | flops | bytes accessed | tf_op | source)
XLA Modules:
  0.0 63.4 jit_solution(6689025993955101919)
XLA Ops:
  0.0 0.0 copy-start.2
  0.0 0.0 copy-start.3
  0.0 0.8 %cut_edges.1 = bf16[3,4,2048]{2,1,0:T(4,128)(2,1)S(1)} custom-call(bf16[512,2048]{1,0:T(8,128)(2,1)} %q_ref.4, bf16[512,2048]{1,0:T(8,128)(2,1)} %k_next.1, bf16[512,2048]{1,0:T(8,128)(2,1)} %v_next.1), custom_call_target="tpu_custom_call" | custom-call | tf_op jit(solution)/shard_map/cut_edges/pallas_call | solution.py:538
  0.8 0.0 slice-start
  0.9 0.0 copy-start
  0.9 2.5 %collective-permute-start = (bf16[3,4,2048]{2,1,0:T(4,128)(2,1)S(1)}, bf16[3,4,2048]{2,1,0:T(4,128)(2,1)S(1)}, u32[]{:S(2)}, u32[]{:S(2)}) collective-permute-start(bf16[3,4,2048]{2,1,0:T(4,128)(2,1)S(1)} %cut_edges.1), channel_id=1, source_target_pairs={{0,1},{1,2},{2,3},{3,4},{4,5},{5,6},{6,7},{8,9},{9,10},{10,11},{11... | collective-permute-start | bytes 147464 | tf_op jit(solution)/shard_map/ppermute | solution.py:599
  3.4 0.0 copy-done.2
  3.4 0.1 copy.31
  3.5 0.3 reduce_window_sum.11
  3.8 0.1 copy.25
  3.9 0.0 copy-done.3
  4.0 0.0 slice-done
  4.0 0.1 copy.26
  4.2 0.1 copy.27
  4.4 0.0 collective-permute-done.halo_ref
  4.4 0.1 copy.28.rows_ref
  4.5 0.0 copy-done
  4.5 17.0 %key_side.1 = (bf16[16,128,512]{2,1,0:T(8,128)(2,1)S(1)}, bf16[16,512,256]{2,1,0:T(8,128)(2,1)S(1)}, bf16[16,128,256]{2,1,0:T(8,128)(2,1)S(1)}, bf16[16,3,128,256]{3,2,1,0:T(8,128)(2,1)S(1)}) custom-call(f32[16,2,512]{2,1,0:T(2,128)S(1)} %copy.28.rows_ref, f32[512,128]{1,0:T(8,128)S(1)} %pad.8.g_ref, f32[3,4,2048]{2,1,0:T(4,128)S(1)} %copy-done, ...), custom_call_target="tpu_custom_call" | custom-call | flops 10000000000 | bytes 20000000 | tf_op jit(solution)/shard_map/key_side/pallas_call | solution.py:454
  21.5 0.0 copy-start.1
  21.5 2.9 %collective-permute-start.1 = (bf16[16,128,256]{2,1,0:T(8,128)(2,1)S(1)}, bf16[16,128,256]{2,1,0:T(8,128)(2,1)S(1)}, u32[]{:S(2)}, u32[]{:S(2)}) collective-permute-start(bf16[16,128,256]{2,1,0:T(8,128)(2,1)S(1)} %get-tuple-element.43.pair_ref), channel_id=1, source_target_pairs={{0,1},{1,0},{2,3},{3,2},{4,5},{5,4},{6,7},{7,6},{8,9},{9,8},{10,11... | collective-permute-start | bytes 3145736 | tf_op jit(solution)/shard_map/ppermute | solution.py:613
  24.4 2.3 %collective-permute-done.1.far_ref.near_ref = bf16[16,128,256]{2,1,0:T(8,128)(2,1)S(1)} collective-permute-done((bf16[16,128,256]{2,1,0:T(8,128)(2,1)S(1)}, bf16[16,128,256]{2,1,0:T(8,128)(2,1)S(1)}, u32[]{:S(2)}, u32[]{:S(2)}) %collective-permute-start.1) | collective-permute-done | bytes 1048608 | tf_op jit(solution)/shard_map/ppermute | solution.py:613
  26.7 0.4 join_near.1.pair_ref
  27.1 2.7 %collective-permute-start.2 = (bf16[8,128,256]{2,1,0:T(8,128)(2,1)S(1)}, bf16[8,128,256]{2,1,0:T(8,128)(2,1)S(1)}, u32[]{:S(2)}, u32[]{:S(2)}) collective-permute-start(bf16[8,128,256]{2,1,0:T(8,128)(2,1)S(1)} %join_near.1.pair_ref), channel_id=1, source_target_pairs={{0,2},{1,3},{2,0},{3,1},{4,6},{5,7},{6,4},{7,5},{8,10},{9,11},{10,... | collective-permute-start | bytes 1572872 | tf_op jit(solution)/shard_map/ppermute | solution.py:626
  29.8 0.0 copy-done.1
  29.8 11.5 %query_side.2 = (bf16[8,512,256]{2,1,0:T(8,128)(2,1)S(1)}, f32[8,512,128]{2,1,0:T(8,128)S(1)}, f32[8,512,128]{2,1,0:T(8,128)S(1)}) custom-call(s32[1]{0:T(128)} %bitcast.6.core_ref.odd_ref.half_ref, f32[16,2,512]{2,1,0:T(2,128)S(1)} %copy.28.rows_ref, f32[512,128]{1,0:T(8,128)S(1)} %pad.8.g_ref, f32[512,128]{1,0:T(8,128)S(1)} %pad.9.weight_ref, ...), custom_call_target="tpu_custom_call" | custom-call | flops 10000000000 | bytes 20000000 | tf_op jit(solution)/shard_map/query_side/pallas_call | solution.py:485
  41.2 0.8 %collective-permute-done.2.far_ref = bf16[8,128,256]{2,1,0:T(8,128)(2,1)S(1)} collective-permute-done((bf16[8,128,256]{2,1,0:T(8,128)(2,1)S(1)}, bf16[8,128,256]{2,1,0:T(8,128)(2,1)S(1)}, u32[]{:S(2)}, u32[]{:S(2)}) %collective-permute-start.2) | collective-permute-done | bytes 524320 | tf_op jit(solution)/shard_map/ppermute | solution.py:626
  42.0 0.4 join_far.1
  42.4 2.8 %collective-permute-start.3 = (bf16[8,128,128]{2,1,0:T(8,128)(2,1)S(1)}, bf16[8,128,128]{2,1,0:T(8,128)(2,1)S(1)}, u32[]{:S(2)}, u32[]{:S(2)}) collective-permute-start(bf16[8,128,128]{2,1,0:T(8,128)(2,1)S(1)} %get-tuple-element.55), channel_id=1, source_target_pairs={{0,4},{1,5},{2,6},{3,7},{4,0},{5,1},{6,2},{7,3},{8,12},{9,13},{10,... | collective-permute-start | bytes 786440 | tf_op jit(solution)/shard_map/ppermute | solution.py:633
  45.2 11.5 %query_side.3 = (bf16[8,512,256]{2,1,0:T(8,128)(2,1)S(1)}, f32[8,512,128]{2,1,0:T(8,128)S(1)}, f32[8,512,128]{2,1,0:T(8,128)S(1)}) custom-call(s32[1]{0:T(128)} %bitcast.6.core_ref.odd_ref.half_ref, f32[16,2,512]{2,1,0:T(2,128)S(1)} %copy.28.rows_ref, f32[512,128]{1,0:T(8,128)S(1)} %pad.8.g_ref, f32[512,128]{1,0:T(8,128)S(1)} %pad.9.weight_ref, ...), custom_call_target="tpu_custom_call" | custom-call | flops 10000000000 | bytes 20000000 | tf_op jit(solution)/shard_map/query_side/pallas_call | solution.py:485
  56.7 0.1 collective-permute-done.3.far_ref
  56.7 0.1 join_top.1.state_ref
  56.9 0.1 collective-permute-start.4
  56.9 3.3 %finish_side.2.rest_0_ = bf16[512,2048]{1,0:T(8,128)(2,1)} custom-call(s32[1]{0:T(128)} %bitcast.6.core_ref.odd_ref.half_ref, s32[1]{0:T(128)} %bitcast.6.core_ref.odd_ref.half_ref, bf16[16,128,256]{2,1,0:T(8,128)(2,1)S(1)} %collective-permute-done.1.far_ref.near_ref, bf16[8,128,256]{2,1,0:T(8,128)(2,1)S(1)} %join_top.1.state_ref, ...), custom_call_target="tpu_custom_call" | custom-call | flops 10000000000 | bytes 20000000 | tf_op jit(solution)/shard_map/finish_side/pallas_call | solution.py:510
  60.2 0.0 collective-permute-done.4.state_ref
  60.2 3.2 %finish_side.3 = bf16[512,2048]{1,0:T(8,128)(2,1)} custom-call(s32[1]{0:T(128)S(6)} %sub.14.half_ref, s32[1]{0:T(128)} %bitcast.6.core_ref.odd_ref.half_ref, bf16[16,128,256]{2,1,0:T(8,128)(2,1)S(1)} %collective-permute-done.1.far_ref.near_ref, bf16[8,128,256]{2,1,0:T(8,128)(2,1)S(1)} %collective-permute-done.4.state_ref, ...), custom_call_target="tpu_custom_call", output_to_operand_aliasing={{}: (10, {})} | custom-call | flops 10000000000 | bytes 20000000 | tf_op jit(solution)/shard_map/finish_side/pallas_call | solution.py:510
  (5 shorter events, 0.1 us)
Async XLA Ops:
  0.0 3.4 %copy-start.2 = (f32[512,16]{0,1:T(8,128)S(1)}, f32[512,16]{0,1:T(8,128)}, u32[]{:S(2)}) copy-start(f32[512,16]{0,1:T(8,128)} %param.13) | copy-start | bytes 98308
  0.0 3.9 %copy-start.3 = (f32[512,16]{0,1:T(8,128)S(1)}, f32[512,16]{0,1:T(8,128)}, u32[]{:S(2)}) copy-start(f32[512,16]{0,1:T(8,128)} %param.14) | copy-start | bytes 98308
  0.8 3.2 %slice-start = ((f32[512,16,6]{0,1,2:T(8,128)}), f32[512,16,4]{0,1,2:T(8,128)S(1)}, s32[]{:S(2)}) async-start(f32[512,16,6]{0,1,2:T(8,128)} %param.15), calls=%async_computation | async-start | bytes 262144 | tf_op jit(solution)/shard_map/slice | solution.py:604
  0.9 3.6 %copy-start = (f32[3,4,2048]{2,1,0:T(4,128)S(1)}, f32[3,4,2048]{2,1,0:T(4,128)}, u32[]{:S(2)}) copy-start(f32[3,4,2048]{2,1,0:T(4,128)} %taps_ref.5) | copy-start | bytes 294916
  0.9 3.5 %collective-permute-start = (bf16[3,4,2048]{2,1,0:T(4,128)(2,1)S(1)}, bf16[3,4,2048]{2,1,0:T(4,128)(2,1)S(1)}, u32[]{:S(2)}, u32[]{:S(2)}) collective-permute-start(bf16[3,4,2048]{2,1,0:T(4,128)(2,1)S(1)} %cut_edges.1), channel_id=1, source_target_pairs={{0,1},{1,2},{2,3},{3,4},{4,5},{5,6},{6,7},{8,9},{9,10},{10,11},{11... | collective-permute-start | bytes 147464 | tf_op jit(solution)/shard_map/ppermute | solution.py:599
  21.5 8.2 %copy-start.1 = (f32[128]{0:T(128)S(1)}, f32[128]{0:T(128)}, u32[]{:S(2)}) copy-start(f32[128]{0:T(128)} %param.17) | copy-start | bytes 1540
  21.5 5.2 %collective-permute-start.1 = (bf16[16,128,256]{2,1,0:T(8,128)(2,1)S(1)}, bf16[16,128,256]{2,1,0:T(8,128)(2,1)S(1)}, u32[]{:S(2)}, u32[]{:S(2)}) collective-permute-start(bf16[16,128,256]{2,1,0:T(8,128)(2,1)S(1)} %get-tuple-element.43.pair_ref), channel_id=1, source_target_pairs={{0,1},{1,0},{2,3},{3,2},{4,5},{5,4},{6,7},{7,6},{8,9},{9,8},{10,11... | collective-permute-start | bytes 3145736 | tf_op jit(solution)/shard_map/ppermute | solution.py:613
  27.1 14.9 %collective-permute-start.2 = (bf16[8,128,256]{2,1,0:T(8,128)(2,1)S(1)}, bf16[8,128,256]{2,1,0:T(8,128)(2,1)S(1)}, u32[]{:S(2)}, u32[]{:S(2)}) collective-permute-start(bf16[8,128,256]{2,1,0:T(8,128)(2,1)S(1)} %join_near.1.pair_ref), channel_id=1, source_target_pairs={{0,2},{1,3},{2,0},{3,1},{4,6},{5,7},{6,4},{7,5},{8,10},{9,11},{10,... | collective-permute-start | bytes 1572872 | tf_op jit(solution)/shard_map/ppermute | solution.py:626
  42.4 14.4 %collective-permute-start.3 = (bf16[8,128,128]{2,1,0:T(8,128)(2,1)S(1)}, bf16[8,128,128]{2,1,0:T(8,128)(2,1)S(1)}, u32[]{:S(2)}, u32[]{:S(2)}) collective-permute-start(bf16[8,128,128]{2,1,0:T(8,128)(2,1)S(1)} %get-tuple-element.55), channel_id=1, source_target_pairs={{0,4},{1,5},{2,6},{3,7},{4,0},{5,1},{6,2},{7,3},{8,12},{9,13},{10,... | collective-permute-start | bytes 786440 | tf_op jit(solution)/shard_map/ppermute | solution.py:633
  56.9 3.3 %collective-permute-start.4 = (bf16[8,128,256]{2,1,0:T(8,128)(2,1)S(1)}, bf16[8,128,256]{2,1,0:T(8,128)(2,1)S(1)}, u32[]{:S(2)}, u32[]{:S(2)}) collective-permute-start(bf16[8,128,256]{2,1,0:T(8,128)(2,1)S(1)} %join_top.1.state_ref), channel_id=1, source_target_pairs={{0,1},{1,0},{2,3},{3,2},{4,5},{5,4},{6,7},{7,6},{8,9},{9,8},{10,11... | collective-permute-start | bytes 1572872 | tf_op jit(solution)/shard_map/ppermute | solution.py:636
